TPU v7x, 32 devices: a whole 2x2x4 slice. The times are simulated.
32 devices in a mesh: groups: 2 (over y), ctx: 16 (over z, x, core).
Axes of the slice: x: 2, y: 2, z: 4, core: 2. Of those that a mesh axis runs over, the one named last changes fastest.
Arguments:
- child_q: bfloat16 [32, 128, 4096], P(('groups', 'ctx')), parts along dimension 0, may hold values from -8 to 8
- child_kv: bfloat16 [32, 128, 2, 512], P(('groups', 'ctx')), parts along dimension 0, may hold values from -12 to 12
- prompt_kv: bfloat16 [128, 2, 512], P(('groups', 'ctx')), parts along dimension 0, may hold values from -12 to 12
- parent_kv: bfloat16 [256, 2, 2, 512], P(('groups', 'ctx')), parts along dimension 0, may hold values from -12 to 12
- fork_list: int32 [32], P('groups'), parts along dimension 0, may hold values from 0 to 1
- owner_map: int32 [4, 16], P('groups'), parts along dimension 0, may hold values from 0 to 15, each once within a row
- lengths: int32 [4], P('groups'), parts along dimension 0, may hold values from 1 to 128, as said below
Outputs:
- child_out: bfloat16 [32, 128, 4096], P(('groups', 'ctx')), parts along dimension 0
There are 2 independent parts, one for each index of `groups`. A program takes and returns all parts, laid end to end along the dimension named above; each array names one. Nothing has to cross between parts.
Inputs may be any that keep to these rules, and one draw needn't show every extreme that they name: `lengths`: some parent has all 128 positions valid.
All inputs are finite; a program needn't handle non-finite values.
Results may differ from a plain program's by a relative error of at most 0.0032.
Values may be sent and summed in bfloat16 or wider, within the bound.
No kernel may reach another device: no remote copies, remote signals or barrier semaphores. Data moves between devices by JAX's collectives and lax.ppermute only.
A program may use at most 64 MiB of HBM per device.

v0:
```python
import jax
import jax.numpy as jnp
from jax import lax
from jax.sharding import PartitionSpec as P

KVH = 4
HD = 128


def head_rows(queries, kv_head, group_size, head_dim):
    row_count = queries.shape[0]
    column_block = queries[
        :, kv_head * group_size * head_dim : (kv_head + 1) * group_size * head_dim
    ]
    return column_block.reshape(row_count * group_size, head_dim)


def level_part(queries, key_rows, value_rows, allowed):
    scaling = queries.shape[1] ** (-0.5)
    scores = (
        jnp.einsum("qd,kd->qk", queries, key_rows, preferred_element_type=jnp.float32) * scaling
    )
    if allowed is not None:
        scores = jnp.where(allowed, scores, -jnp.inf)
    highest = jnp.max(scores, axis=1)
    weights = jnp.exp(scores - highest[:, None])
    if allowed is not None:
        weights = jnp.where(allowed, weights, 0.0)
    weights = lax.optimization_barrier(weights.astype(jnp.bfloat16))
    totals = jnp.sum(weights.astype(jnp.float32), axis=1)
    weighted = jnp.dot(weights, value_rows, preferred_element_type=jnp.float32)
    return (highest, totals, weighted)


def merge_levels(former, latter):
    highest = jnp.maximum(former[0], latter[0])
    weight_one = jnp.exp(former[0] - highest)
    weight_two = jnp.exp(latter[0] - highest)
    totals = former[1] * weight_one + latter[1] * weight_two
    weighted = former[2] * weight_one[:, None] + latter[2] * weight_two[:, None]
    return (highest, totals, weighted)


def body(child_q, child_kv, prompt_kv, parent_kv, fork_list, owner_map, lengths):
    queries = child_q[0]
    own_rows = child_kv[0]
    span_rows = queries.shape[0]
    kv_width = own_rows.shape[2]
    head_dim = HD
    kv_heads = KVH
    group_size = queries.shape[1] // kv_width
    query_rows = span_rows * group_size
    device = lax.axis_index("ctx")
    axis_size = lax.axis_size("ctx")
    seg_rows = parent_kv.shape[0]
    parent = lax.dynamic_index_in_dim(fork_list, device, 0, keepdims=False)
    owner_row = lax.dynamic_index_in_dim(owner_map, parent, 0, keepdims=False)
    places = jnp.arange(axis_size, dtype=jnp.int32)
    matches = owner_row[None, :] == places[:, None]
    pieces = jnp.sum(jnp.where(matches, places[None, :], 0), axis=1)
    positions = jnp.arange(seg_rows, dtype=jnp.int32)[:, None] + pieces[None, :] * seg_rows
    live_length = lax.dynamic_index_in_dim(lengths, parent, 0, keepdims=False)
    allowed = (positions < live_length).reshape(1, seg_rows * axis_size)
    outgoing = jnp.take(parent_kv, fork_list, axis=1)
    query_time = jnp.arange(query_rows, dtype=jnp.int32) // group_size
    causal = jnp.arange(span_rows, dtype=jnp.int32)[None, :] <= query_time[:, None]
    head_queries = []
    for kv_head in range(kv_heads):
        head_queries.append(head_rows(queries, kv_head, group_size, head_dim))
    prompt_copies = jnp.broadcast_to(
        prompt_kv[:, None], (prompt_kv.shape[0], axis_size, 2, kv_width)
    )
    prompt_in, arrived = (
        lax.all_to_all(prompt_copies, "ctx", split_axis=1, concat_axis=1, tiled=True),
        lax.all_to_all(outgoing, "ctx", split_axis=1, concat_axis=1, tiled=True),
    )
    prompt_all = prompt_in.reshape(prompt_kv.shape[0] * axis_size, 2, kv_width)
    segment = arrived.reshape(seg_rows * axis_size, 2, kv_width)
    results = []
    for kv_head in range(kv_heads):
        low = kv_head * head_dim
        prompt_stats = level_part(
            head_queries[kv_head],
            prompt_all[:, 0, low : low + head_dim],
            prompt_all[:, 1, low : low + head_dim],
            None,
        )
        parent_stats = level_part(
            head_queries[kv_head],
            segment[:, 0, low : low + head_dim],
            segment[:, 1, low : low + head_dim],
            allowed,
        )
        own_stats = level_part(
            head_queries[kv_head],
            own_rows[:, 0, low : low + head_dim],
            own_rows[:, 1, low : low + head_dim],
            causal,
        )
        merged = merge_levels(merge_levels(prompt_stats, parent_stats), own_stats)
        results.append((merged[2] / merged[1][:, None]).reshape(span_rows, group_size * head_dim))
    return jnp.concatenate(results, axis=1).astype(jnp.bfloat16)[None]


def solution(mesh):
    placed = (
        P(("groups", "ctx"), None, None),
        P(("groups", "ctx"), None, None, None),
        P(("groups", "ctx"), None, None),
        P(("groups", "ctx"), None, None, None),
        P("groups"),
        P("groups", None),
        P("groups"),
    )
    return jax.shard_map(
        body,
        mesh=mesh,
        in_specs=placed,
        out_specs=P(("groups", "ctx"), None, None),
        check_vma=False,
    )
```

profile of v0, /device:TPU:0, one launch (start us, length us, event | category | flops | bytes accessed | tf_op | source)
XLA Modules:
  0.0 47.7 jit_solution(876810784480943631)
XLA Ops:
  0.0 0.0 copy-start
  0.0 0.7 %copy.17 = bf16[4,2,512]{2,0,1:T(4,128)(2,1)S(1)} copy(bf16[4,2,512]{2,1,0:T(2,128)(2,1)} %param.9) | data formatting | bytes 16384 | tf_op args[2]
  0.7 0.7 %broadcast_in_dim.125 = bf16[4,16,2,512]{3,0,2,1:T(4,128)(2,1)} broadcast(bf16[4,2,512]{2,0,1:T(4,128)(2,1)S(1)} %copy.17), dimensions={0,2,3} | broadcast | bytes 139264 | tf_op jit(solution)/shard_map/broadcast_in_dim | solution.py:70
  1.4 7.4 %all-to-all-start = ((bf16[4,16,2,512]{3,0,2,1:T(4,128)(2,1)}), bf16[4,16,2,512]{3,0,2,1:T(4,128)(2,1)S(1)}, u32[]{:S(2)}, u32[]{:S(2)}) async-start(bf16[4,16,2,512]{3,0,2,1:T(4,128)(2,1)} %broadcast_in_dim.125), calls=%async_computation | async-start | bytes 262144 | tf_op jit(solution)/shard_map/all_to_all | solution.py:74
  8.8 0.7 %compare_select_fusion = s32[16]{0:T(128)S(1)} fusion(s32[16]{0:T(128)} %param.11), kind=kLoop, calls=%fused_computation.149 | loop fusion | flops 48 | bytes 128 | tf_op jit(solution)/shard_map/jit(_take)/jit(_where)/select_n | solution.py:64
  9.5 0.7 %compare_and_fusion = pred[16]{0:T(512)(128)(4,1)S(1)} fusion(s32[16]{0:T(128)} %param.11), kind=kLoop, calls=%fused_computation.150 | loop fusion | flops 96 | bytes 80 | tf_op jit(solution)/shard_map/jit(_take)/and | solution.py:64
  10.1 1.3 %fusion.52 = (bf16[128,1024]{1,0:T(8,128)(2,1)S(1)}, bf16[128,1024]{1,0:T(8,128)(2,1)S(1)}, bf16[128,1024]{1,0:T(8,128)(2,1)S(1)}, bf16[128,1024]{1,0:T(8,128)(2,1)S(1)}) fusion(bf16[128,4096]{1,0:T(8,128)(2,1)} %bitcast.148), kind=kLoop, calls=%fused_computation.153 | loop fusion | bytes 2097152 | tf_op jit(solution)/shard_map/slice | solution.py:12
  11.4 0.1 reshape.330
  11.6 0.0 copy-done.3
  11.6 0.1 reshape.335
  11.7 0.2 fusion.53
  12.0 1.0 %fusion.54 = (f32[1024]{0:T(1024)S(1)}, f32[1024,128]{0,1:T(8,128)}) fusion(bf16[1024,128]{1,0:T(8,128)(2,1)S(1)} %reshape.335, bf16[128,2,512]{2,0,1:T(8,128)(2,1)S(1)} %bitcast.150, s32[1024]{0:T(1024)S(1)} %add_select_fusion), kind=kOutput, calls=%fused_computation.155 | convolution fusion | flops 34077696 | bytes 827392 | tf_op jit(solution)/shard_map/qd,kd->qk/dot_general | solution.py:21
  13.0 0.1 reshape.334
  13.1 0.0 copy-start.5
  13.1 0.0 copy-start.6
  13.2 0.0 copy-start.4
  13.2 1.0 %fusion.55 = (f32[1024]{0:T(1024)S(1)}, f32[1024,128]{0,1:T(8,128)}) fusion(bf16[1024,128]{1,0:T(8,128)(2,1)S(1)} %reshape.334, bf16[128,2,512]{2,0,1:T(8,128)(2,1)S(1)} %bitcast.151, s32[1024]{0:T(1024)S(1)} %add_select_fusion), kind=kOutput, calls=%fused_computation.156 | convolution fusion | flops 34077696 | bytes 827392 | tf_op jit(solution)/shard_map/qd,kd->qk/dot_general | solution.py:21
  14.2 0.1 reshape.333
  14.3 1.1 %fusion.56 = (f32[1024]{0:T(1024)S(1)}, f32[1024,128]{0,1:T(8,128)}) fusion(bf16[1024,128]{1,0:T(8,128)(2,1)S(1)} %reshape.333, bf16[128,2,512]{2,0,1:T(8,128)(2,1)S(1)} %bitcast.152, s32[1024]{0:T(1024)S(1)} %add_select_fusion), kind=kOutput, calls=%fused_computation.157 | convolution fusion | flops 34077696 | bytes 827392 | tf_op jit(solution)/shard_map/qd,kd->qk/dot_general | solution.py:21
  15.4 0.0 copy-done.5
  15.4 0.6 %dynamic_slice.12 = s32[1]{0:T(128)} dynamic-slice(s32[16]{0:T(128)S(1)} %copy-done.5, s32[]{:T(128)S(6)} %select_n.100), dynamic_slice_sizes={1} | dynamic-slice | bytes 12 | tf_op jit(solution)/shard_map/jit(dynamic_index_in_dim)/dynamic_slice | solution.py:56
  17.9 0.6 %dynamic_slice.14 = s32[1]{0:T(128)} dynamic-slice(s32[2]{0:T(128)S(1)} %copy-done.6, s32[]{:T(128)S(6)} %select_n.101), dynamic_slice_sizes={1} | dynamic-slice | bytes 12 | tf_op jit(solution)/shard_map/jit(dynamic_index_in_dim)/dynamic_slice | solution.py:62
  18.5 0.1 select_reduce_fusion
  18.7 0.6 %add_compare_fusion = pred[8,16]{1,0:T(8,128)(4,1)S(1)} fusion(s32[]{:T(128)} %bitcast.6, s32[16]{0:T(128)S(1)} %broadcast_multiply_fusion), kind=kLoop, calls=%fused_computation.147 | loop fusion | flops 256 | bytes 196 | tf_op jit(solution)/shard_map/lt | solution.py:63
  19.3 1.7 %select_convert_fusion.7 = (bf16[1024,128]{0,1:T(8,128)(2,1)S(1)}, bf16[1024,128]{0,1:T(8,128)(2,1)S(1)}, bf16[1024,128]{0,1:T(8,128)(2,1)S(1)}, bf16[1024,128]{0,1:T(8,128)(2,1)S(1)}) fusion(f32[1024,128]{0,1:T(8,128)S(1)} %get-tuple-element.38, f32[1024]{0:T(1024)S(1)} %get-tuple-element.37, s32[1024]{0:T(1024)S(1)} %add_select_fusion, ...), kind=kLoop, calls=%fused_computation.69 | loop fusion | flops 1703936 | bytes 3166208 | tf_op jit(solution)/shard_map/convert_element_type | solution.py:29
  21.0 0.1 lt.31
  21.1 1.1 %gather_fusion = bf16[16,8,2,512]{3,2,1,0:T(2,128)(2,1)S(1)} fusion(bf16[8,2,2,512]{3,2,1,0:T(2,128)(2,1)S(1)} %copy-done, s32[1024]{0:T(1024)S(1)} %pad_clamp_fusion), kind=kCustom, calls=%fused_computation | custom fusion | bytes 524352 | tf_op jit(solution)/shard_map/jit(_take)/gather | solution.py:64
  22.2 1.0 %fusion.32 = bf16[8,16,2,512]{3,2,0,1:T(2,128)(2,1)} fusion(bf16[16,8,2,512]{3,2,1,0:T(2,128)(2,1)S(1)} %gather_fusion, pred[16]{0:T(512)(128)(4,1)S(1)} %compare_and_fusion), kind=kLoop, calls=%fused_computation.85 | loop fusion | flops 131072 | bytes 524304 | tf_op jit(solution)/shard_map/jit(_take)/select_n | solution.py:64
  23.3 0.0 all-to-all-done
  23.3 6.0 %all-to-all-start.1 = ((bf16[8,16,2,512]{3,2,0,1:T(2,128)(2,1)}), bf16[8,16,2,512]{3,2,0,1:T(2,128)(2,1)S(1)}, u32[]{:S(2)}, u32[]{:S(2)}) async-start(bf16[8,16,2,512]{3,2,0,1:T(2,128)(2,1)} %fusion.32), calls=%async_computation.1 | async-start | bytes 524288 | tf_op jit(solution)/shard_map/all_to_all | solution.py:75
  29.3 0.0 copy-start.1
  29.3 0.2 fusion.61
  29.6 0.2 fusion.62
  29.8 0.2 fusion.63
  30.0 0.2 fusion.64
  30.6 8.7 %all-to-all-done.1 = bf16[8,16,2,512]{3,2,0,1:T(2,128)(2,1)S(1)} async-done(((bf16[8,16,2,512]{3,2,0,1:T(2,128)(2,1)}), bf16[8,16,2,512]{3,2,0,1:T(2,128)(2,1)S(1)}, u32[]{:S(2)}, u32[]{:S(2)}) %all-to-all-start.1) | async-done | bytes 262176 | tf_op jit(solution)/shard_map/all_to_all | solution.py:75
  39.3 0.1 copy.19
  39.4 0.2 fusion.57
  39.7 0.2 fusion.58
  39.9 0.2 fusion.59
  40.2 0.2 fusion.60
  40.4 0.4 fusion.28
  40.9 0.1 convert_reduce_fusion
  41.0 0.3 convolution_multiply_fusion
  41.3 0.3 convolution_multiply_fusion.2
  41.6 0.2 copy-done.2
  41.7 0.6 %fusion.24 = bf16[1024,128]{1,0:T(8,128)(2,1)S(1)} fusion(f32[1024,128]{1,0:T(8,128)S(1)} %convolution_multiply_fusion, f32[1024,128]{1,0:T(8,128)S(1)} %convolution_multiply_fusion.2, bf16[1024,64]{0,1:T(8,128)(2,1)S(1)} %exponential_convert_fusion, f32[1024]{0:T(1024)S(1)} %get-tuple-element.20, f32[1024]{0:T(1024)S(1)} %get-tuple-element.22, ...), kind=kOutput, calls=%fused_computation.45 | convolution fusion | flops 17563648 | bytes 1470464 | tf_op jit(solution)/shard_map/dot_general | solution.py:31
  42.3 0.1 concatenate.22
  42.4 0.1 convert_reduce_fusion.2
  42.6 0.3 convolution_multiply_fusion.5
  42.9 0.3 convolution_multiply_fusion.7
  43.2 0.6 %fusion.25 = bf16[1024,128]{1,0:T(8,128)(2,1)S(1)} fusion(f32[1024,128]{1,0:T(8,128)S(1)} %convolution_multiply_fusion.5, f32[1024,128]{1,0:T(8,128)S(1)} %convolution_multiply_fusion.7, bf16[1024,64]{0,1:T(8,128)(2,1)S(1)} %exponential_convert_fusion.1, f32[1024]{0:T(1024)S(1)} %get-tuple-element.15, f32[1024]{0:T(1024)S(1)} %get-tuple-element.17, ...), kind=kOutput, calls=%fused_computation.46 | convolution fusion | flops 17563648 | bytes 1470464 | tf_op jit(solution)/shard_map/dot_general | solution.py:31
  43.7 0.1 concatenate.21
  43.8 0.1 convert_reduce_fusion.4
  44.0 0.3 convolution_multiply_fusion.10
  44.3 0.3 convolution_multiply_fusion.12
  44.6 0.6 %fusion.26 = bf16[1024,128]{1,0:T(8,128)(2,1)S(1)} fusion(f32[1024,128]{1,0:T(8,128)S(1)} %convolution_multiply_fusion.10, f32[1024,128]{1,0:T(8,128)S(1)} %convolution_multiply_fusion.12, bf16[1024,64]{0,1:T(8,128)(2,1)S(1)} %exponential_convert_fusion.2, f32[1024]{0:T(1024)S(1)} %get-tuple-element.10, f32[1024]{0:T(1024)S(1)} %get-tuple-element.12, ...), kind=kOutput, calls=%fused_computation.47 | convolution fusion | flops 17563648 | bytes 1470464 | tf_op jit(solution)/shard_map/dot_general | solution.py:31
  45.1 0.1 concatenate.20
  45.3 0.1 convert_reduce_fusion.6
  45.4 0.3 convolution_multiply_fusion.15
  45.7 0.3 convolution_multiply_fusion.17
  46.0 0.6 %fusion.27 = bf16[1024,128]{1,0:T(8,128)(2,1)S(1)} fusion(f32[1024,128]{1,0:T(8,128)S(1)} %convolution_multiply_fusion.15, f32[1024,128]{1,0:T(8,128)S(1)} %convolution_multiply_fusion.17, bf16[1024,64]{0,1:T(8,128)(2,1)S(1)} %exponential_convert_fusion.3, f32[1024]{0:T(1024)S(1)} %get-tuple-element.5, f32[1024]{0:T(1024)S(1)} %get-tuple-element.7, ...), kind=kOutput, calls=%fused_computation.48 | convolution fusion | flops 17563648 | bytes 1470464 | tf_op jit(solution)/shard_map/dot_general | solution.py:31
  46.6 0.1 concatenate.19
  46.7 1.0 %pad_maximum_fusion = bf16[1,128,4096]{2,1,0:T(8,128)(2,1)} fusion(bf16[1,128,1024]{2,1,0:T(8,128)(2,1)S(1)} %concatenate.22, bf16[1,128,1024]{2,1,0:T(8,128)(2,1)S(1)} %concatenate.21, bf16[1,128,1024]{2,1,0:T(8,128)(2,1)S(1)} %concatenate.20, bf16[1,128,1024]{2,1,0:T(8,128)(2,1)S(1)} %concatenate.19), kind=kLoop, calls=%fused_computation.53 | loop fusion | flops 4194304 | bytes 2097152 | tf_op jit(solution)/shard_map/concatenate | solution.py:102
  (24 shorter events, 0.5 us)
Async XLA Ops:
  0.0 21.1 %copy-start = (bf16[8,2,2,512]{3,2,1,0:T(2,128)(2,1)S(1)}, bf16[8,2,2,512]{3,2,1,0:T(2,128)(2,1)}, u32[]{:S(2)}) copy-start(bf16[8,2,2,512]{3,2,1,0:T(2,128)(2,1)} %param.10) | copy-start | bytes 98308
  1.4 21.9 %all-to-all-start = ((bf16[4,16,2,512]{3,0,2,1:T(4,128)(2,1)}), bf16[4,16,2,512]{3,0,2,1:T(4,128)(2,1)S(1)}, u32[]{:S(2)}, u32[]{:S(2)}) async-start(bf16[4,16,2,512]{3,0,2,1:T(4,128)(2,1)} %broadcast_in_dim.125), calls=%async_computation | async-start | bytes 262144 | tf_op jit(solution)/shard_map/all_to_all | solution.py:74
  10.1 1.4 %copy-start.3 = (bf16[1,128,2,512]{3,2,1,0:T(2,128)(2,1)S(1)}, bf16[1,128,2,512]{3,2,1,0:T(2,128)(2,1)}, u32[]{:S(2)}) copy-start(bf16[1,128,2,512]{3,2,1,0:T(2,128)(2,1)} %param.8) | copy-start | bytes 786436
  13.1 2.2 %copy-start.5 = (s32[16]{0:T(128)S(1)}, s32[16]{0:T(128)}, u32[]{:S(2)}) copy-start(s32[16]{0:T(128)} %param.11) | copy-start | bytes 196
  13.1 4.7 %copy-start.6 = (s32[2]{0:T(128)S(1)}, s32[2]{0:T(128)}, u32[]{:S(2)}) copy-start(s32[2]{0:T(128)} %param.13) | copy-start | bytes 28
  13.2 5.4 %copy-start.4 = (s32[2,16]{1,0:T(2,128)S(1)}, s32[2,16]{1,0:T(2,128)}, u32[]{:S(2)}) copy-start(s32[2,16]{1,0:T(2,128)} %param.12) | copy-start | bytes 388
  23.3 16.0 %all-to-all-start.1 = ((bf16[8,16,2,512]{3,2,0,1:T(2,128)(2,1)}), bf16[8,16,2,512]{3,2,0,1:T(2,128)(2,1)S(1)}, u32[]{:S(2)}, u32[]{:S(2)}) async-start(bf16[8,16,2,512]{3,2,0,1:T(2,128)(2,1)} %fusion.32), calls=%async_computation.1 | async-start | bytes 524288 | tf_op jit(solution)/shard_map/all_to_all | solution.py:75
  29.3 0.9 %copy-start.1 = (bf16[4,16,2,512]{3,1,0,2:T(8,128)(2,1)}, bf16[4,16,2,512]{3,1,0,2:T(8,128)(2,1)S(1)}, u32[]{:S(2)}) copy-start(bf16[4,16,2,512]{3,1,0,2:T(8,128)(2,1)S(1)} %copy.18) | copy-start | bytes 393220
  40.8 0.9 %copy-start.2 = (bf16[4,16,2,512]{3,1,0,2:T(8,128)(2,1)S(1)}, bf16[4,16,2,512]{3,1,0,2:T(8,128)(2,1)}, u32[]{:S(2)}) copy-start(bf16[4,16,2,512]{3,1,0,2:T(8,128)(2,1)} %copy-done.1) | copy-start | bytes 393220
where the time goes:
time: 48.2 us; the launch traced here: 47.7 us
  starting transfers between devices  13.4 us (28%)
  matrix products  9.77 us (20%)
  waiting for transfers between devices  8.69 us (18%)
  other arithmetic  7.01 us (15%)
  local copies, waits for them, and re-layouts  6.53 us (14%)
  between operations  2.33 us (5%)
    all_to_all x1, waiting for transfers between devices, body(): lax.all_to_all(outgoing, 'ctx', split_axis=1, concat_axis=1, tiled=True)  8.68 us
    all_to_all x1, starting transfers between devices, body(): lax.all_to_all(prompt_copies, 'ctx', split_axis=1, concat_axis=1, tiled=T...  7.39 us
    all_to_all x1, starting transfers between devices, body(): lax.all_to_all(outgoing, 'ctx', split_axis=1, concat_axis=1, tiled=True)  6 us
    dot_general x12, matrix products, level_part(): jnp.einsum('qd,kd->qk', queries, key_rows, preferred_element_type=jnp.flo...  5.17 us
    dot_general x12, matrix products, level_part(): weighted = jnp.dot(weights, value_rows, preferred_element_type=jnp.float32)  4.61 us
    convert_element_type x6, other arithmetic, level_part(): weights = lax.optimization_barrier(weights.astype(jnp.bfloat16))  2.32 us
    select_n x2, other arithmetic, body(): outgoing = jnp.take(parent_kv, fork_list, axis=1)  1.68 us
    slice x1, local copies, waits for them, and re-layouts, head_rows(): queries[:, kv_head * group_size * head_dim:(kv_head + 1) * group_size * h...  1.31 us
  transfers between devices with their start and end apart: 2, of which 1 were waited for; matrix products, arithmetic and copies ran while one was open for 29% of the time, Pallas kernels for 0%

commit v1 on v0

v1 whole, which is shorter than its diff:
```python
import functools

import jax
import jax.numpy as jnp
from jax import lax
from jax.experimental import pallas as pl
from jax.experimental.pallas import tpu as pltpu
from jax.sharding import PartitionSpec as P

HD = 128
LOG2E = 1.4426950408889634
F32 = jnp.float32
BF16 = jnp.bfloat16


def pack_kernel(fork_ref, prompt_ref, parent_ref, send_ref, table_ref):
    prompt = prompt_ref[...].astype(F32)
    shared = [prompt[:, 0, :], prompt[:, 1, :]]
    for p in range(parent_ref.shape[1]):
        piece = parent_ref[:, p].astype(F32)
        table_ref[p] = jnp.concatenate([piece[:, 0, :], piece[:, 1, :], *shared], axis=0).astype(BF16)

    def place(d, carry):
        send_ref[d] = table_ref[fork_ref[d]]
        return carry

    lax.fori_loop(0, send_ref.shape[0], place, 0, unroll=min(8, send_ref.shape[0]))


def mask_kernel(seg_rows, prompt_rows, fork_ref, owner_ref, lengths_ref, bias_ref):
    blocks = owner_ref.shape[1]
    device = lax.axis_index("ctx")
    parent = fork_ref[device]
    lane = lax.broadcasted_iota(jnp.int32, (8, blocks * seg_rows), 1)
    block, row = lane // seg_rows, lane % seg_rows

    def step(j, position):
        return jnp.where(block == owner_ref[parent, j], j * seg_rows + row, position)

    position = lax.fori_loop(0, blocks, step, jnp.zeros_like(lane), unroll=min(8, blocks))
    bias_ref[:, : blocks * seg_rows] = jnp.where(position < lengths_ref[parent], 0.0, -jnp.inf)
    tile = lax.broadcasted_iota(jnp.int32, (8, blocks * 2 * prompt_rows), 1)
    bias_ref[:, blocks * seg_rows :] = jnp.where(tile % (2 * prompt_rows) < prompt_rows, 0.0, -jnp.inf)


def attend_kernel(seg_rows, prompt_rows, q_ref, own_ref, got_ref, bias_ref, out_ref):
    span = q_ref.shape[1]
    group = q_ref.shape[2] // HD
    n = got_ref.shape[0]
    got = got_ref[...].astype(F32)
    par_k = got[:, :seg_rows].reshape(n * seg_rows, HD)
    par_v = got[:, seg_rows : 2 * seg_rows].reshape(n * seg_rows, HD)
    pro = got[:, 2 * seg_rows :].reshape(n * 2 * prompt_rows, HD)
    pro_v = pltpu.roll(pro, pro.shape[0] - prompt_rows, 0)
    own = own_ref[...].astype(F32)
    keys = jnp.concatenate([par_k, pro, own[:, 0, :]], axis=0).astype(BF16)
    values = jnp.concatenate([par_v, pro_v, own[:, 1, :]], axis=0)
    values = jnp.concatenate([values, jnp.ones_like(values)], axis=1).astype(BF16)
    far = n * (seg_rows + 2 * prompt_rows)
    factor = LOG2E * HD**-0.5
    row = lax.broadcasted_iota(jnp.int32, (span, span), 0)
    column = lax.broadcasted_iota(jnp.int32, (span, span), 1)
    causal = jnp.where(column <= row, 0.0, -jnp.inf)
    bias = jnp.concatenate([jnp.broadcast_to(bias_ref[0:1, :], (span, far)), causal], axis=1)
    for h in range(group):
        query = q_ref[0, :, h * HD : (h + 1) * HD]
        scores = lax.dot_general(query, keys, (((1,), (1,)), ((), ())), preferred_element_type=F32)
        scores = scores * factor + bias
        highest = jnp.max(scores, axis=1, keepdims=True)
        weights = jnp.exp2(scores - highest).astype(BF16)
        both = jnp.dot(weights, values, preferred_element_type=F32)
        out_ref[0, :, h * HD : (h + 1) * HD] = (both[:, :HD] / both[:, HD:]).astype(BF16)


def body(child_q, child_kv, prompt_kv, parent_kv, fork_list, owner_map, lengths):
    n = lax.axis_size("ctx")
    seg_rows, prompt_rows = parent_kv.shape[0], prompt_kv.shape[0]
    span, width = child_kv.shape[1], child_kv.shape[3]
    columns = child_q.shape[2]
    kv_heads = width // HD
    group_width = columns // kv_heads
    chunk = 2 * (seg_rows + prompt_rows)
    vmem = pl.BlockSpec(memory_space=pltpu.VMEM)
    smem = pl.BlockSpec(memory_space=pltpu.SMEM)
    send = pl.pallas_call(
        pack_kernel,
        out_shape=jax.ShapeDtypeStruct((n, chunk, width), BF16),
        in_specs=[smem, vmem, vmem],
        out_specs=vmem,
        scratch_shapes=[pltpu.VMEM((parent_kv.shape[1], chunk, width), BF16)],
        name="pack",
    )(fork_list, prompt_kv, parent_kv)
    got = lax.all_to_all(send, "ctx", split_axis=0, concat_axis=0, tiled=True)
    far = n * (seg_rows + 2 * prompt_rows)
    bias = pl.pallas_call(
        functools.partial(mask_kernel, seg_rows, prompt_rows),
        out_shape=jax.ShapeDtypeStruct((8, far), F32),
        in_specs=[smem, smem, smem],
        out_specs=vmem,
        name="mask",
    )(fork_list, owner_map, lengths)
    return pl.pallas_call(
        functools.partial(attend_kernel, seg_rows, prompt_rows),
        out_shape=jax.ShapeDtypeStruct(child_q.shape, BF16),
        grid=(kv_heads,),
        in_specs=[
            pl.BlockSpec((1, span, group_width), lambda g: (0, 0, g)),
            pl.BlockSpec((span, 2, HD), lambda g: (0, 0, g)),
            pl.BlockSpec((n, chunk, HD), lambda g: (0, 0, g)),
            pl.BlockSpec((8, far), lambda g: (0, 0)),
        ],
        out_specs=pl.BlockSpec((1, span, group_width), lambda g: (0, 0, g)),
        name="attend",
    )(child_q, child_kv[0], got, bias)


def solution(mesh):
    placed = (
        P(("groups", "ctx"), None, None),
        P(("groups", "ctx"), None, None, None),
        P(("groups", "ctx"), None, None),
        P(("groups", "ctx"), None, None, None),
        P("groups"),
        P("groups", None),
        P("groups"),
    )
    return jax.shard_map(
        body,
        mesh=mesh,
        in_specs=placed,
        out_specs=P(("groups", "ctx"), None, None),
        check_vma=False,
    )
```

time: 48.2 us -> 28.2 us (0.59)
  matrix products: 9.77 us -> 0 us
  Pallas kernels: 0 us -> 8.81 us
  other arithmetic: 7.01 us -> 0 us
  starting transfers between devices: 13.4 us -> 7.39 us
  local copies, waits for them, and re-layouts: 6.53 us -> 0.76 us
  between operations: 2.33 us -> 0.01 us
  waiting for transfers between devices: 8.69 us -> 10.8 us
    dot_general x24 -> x0, matrix products: 9.77 us -> none  [the longest x12 5.17 us: level_part(): jnp.einsum('qd,kd->qk', queries, key_rows, preferred_element_type=jnp.flo...]
    pallas_call x0 -> x3, Pallas kernels: none -> 8.81 us  [the longest x1 5.88 us: body(): pl.pallas_call(functools.partial(attend_kernel, seg_rows, prompt_rows), o...]
    all_to_all x2 -> x1, starting transfers between devices: 13.4 us -> 7.39 us  [body(): got = lax.all_to_all(send, 'ctx', split_axis=0, concat_axis=0, tiled=True)]
    convert_element_type x6 -> x0, other arithmetic: 2.32 us -> none  [level_part(): weights = lax.optimization_barrier(weights.astype(jnp.bfloat16))]
    all_to_all x2 -> x1, waiting for transfers between devices: 8.69 us -> 10.8 us  [body(): got = lax.all_to_all(send, 'ctx', split_axis=0, concat_axis=0, tiled=True)]
    select_n x3 -> x0, other arithmetic: 1.68 us -> none  [the longest x2 1.68 us: body(): outgoing = jnp.take(parent_kv, fork_list, axis=1)]
    slice x1 -> x0, local copies, waits for them, and re-layouts: 1.31 us -> none  [head_rows(): queries[:, kv_head * group_size * head_dim:(kv_head + 1) * group_size * h...]
    dynamic_slice x2 -> x0, local copies, waits for them, and re-layouts: 1.29 us -> none  [the longest x1 0.65 us: body(): live_length = lax.dynamic_index_in_dim(lengths, parent, 0, keepdims=False)]
  transfers between devices with their start and end apart: 2 -> 1, of which waited for: 1 -> 1; matrix products, arithmetic and copies ran while one was open for 29% -> 0% of each run, Pallas kernels for 0% -> 5%
where the time goes in v1:
time: 28.2 us; the launch traced here: 27.8 us
  waiting for transfers between devices  10.8 us (38%)
  Pallas kernels  8.81 us (31%)
  starting transfers between devices  7.39 us (26%)
  local copies, waits for them, and re-layouts  0.76 us (3%)
    all_to_all x1, waiting for transfers between devices, body(): got = lax.all_to_all(send, 'ctx', split_axis=0, concat_axis=0, tiled=True)  10.8 us
    all_to_all x1, starting transfers between devices, body(): got = lax.all_to_all(send, 'ctx', split_axis=0, concat_axis=0, tiled=True)  7.39 us
    pallas_call x1, Pallas kernels, body(): pl.pallas_call(functools.partial(attend_kernel, seg_rows, prompt_rows), o...  5.88 us
    pallas_call x1, Pallas kernels, body(): pl.pallas_call(pack_kernel, out_shape=jax.ShapeDtypeStruct((n, chunk, wid...  1.59 us
    pallas_call x1, Pallas kernels, body(): pl.pallas_call(functools.partial(mask_kernel, seg_rows, prompt_rows), out...  1.34 us
    unnamed x2, local copies, waits for them, and re-layouts  0.76 us
  transfers between devices with their start and end apart: 1, of which 1 were waited for; matrix products, arithmetic and copies ran while one was open for 0% of the time, Pallas kernels for 5%

profile of v1, /device:TPU:0, one launch (start us, length us, event | category | flops | bytes accessed | tf_op | source)
XLA Modules:
  0.0 27.8 jit_solution(2285004916661051341)
XLA Ops:
  0.0 1.6 %pack.1 = bf16[16,24,512]{2,1,0:T(8,128)(2,1)} custom-call(s32[16]{0:T(128)} %fork_ref.3, bf16[4,2,512]{2,1,0:T(2,128)(2,1)} %prompt_ref.1, bf16[8,2,2,512]{3,2,1,0:T(2,128)(2,1)} %parent_ref.1), custom_call_target="tpu_custom_call" | custom-call | tf_op jit(solution)/shard_map/pack/pallas_call | solution.py:85
  1.6 7.4 %all-to-all-start = ((bf16[16,24,512]{2,1,0:T(8,128)(2,1)}), bf16[16,24,512]{2,1,0:T(8,128)(2,1)S(1)}, u32[]{:S(2)}, u32[]{:S(2)}) async-start(bf16[16,24,512]{2,1,0:T(8,128)(2,1)} %pack.1), calls=%async_computation | async-start | bytes 786432 | tf_op jit(solution)/shard_map/all_to_all | solution.py:93
  9.0 1.3 %mask.1.bias_ref = f32[8,256]{1,0:T(8,128)} custom-call(s32[16]{0:T(128)} %fork_ref.3, s32[2,16]{1,0:T(2,128)} %owner_ref.1, s32[2]{0:T(128)} %lengths_ref.1), custom_call_target="tpu_custom_call" | custom-call | tf_op jit(solution)/shard_map/mask/pallas_call | solution.py:95
  10.3 10.8 %all-to-all-done.got_ref = bf16[16,24,512]{2,1,0:T(8,128)(2,1)S(1)} async-done(((bf16[16,24,512]{2,1,0:T(8,128)(2,1)}), bf16[16,24,512]{2,1,0:T(8,128)(2,1)S(1)}, u32[]{:S(2)}, u32[]{:S(2)}) %all-to-all-start) | async-done | bytes 393248 | tf_op jit(solution)/shard_map/all_to_all | solution.py:93
  21.2 0.0 copy-start
  21.2 0.8 %copy-done = bf16[16,24,512]{2,1,0:T(8,128)(2,1)} copy-done((bf16[16,24,512]{2,1,0:T(8,128)(2,1)}, bf16[16,24,512]{2,1,0:T(8,128)(2,1)S(1)}, u32[]{:S(2)}) %copy-start) | copy-done | bytes 393240
  21.9 5.9 %attend.1 = bf16[1,128,4096]{2,1,0:T(8,128)(2,1)} custom-call(bf16[1,128,4096]{2,1,0:T(8,128)(2,1)} %q_ref.1, bf16[128,2,512]{2,1,0:T(2,128)(2,1)} %bitcast.1, bf16[16,24,512]{2,1,0:T(8,128)(2,1)} %copy-done, f32[8,256]{1,0:T(8,128)} %mask.1.bias_ref), custom_call_target="tpu_custom_call" | custom-call | tf_op jit(solution)/shard_map/attend/pallas_call | solution.py:102
Async XLA Ops:
  1.6 19.6 %all-to-all-start = ((bf16[16,24,512]{2,1,0:T(8,128)(2,1)}), bf16[16,24,512]{2,1,0:T(8,128)(2,1)S(1)}, u32[]{:S(2)}, u32[]{:S(2)}) async-start(bf16[16,24,512]{2,1,0:T(8,128)(2,1)} %pack.1), calls=%async_computation | async-start | bytes 786432 | tf_op jit(solution)/shard_map/all_to_all | solution.py:93
  21.2 0.8 %copy-start = (bf16[16,24,512]{2,1,0:T(8,128)(2,1)}, bf16[16,24,512]{2,1,0:T(8,128)(2,1)S(1)}, u32[]{:S(2)}) copy-start(bf16[16,24,512]{2,1,0:T(8,128)(2,1)S(1)} %all-to-all-done.got_ref) | copy-start | bytes 1179652

commit v2 on v1

v2 whole, which is shorter than its diff:
```python
import functools

import jax
import jax.numpy as jnp
from jax import lax
from jax.experimental import pallas as pl
from jax.experimental.pallas import tpu as pltpu
from jax.sharding import PartitionSpec as P

HD = 128
LOG2E = 1.4426950408889634
F32 = jnp.float32
BF16 = jnp.bfloat16
VMEM = pl.BlockSpec(memory_space=pltpu.VMEM)
SMEM = pl.BlockSpec(memory_space=pltpu.SMEM)
ANY = pl.BlockSpec(memory_space=pl.ANY)


def limit(mib):
    return pltpu.CompilerParams(vmem_limit_bytes=mib << 20)


def shard_rows(prompt_ref, parent_ref):
    prompt = prompt_ref[...].astype(F32)
    rows = []
    for p in range(parent_ref.shape[1]):
        piece = parent_ref[:, p].astype(F32)
        rows += [piece[:, 0, :], piece[:, 1, :]]
    return rows, [prompt[:, 0, :], prompt[:, 1, :]]


def shard_kernel(prompt_ref, parent_ref, out_ref):
    pieces, shared = shard_rows(prompt_ref, parent_ref)
    out_ref[...] = jnp.concatenate(pieces + shared, axis=0).astype(BF16)


def pack_kernel(fork_ref, prompt_ref, parent_ref, send_ref, table_ref):
    pieces, shared = shard_rows(prompt_ref, parent_ref)
    for p in range(parent_ref.shape[1]):
        table_ref[p] = jnp.concatenate(pieces[2 * p : 2 * p + 2] + shared, axis=0).astype(BF16)

    def place(d, carry):
        send_ref[d] = table_ref[fork_ref[d]]
        return carry

    lax.fori_loop(0, send_ref.shape[0], place, 0, unroll=min(8, send_ref.shape[0]))


def mask_kernel(seg_rows, prompt_rows, offsets, fork_ref, owner_ref, lengths_ref, bias_ref):
    n = owner_ref.shape[1]
    device = lax.axis_index("ctx")
    parent = fork_ref[device]
    lane = lax.broadcasted_iota(jnp.int32, (8, n * seg_rows), 1)
    block, row = lane // seg_rows, lane % seg_rows
    if offsets is not None:
        place = block
        block = jnp.zeros_like(lane)
        for k in range(n):
            owner = device ^ jnp.where(device % 2 == 0, offsets[0][k], offsets[1][k])
            block = jnp.where(place == k, owner, block)

    def step(j, position):
        return jnp.where(block == owner_ref[parent, j], j * seg_rows + row, position)

    position = lax.fori_loop(0, n, step, jnp.zeros_like(lane), unroll=min(16, n))
    bias_ref[:, : n * seg_rows] = jnp.where(position < lengths_ref[parent], 0.0, -jnp.inf)
    tile = lax.broadcasted_iota(jnp.int32, (8, n * 2 * prompt_rows), 1)
    bias_ref[:, n * seg_rows :] = jnp.where(tile % (2 * prompt_rows) < prompt_rows, 0.0, -jnp.inf)


def attend_kernel(seg_rows, prompt_rows, one_parent, fork_ref, q_ref, own_ref, bias_ref, *refs):
    *shards, out_ref, stage, sems = refs
    span, columns = q_ref.shape[1:]
    kv_heads = own_ref.shape[2] // HD
    group = columns // HD // kv_heads
    first = 0 if one_parent else fork_ref[lax.axis_index("ctx")] * (2 * seg_rows)
    row = lax.broadcasted_iota(jnp.int32, (span, span), 0)
    column = lax.broadcasted_iota(jnp.int32, (span, span), 1)
    causal = jnp.where(column <= row, 0.0, -jnp.inf)
    bias = jnp.concatenate([jnp.broadcast_to(bias_ref[0:1, :], (span, bias_ref.shape[1])), causal], axis=1)
    factor = LOG2E * HD**-0.5

    def gathered(start, size, g):
        parts = [r[:, pl.ds(start, size), g * HD : (g + 1) * HD].astype(F32).reshape(-1, HD) for r in shards]
        return jnp.concatenate(parts, axis=0)

    copies = []
    for g in range(kv_heads):
        own = own_ref[:, :, g * HD : (g + 1) * HD].astype(F32)
        prompt = gathered(shards[0].shape[1] - 2 * prompt_rows, 2 * prompt_rows, g)
        prompt_values = pltpu.roll(prompt, prompt.shape[0] - prompt_rows, 0)
        parent_keys = gathered(pl.multiple_of(first, 8), seg_rows, g)
        parent_values = gathered(pl.multiple_of(first + seg_rows, 8), seg_rows, g)
        keys = jnp.concatenate([parent_keys, prompt, own[:, 0, :]], axis=0).astype(BF16)
        values = jnp.concatenate([parent_values, prompt_values, own[:, 1, :]], axis=0)
        values = jnp.concatenate([values, jnp.ones_like(values)], axis=1).astype(BF16)
        for h in range(g * group, (g + 1) * group):
            query = q_ref[0, :, h * HD : (h + 1) * HD]
            scores = lax.dot_general(query, keys, (((1,), (1,)), ((), ())), preferred_element_type=F32)
            scores = scores * factor + bias
            highest = jnp.max(scores, axis=1, keepdims=True)
            weights = jnp.exp2(scores - highest).astype(BF16)
            both = jnp.dot(weights, values, preferred_element_type=F32)
            stage[:, h * HD : (h + 1) * HD] = (both[:, :HD] / both[:, HD:]).astype(BF16)
        part = pl.ds(g * group * HD, group * HD)
        copies.append(pltpu.make_async_copy(stage.at[:, part], out_ref.at[0, :, part], sems.at[g]))
        copies[-1].start()
    for copy in copies:
        copy.wait()


def permute(x, target, n):
    return lax.ppermute(x, "ctx", [(i, target(i)) for i in range(n)])


def gather_shards(shard, n):
    chips = n // 2
    far, near = 2 * (chips - 2), 2
    first = permute(shard, lambda i: i ^ far, n)
    mate = permute(shard, lambda i: i ^ 1, n)
    side = permute(shard, lambda i: i ^ near, n)
    both = jnp.concatenate([shard, mate], axis=0)
    pairs = range(chips // 2 - 2, 0, -1)
    wide = [permute(both, lambda i, j=j: i ^ (2 * (2 * j + i % 2)), n) for j in pairs]
    passed = permute(first, lambda i: i ^ near, n)
    mine = jnp.concatenate([first, passed, side, *wide], axis=0)
    theirs = permute(mine, lambda i: i ^ 1, n)
    got = [[far, far ^ near, near], [far, far ^ near, near]]
    for j in pairs:
        for core in range(2):
            d = 2 * (2 * j + core)
            got[core] += [d, d ^ 1]
    offsets = [[0, 1, *got[core], *[o ^ 1 for o in got[1 - core]]] for core in range(2)]
    return [shard, mate, mine, theirs], offsets


def body(child_q, child_kv, prompt_kv, parent_kv, fork_list, owner_map, lengths):
    n = lax.axis_size("ctx")
    seg_rows, prompt_rows = parent_kv.shape[0], prompt_kv.shape[0]
    parents = parent_kv.shape[1]
    span, width = child_kv.shape[1], child_kv.shape[3]
    kv_heads = width // HD
    gather = n >= 8 and n & (n - 1) == 0 and parents * seg_rows + prompt_rows <= 2 * (seg_rows + prompt_rows)
    if gather:
        rows = 2 * (parents * seg_rows + prompt_rows)
        shard = pl.pallas_call(
            shard_kernel,
            out_shape=jax.ShapeDtypeStruct((rows, width), BF16),
            in_specs=[VMEM, VMEM],
            out_specs=VMEM,
            compiler_params=limit(2),
            name="shard",
        )(prompt_kv, parent_kv)
        shards, offsets = gather_shards(shard, n)
    else:
        rows = 2 * (seg_rows + prompt_rows)
        send = pl.pallas_call(
            pack_kernel,
            out_shape=jax.ShapeDtypeStruct((n, rows, width), BF16),
            in_specs=[SMEM, VMEM, VMEM],
            out_specs=VMEM,
            scratch_shapes=[pltpu.VMEM((parents, rows, width), BF16)],
            name="pack",
        )(fork_list, prompt_kv, parent_kv)
        shards, offsets = [lax.all_to_all(send, "ctx", split_axis=0, concat_axis=0, tiled=True)], None
    shards = [s.reshape(-1, rows, width) for s in shards]
    bias = pl.pallas_call(
        functools.partial(mask_kernel, seg_rows, prompt_rows, offsets),
        out_shape=jax.ShapeDtypeStruct((8, n * (seg_rows + 2 * prompt_rows)), F32),
        in_specs=[SMEM, SMEM, SMEM],
        out_specs=VMEM,
        compiler_params=limit(2),
        name="mask",
    )(fork_list, owner_map, lengths)
    return pl.pallas_call(
        functools.partial(attend_kernel, seg_rows, prompt_rows, not gather),
        out_shape=jax.ShapeDtypeStruct(child_q.shape, BF16),
        in_specs=[SMEM, VMEM, VMEM, VMEM] + [VMEM] * len(shards),
        out_specs=ANY,
        scratch_shapes=[pltpu.VMEM(child_q.shape[1:], BF16), pltpu.SemaphoreType.DMA((kv_heads,))],
        compiler_params=limit(16 if gather else 48),
        name="attend",
    )(fork_list, child_q, child_kv[0], bias, *shards)


def solution(mesh):
    placed = (
        P(("groups", "ctx"), None, None),
        P(("groups", "ctx"), None, None, None),
        P(("groups", "ctx"), None, None),
        P(("groups", "ctx"), None, None, None),
        P("groups"),
        P("groups", None),
        P("groups"),
    )
    return jax.shard_map(
        body,
        mesh=mesh,
        in_specs=placed,
        out_specs=P(("groups", "ctx"), None, None),
        check_vma=False,
    )
```

time: 28.2 us -> 23.1 us (0.82)
  waiting for transfers between devices: 10.8 us -> 6.36 us
  Pallas kernels: 8.81 us -> 5.08 us
  local copies, waits for them, and re-layouts: 0.76 us -> 2.73 us
  starting transfers between devices: 7.39 us -> 8.57 us
    all_to_all x1 -> x0, waiting for transfers between devices: 10.8 us -> none  [body(): got = lax.all_to_all(send, 'ctx', split_axis=0, concat_axis=0, tiled=True)]
    ppermute x0 -> x7, starting transfers between devices: none -> 8.57 us  [permute(): return lax.ppermute(x, 'ctx', [(i, target(i)) for i in range(n)])]
    all_to_all x1 -> x0, starting transfers between devices: 7.39 us -> none  [body(): got = lax.all_to_all(send, 'ctx', split_axis=0, concat_axis=0, tiled=True)]
    ppermute x0 -> x7, waiting for transfers between devices: none -> 6.36 us  [permute(): return lax.ppermute(x, 'ctx', [(i, target(i)) for i in range(n)])]
    pallas_call x3, Pallas kernels: 8.81 us -> 5.08 us  [the longest x1 4.46 us: body(): pl.pallas_call(functools.partial(attend_kernel, seg_rows, prompt_rows, no...]
    unnamed x2 -> x18, local copies, waits for them, and re-layouts: 0.76 us -> 2.72 us
  transfers between devices with their start and end apart: 1 -> 7, of which waited for: 1 -> 3; matrix products, arithmetic and copies ran while one was open for 0% -> 0% of each run, Pallas kernels for 5% -> 3%
where the time goes in v2:
time: 23.1 us; the launch traced here: 22.8 us
  starting transfers between devices  8.57 us (37%)
  waiting for transfers between devices  6.36 us (28%)
  Pallas kernels  5.08 us (22%)
  local copies, waits for them, and re-layouts  2.73 us (12%)
    ppermute x7, starting transfers between devices, permute(): return lax.ppermute(x, 'ctx', [(i, target(i)) for i in range(n)])  8.57 us
    ppermute x7, waiting for transfers between devices, permute(): return lax.ppermute(x, 'ctx', [(i, target(i)) for i in range(n)])  6.36 us
    pallas_call x1, Pallas kernels, body(): pl.pallas_call(functools.partial(attend_kernel, seg_rows, prompt_rows, no...  4.46 us
    unnamed x18, local copies, waits for them, and re-layouts  2.72 us
    pallas_call x1, Pallas kernels, body(): pl.pallas_call(functools.partial(mask_kernel, seg_rows, prompt_rows, offs...  0.59 us
  transfers between devices with their start and end apart: 7, of which 3 were waited for; matrix products, arithmetic and copies ran while one was open for 0% of the time, Pallas kernels for 3%

profile of v2, /device:TPU:0, one launch (start us, length us, event | category | flops | bytes accessed | tf_op | source)
XLA Modules:
  0.0 22.8 jit_solution(6608363056296659065)
XLA Ops:
  0.0 0.0 copy-start.2
  0.0 0.8 %copy-done.2 = bf16[8,2,2,512]{3,2,1,0:T(2,128)(2,1)S(1)} copy-done((bf16[8,2,2,512]{3,2,1,0:T(2,128)(2,1)S(1)}, bf16[8,2,2,512]{3,2,1,0:T(2,128)(2,1)}, u32[]{:S(2)}) %copy-start.2) | copy-done | bytes 32792
  0.8 0.0 copy-start.3
  0.8 0.7 %copy-done.3 = bf16[4,2,512]{2,1,0:T(2,128)(2,1)S(1)} copy-done((bf16[4,2,512]{2,1,0:T(2,128)(2,1)S(1)}, bf16[4,2,512]{2,1,0:T(2,128)(2,1)}, u32[]{:S(2)}) %copy-start.3) | copy-done | bytes 8216
  1.5 0.6 %collective-permute-start = (bf16[40,512]{1,0:T(8,128)(2,1)S(1)}, bf16[40,512]{1,0:T(8,128)(2,1)S(1)}, u32[]{:S(2)}, u32[]{:S(2)}) collective-permute-start(bf16[40,512]{1,0:T(8,128)(2,1)S(1)} %shard.1), channel_id=1, source_target_pairs={{0,1},{1,0},{2,3},{3,2},{4,5},{5,4},{6,7},{7,6},{8,9},{9,8},{10,11... | collective-permute-start | bytes 122888 | tf_op jit(solution)/shard_map/ppermute | solution.py:113
  2.0 2.6 %collective-permute-start.3 = (bf16[40,512]{1,0:T(8,128)(2,1)S(1)}, bf16[40,512]{1,0:T(8,128)(2,1)S(1)}, u32[]{:S(2)}, u32[]{:S(2)}) collective-permute-start(bf16[40,512]{1,0:T(8,128)(2,1)S(1)} %shard.1), channel_id=1, source_target_pairs={{0,2},{1,3},{2,0},{3,1},{4,6},{5,7},{6,4},{7,5},{8,10},{9,11},{10,... | collective-permute-start | bytes 122888 | tf_op jit(solution)/shard_map/ppermute | solution.py:113
  4.6 3.6 %collective-permute-start.1 = (bf16[40,512]{1,0:T(8,128)(2,1)S(1)}, bf16[40,512]{1,0:T(8,128)(2,1)S(1)}, u32[]{:S(2)}, u32[]{:S(2)}) collective-permute-start(bf16[40,512]{1,0:T(8,128)(2,1)S(1)} %shard.1), channel_id=1, source_target_pairs={{0,12},{1,13},{2,14},{3,15},{4,8},{5,9},{6,10},{7,11},{8,4},{9,5},... | collective-permute-start | bytes 122888 | tf_op jit(solution)/shard_map/ppermute | solution.py:113
  8.2 0.0 collective-permute-done
  8.2 0.1 collective-permute-start.5
  8.3 0.8 %collective-permute-start.4 = (bf16[80,512]{1,0:T(8,128)(2,1)S(1)}, bf16[80,512]{1,0:T(8,128)(2,1)S(1)}, u32[]{:S(2)}, u32[]{:S(2)}) collective-permute-start(bf16[80,512]{1,0:T(8,128)(2,1)S(1)} %pad_maximum_fusion), channel_id=1, source_target_pairs={{0,8},{1,11},{2,10},{3,9},{4,12},{5,15},{6,14},{7,13},{8,0},{9,3},... | collective-permute-start | bytes 245768 | tf_op jit(solution)/shard_map/ppermute | solution.py:113
  9.1 1.8 %collective-permute-done.1 = bf16[40,512]{1,0:T(8,128)(2,1)S(1)} collective-permute-done((bf16[40,512]{1,0:T(8,128)(2,1)S(1)}, bf16[40,512]{1,0:T(8,128)(2,1)S(1)}, u32[]{:S(2)}, u32[]{:S(2)}) %collective-permute-start.1) | collective-permute-done | bytes 40992 | tf_op jit(solution)/shard_map/ppermute | solution.py:113
  10.8 0.0 collective-permute-start.2
  10.8 0.0 copy-start.1
  10.9 4.0 %collective-permute-done.2 = bf16[40,512]{1,0:T(8,128)(2,1)S(1)} collective-permute-done((bf16[40,512]{1,0:T(8,128)(2,1)S(1)}, bf16[40,512]{1,0:T(8,128)(2,1)S(1)}, u32[]{:S(2)}, u32[]{:S(2)}) %collective-permute-start.2) | collective-permute-done | bytes 40992 | tf_op jit(solution)/shard_map/ppermute | solution.py:113
  14.8 0.0 collective-permute-done.3
  14.9 0.0 collective-permute-done.4
  14.9 0.0 copy-start.4
  14.9 0.0 copy-start.5
  14.9 0.0 copy-start.6
  14.9 0.0 collective-permute-done.5
  14.9 1.0 %collective-permute-start.6 = (bf16[280,512]{1,0:T(8,128)(2,1)S(1)}, bf16[280,512]{1,0:T(8,128)(2,1)S(1)}, u32[]{:S(2)}, u32[]{:S(2)}) collective-permute-start(bf16[280,512]{1,0:T(8,128)(2,1)S(1)} %constant_dynamic-update-slice_fusion), channel_id=1, source_target_pairs={{0,1},{1,0},{2,3},{3,2},{4,5},{5,4},{6,7},{7,6},{8,9},{9,8},{10,11... | collective-permute-start | bytes 860168 | tf_op jit(solution)/shard_map/ppermute | solution.py:113
  16.0 0.0 copy-done.4
  16.0 0.0 copy-done.5
  16.0 0.0 copy-done.6
  16.0 0.6 %mask.1.bias_ref = f32[8,256]{1,0:T(8,128)S(1)} custom-call(s32[16]{0:T(128)S(1)} %copy-done.4, s32[2,16]{1,0:T(2,128)S(1)} %copy-done.5, s32[2]{0:T(128)S(1)} %copy-done.6), custom_call_target="tpu_custom_call" | custom-call | tf_op jit(solution)/shard_map/mask/pallas_call | solution.py:167
  16.6 0.6 %collective-permute-done.6 = bf16[280,512]{1,0:T(8,128)(2,1)S(1)} collective-permute-done((bf16[280,512]{1,0:T(8,128)(2,1)S(1)}, bf16[280,512]{1,0:T(8,128)(2,1)S(1)}, u32[]{:S(2)}, u32[]{:S(2)}) %collective-permute-start.6) | collective-permute-done | bytes 286752 | tf_op jit(solution)/shard_map/ppermute | solution.py:113
  17.2 0.0 copy-done.1
  17.2 0.0 copy-start
  17.2 1.2 %copy-done = bf16[1,128,4096]{2,1,0:T(8,128)(2,1)S(1)} copy-done((bf16[1,128,4096]{2,1,0:T(8,128)(2,1)S(1)}, bf16[1,128,4096]{2,1,0:T(8,128)(2,1)}, u32[]{:S(2)}) %copy-start) | copy-done | bytes 1048600
  18.4 4.5 %attend.1 = bf16[1,128,4096]{2,1,0:T(8,128)(2,1)} custom-call(s32[16]{0:T(128)S(1)} %copy-done.4, bf16[1,128,4096]{2,1,0:T(8,128)(2,1)S(1)} %copy-done, bf16[128,2,512]{2,1,0:T(2,128)(2,1)S(1)} %bitcast.8, f32[8,256]{1,0:T(8,128)S(1)} %mask.1.bias_ref, bf16[1,40,512]{2,1,0:T(8,128)(2,1)S(1)} %bitcast.6, bf16[1,40,512]{2,1,0:T(8,128)(2,1)S(1)} %bitcast.9, ...), custom_call_target="tpu_custom_call" | custom-call | tf_op jit(solution)/shard_map/attend/pallas_call | solution.py:175
  (7 shorter events, 0.1 us)
Async XLA Ops:
  0.0 0.8 %copy-start.2 = (bf16[8,2,2,512]{3,2,1,0:T(2,128)(2,1)S(1)}, bf16[8,2,2,512]{3,2,1,0:T(2,128)(2,1)}, u32[]{:S(2)}) copy-start(bf16[8,2,2,512]{3,2,1,0:T(2,128)(2,1)} %parent_ref.1) | copy-start | bytes 98308
  0.8 0.7 %copy-start.3 = (bf16[4,2,512]{2,1,0:T(2,128)(2,1)S(1)}, bf16[4,2,512]{2,1,0:T(2,128)(2,1)}, u32[]{:S(2)}) copy-start(bf16[4,2,512]{2,1,0:T(2,128)(2,1)} %prompt_ref.1) | copy-start | bytes 24580
  1.5 6.7 %collective-permute-start = (bf16[40,512]{1,0:T(8,128)(2,1)S(1)}, bf16[40,512]{1,0:T(8,128)(2,1)S(1)}, u32[]{:S(2)}, u32[]{:S(2)}) collective-permute-start(bf16[40,512]{1,0:T(8,128)(2,1)S(1)} %shard.1), channel_id=1, source_target_pairs={{0,1},{1,0},{2,3},{3,2},{4,5},{5,4},{6,7},{7,6},{8,9},{9,8},{10,11... | collective-permute-start | bytes 122888 | tf_op jit(solution)/shard_map/ppermute | solution.py:113
  2.0 12.8 %collective-permute-start.3 = (bf16[40,512]{1,0:T(8,128)(2,1)S(1)}, bf16[40,512]{1,0:T(8,128)(2,1)S(1)}, u32[]{:S(2)}, u32[]{:S(2)}) collective-permute-start(bf16[40,512]{1,0:T(8,128)(2,1)S(1)} %shard.1), channel_id=1, source_target_pairs={{0,2},{1,3},{2,0},{3,1},{4,6},{5,7},{6,4},{7,5},{8,10},{9,11},{10,... | collective-permute-start | bytes 122888 | tf_op jit(solution)/shard_map/ppermute | solution.py:113
  4.6 6.2 %collective-permute-start.1 = (bf16[40,512]{1,0:T(8,128)(2,1)S(1)}, bf16[40,512]{1,0:T(8,128)(2,1)S(1)}, u32[]{:S(2)}, u32[]{:S(2)}) collective-permute-start(bf16[40,512]{1,0:T(8,128)(2,1)S(1)} %shard.1), channel_id=1, source_target_pairs={{0,12},{1,13},{2,14},{3,15},{4,8},{5,9},{6,10},{7,11},{8,4},{9,5},... | collective-permute-start | bytes 122888 | tf_op jit(solution)/shard_map/ppermute | solution.py:113
  8.2 6.7 %collective-permute-start.5 = (bf16[80,512]{1,0:T(8,128)(2,1)S(1)}, bf16[80,512]{1,0:T(8,128)(2,1)S(1)}, u32[]{:S(2)}, u32[]{:S(2)}) collective-permute-start(bf16[80,512]{1,0:T(8,128)(2,1)S(1)} %pad_maximum_fusion), channel_id=1, source_target_pairs={{0,4},{1,7},{2,6},{3,5},{4,0},{5,3},{6,2},{7,1},{8,12},{9,15},{10,... | collective-permute-start | bytes 245768 | tf_op jit(solution)/shard_map/ppermute | solution.py:113
  8.3 6.6 %collective-permute-start.4 = (bf16[80,512]{1,0:T(8,128)(2,1)S(1)}, bf16[80,512]{1,0:T(8,128)(2,1)S(1)}, u32[]{:S(2)}, u32[]{:S(2)}) collective-permute-start(bf16[80,512]{1,0:T(8,128)(2,1)S(1)} %pad_maximum_fusion), channel_id=1, source_target_pairs={{0,8},{1,11},{2,10},{3,9},{4,12},{5,15},{6,14},{7,13},{8,0},{9,3},... | collective-permute-start | bytes 245768 | tf_op jit(solution)/shard_map/ppermute | solution.py:113
  10.8 4.0 %collective-permute-start.2 = (bf16[40,512]{1,0:T(8,128)(2,1)S(1)}, bf16[40,512]{1,0:T(8,128)(2,1)S(1)}, u32[]{:S(2)}, u32[]{:S(2)}) collective-permute-start(bf16[40,512]{1,0:T(8,128)(2,1)S(1)} %collective-permute-done.1), channel_id=1, source_target_pairs={{0,2},{1,3},{2,0},{3,1},{4,6},{5,7},{6,4},{7,5},{8,10},{9,11},{10,... | collective-permute-start | bytes 122888 | tf_op jit(solution)/shard_map/ppermute | solution.py:113
  10.8 6.3 %copy-start.1 = (bf16[1,128,2,512]{3,2,1,0:T(2,128)(2,1)S(1)}, bf16[1,128,2,512]{3,2,1,0:T(2,128)(2,1)}, u32[]{:S(2)}) copy-start(bf16[1,128,2,512]{3,2,1,0:T(2,128)(2,1)} %param.8) | copy-start | bytes 786436
  14.9 1.1 %copy-start.4 = (s32[16]{0:T(128)S(1)}, s32[16]{0:T(128)}, u32[]{:S(2)}) copy-start(s32[16]{0:T(128)} %fork_ref.3) | copy-start | bytes 196
  14.9 1.1 %copy-start.5 = (s32[2,16]{1,0:T(2,128)S(1)}, s32[2,16]{1,0:T(2,128)}, u32[]{:S(2)}) copy-start(s32[2,16]{1,0:T(2,128)} %owner_ref.1) | copy-start | bytes 388
  14.9 1.1 %copy-start.6 = (s32[2]{0:T(128)S(1)}, s32[2]{0:T(128)}, u32[]{:S(2)}) copy-start(s32[2]{0:T(128)} %lengths_ref.1) | copy-start | bytes 28
  14.9 2.2 %collective-permute-start.6 = (bf16[280,512]{1,0:T(8,128)(2,1)S(1)}, bf16[280,512]{1,0:T(8,128)(2,1)S(1)}, u32[]{:S(2)}, u32[]{:S(2)}) collective-permute-start(bf16[280,512]{1,0:T(8,128)(2,1)S(1)} %constant_dynamic-update-slice_fusion), channel_id=1, source_target_pairs={{0,1},{1,0},{2,3},{3,2},{4,5},{5,4},{6,7},{7,6},{8,9},{9,8},{10,11... | collective-permute-start | bytes 860168 | tf_op jit(solution)/shard_map/ppermute | solution.py:113
  17.2 1.2 %copy-start = (bf16[1,128,4096]{2,1,0:T(8,128)(2,1)S(1)}, bf16[1,128,4096]{2,1,0:T(8,128)(2,1)}, u32[]{:S(2)}) copy-start(bf16[1,128,4096]{2,1,0:T(8,128)(2,1)} %q_ref.1) | copy-start | bytes 3145732

commit v3 on v2

v3 whole, which is shorter than its diff:
```python
import functools

import jax
import jax.numpy as jnp
from jax import lax
from jax.experimental import pallas as pl
from jax.experimental.pallas import tpu as pltpu
from jax.sharding import PartitionSpec as P

HD = 128
LOG2E = 1.4426950408889634
F32 = jnp.float32
BF16 = jnp.bfloat16
PAIR = 2
VMEM = pl.BlockSpec(memory_space=pltpu.VMEM)
SMEM = pl.BlockSpec(memory_space=pltpu.SMEM)
HBM = pl.BlockSpec(memory_space=pltpu.HBM)


def in_hbm(*arrays):
    return [pltpu.with_memory_space_constraint(x, pltpu.HBM) for x in arrays]


def limit(mib):
    return pltpu.CompilerParams(vmem_limit_bytes=mib << 20)


def shard_rows(prompt_ref, parent_ref):
    prompt = prompt_ref[...].astype(F32)
    rows = []
    for p in range(parent_ref.shape[1]):
        piece = parent_ref[:, p].astype(F32)
        rows += [piece[:, 0, :], piece[:, 1, :]]
    return rows, [prompt[:, 0, :], prompt[:, 1, :]]


def shard_kernel(prompt_hbm, parent_hbm, out_ref, prompt_ref, parent_ref, sems):
    copies = [
        pltpu.make_async_copy(parent_hbm, parent_ref, sems.at[0]),
        pltpu.make_async_copy(prompt_hbm, prompt_ref, sems.at[1]),
    ]
    for copy in copies:
        copy.start()
    for copy in copies:
        copy.wait()
    pieces, shared = shard_rows(prompt_ref, parent_ref)
    out_ref[...] = jnp.concatenate(pieces + shared, axis=0).astype(BF16)


def pack_kernel(fork_ref, prompt_ref, parent_ref, send_ref, table_ref):
    pieces, shared = shard_rows(prompt_ref, parent_ref)
    for p in range(parent_ref.shape[1]):
        table_ref[p] = jnp.concatenate(pieces[2 * p : 2 * p + 2] + shared, axis=0).astype(BF16)

    def place(d, carry):
        send_ref[d] = table_ref[fork_ref[d]]
        return carry

    lax.fori_loop(0, send_ref.shape[0], place, 0, unroll=min(8, send_ref.shape[0]))


def valid_keys(key, span, seg_rows, prompt_rows, counts, offsets, fork_ref, owner_ref, lengths_ref):
    n = owner_ref.shape[1]
    device = lax.axis_index("ctx")
    parent = fork_ref[device]
    place, row = jnp.full_like(key, -1), jnp.zeros_like(key)
    prompt = key < 0
    start, shard = span, 0
    for count in counts:
        slot = key - start
        here = (slot >= 0) & (slot < count * seg_rows)
        place = jnp.where(here, shard + slot // seg_rows, place)
        row = jnp.where(here, slot % seg_rows, row)
        slot = slot - count * seg_rows
        here = (slot >= 0) & (slot < count * 2 * prompt_rows)
        prompt = prompt | (here & (slot % (2 * prompt_rows) < prompt_rows))
        start += count * (seg_rows + 2 * prompt_rows)
        shard += count
    block = place
    if offsets is not None:
        block = jnp.full_like(key, -1)
        for k in range(n):
            owner = device ^ jnp.where(device % 2 == 0, offsets[0][k], offsets[1][k])
            block = jnp.where(place == k, owner, block)

    def step(j, position):
        return jnp.where(block == owner_ref[parent, j], j * seg_rows + row, position)

    far = jnp.full_like(key, n * seg_rows)
    position = lax.fori_loop(0, n, step, far, unroll=min(16, n))
    return (key < span) | prompt | (position < lengths_ref[parent])


def mask_kernel(sizes, stride, fork_hbm, owner_hbm, lengths_hbm, *refs):
    *outs, first_ref, fork_ref, owner_ref, lengths_ref, sems = refs
    pairs = ((fork_hbm, fork_ref), (owner_hbm, owner_ref), (lengths_hbm, lengths_ref))
    copies = [pltpu.make_async_copy(src, dst, sems.at[k]) for k, (src, dst) in enumerate(pairs)]
    for copy in copies:
        copy.start()
    for copy in copies:
        copy.wait()
    first_ref[0] = fork_ref[lax.axis_index("ctx")] * stride
    start = 0
    for down_ref, across_ref in zip(outs[::2], outs[1::2], strict=True):
        key = lax.broadcasted_iota(jnp.int32, down_ref.shape, 0) + start
        down_ref[...] = valid_keys(key, *sizes, fork_ref, owner_ref, lengths_ref).astype(F32)
        key = lax.broadcasted_iota(jnp.int32, (8, across_ref.shape[1]), 1) + start
        row = valid_keys(key, *sizes, fork_ref, owner_ref, lengths_ref).astype(F32)
        across_ref[...] = jnp.concatenate([row, row], axis=0).astype(BF16)
        start += down_ref.shape[0]


def split_keys(keys):
    keys = keys * (LOG2E * HD**-0.5)
    high = keys.astype(BF16)
    return jnp.concatenate([high, (keys - high.astype(F32)).astype(BF16)], axis=1)


def shard_keys(shards, seg_rows, prompt_rows, first, mask, fill, g):
    def rows(start, size):
        parts = [r[:, pl.ds(start, size), g * HD : (g + 1) * HD].astype(F32).reshape(-1, HD) for r in shards]
        return jnp.concatenate(parts, axis=0)

    prompt = rows(shards[0].shape[1] - 2 * prompt_rows, 2 * prompt_rows)
    keys = jnp.concatenate([rows(pl.multiple_of(first, 8), seg_rows), prompt], axis=0)
    shifted = pltpu.roll(prompt, prompt.shape[0] - prompt_rows, 0)
    values = jnp.concatenate([rows(pl.multiple_of(first + seg_rows, 8), seg_rows), shifted], axis=0)
    keys = split_keys(jnp.where(mask > 0, keys, fill))
    return keys, jnp.where(mask > 0, values, 0.0).astype(BF16)


def attend(q_ref, ready, causal, take, group):
    span, columns = q_ref.shape[1:]
    kept = {}

    def score(c):
        g = c * PAIR // group
        if g not in kept:
            kept.clear()
            kept[g] = ready(g)
        keys, values = kept[g]
        query = jnp.concatenate([q_ref[0, :, i * HD : (i + 1) * HD] for i in range(c * PAIR, (c + 1) * PAIR)], axis=0)
        query = jnp.concatenate([query, query], axis=1)
        scores = lax.dot_general(keys, query, (((1,), (1,)), ((), ())), preferred_element_type=F32)
        if causal is not None:
            own = scores[:span] + causal
            scores = jnp.concatenate([own, scores[span:]], axis=0) if scores.shape[0] > span else own
        return scores, jnp.max(scores, axis=0, keepdims=True), values

    chunks = columns // HD // PAIR
    made = score(0)
    for c in range(chunks):
        (scores, highest, values), made = made, score(c + 1) if c + 1 < chunks else None

        def weigh(top, scores=scores, values=values):
            weights = jnp.exp2(scores - top).astype(BF16)
            return jnp.dot(values, weights, preferred_element_type=F32)

        take(c, pl.ds(c * PAIR * span, PAIR * span), highest, weigh)


def near_kernel(seg_rows, prompt_rows, first_ref, q_hbm, own_hbm, down_ref, across_ref, *refs):
    *shards, q_ref, state_ref, fill_ref, own_ref, sems = refs
    span = q_ref.shape[1]
    kv_heads = own_ref.shape[2] // HD
    group = q_ref.shape[2] // HD // kv_heads
    own_copy = pltpu.make_async_copy(own_hbm, own_ref, sems.at[kv_heads])
    own_copy.start()
    parts = [pl.ds(g * group * HD, group * HD) for g in range(kv_heads)]
    copies = [pltpu.make_async_copy(q_hbm.at[:, :, p], q_ref.at[:, :, p], sems.at[g]) for g, p in enumerate(parts)]
    for copy in copies:
        copy.start()
    own_copy.wait()
    first = first_ref[0]
    own = jnp.swapaxes(own_ref[...], 0, 1)
    time = lax.broadcasted_iota(jnp.int32, (span, PAIR * span), 1) % span
    causal = jnp.where(lax.broadcasted_iota(jnp.int32, time.shape, 0) <= time, 0.0, -jnp.inf)

    def ready(g):
        copies[g].wait()
        part = slice(g * HD, (g + 1) * HD)
        keys = own[0, :, part].astype(F32)
        fill = keys[0:1]
        fill_ref[g] = jnp.broadcast_to(fill, (8, HD))
        keys, values = split_keys(keys), own[1, :, part]
        if shards:
            more = shard_keys(shards, seg_rows, prompt_rows, first, down_ref[span:], fill, g)
            keys, values = jnp.concatenate([keys, more[0]], axis=0), jnp.concatenate([values, more[1]], axis=0)
        return keys, jnp.concatenate([values.T, across_ref[...]], axis=0)

    def take(c, lanes, highest, weigh):
        state_ref[: HD + 8, lanes] = weigh(highest)[: HD + 8]
        state_ref[HD + 8 :, lanes] = jnp.broadcast_to(highest, (8, highest.shape[1]))

    attend(q_ref, ready, causal, take, group)


def far_kernel(seg_rows, prompt_rows, first_ref, q_ref, state_ref, fill_ref, down_ref, across_ref, *refs):
    *shards, out_ref, stage, sems = refs
    span, columns = q_ref.shape[1:]
    kv_heads = fill_ref.shape[0]
    group = columns // HD // kv_heads
    first = first_ref[0]
    copies = []

    def ready(g):
        keys, values = shard_keys(shards, seg_rows, prompt_rows, first, down_ref[...], fill_ref[g, 0:1], g)
        return keys, jnp.concatenate([values.T, across_ref[...]], axis=0)

    def take(c, lanes, highest, weigh):
        former = state_ref[HD + 8 :, lanes]
        top = jnp.maximum(former, highest)
        both = weigh(top[0:1])
        scale = jnp.exp2(former - top)
        share = 1.0 / (state_ref[HD : HD + 8, lanes] * scale + both[HD : HD + 8])
        scale = scale * share
        rows = (HD // 8, 8, -1)
        result = state_ref[:HD, lanes].reshape(rows) * scale[None] + both[:HD].reshape(rows) * share[None]
        result = result.reshape(HD, -1).astype(BF16)
        for k in range(PAIR):
            i = c * PAIR + k
            stage[:, i * HD : (i + 1) * HD] = result[:, k * span : (k + 1) * span].T
        if (c + 1) * PAIR % group == 0:
            g = c * PAIR // group
            part = pl.ds(g * group * HD, group * HD)
            copies.append(pltpu.make_async_copy(stage.at[:, part], out_ref.at[0, :, part], sems.at[g]))
            copies[-1].start()

    attend(q_ref, ready, None, take, group)
    for copy in copies:
        copy.wait()


def permute(x, target, n):
    return lax.ppermute(x, "ctx", [(i, target(i)) for i in range(n)])


def pair_steps(n):
    return range(n // 4 - 2, 0, -1)


def gather_shards(shard, n):
    far, near = n - 4, 2
    mate = permute(shard, lambda i: i ^ 1, n)
    first = permute(shard, lambda i: i ^ far, n)
    both = jnp.concatenate([shard, mate], axis=0)
    pairs = pair_steps(n)
    wide = [permute(both, lambda i, j=j: i ^ (2 * (2 * j + i % 2)), n) for j in pairs]
    side = permute(shard, lambda i: i ^ near, n)
    passed = permute(first, lambda i: i ^ near, n)
    mine = jnp.concatenate([first, passed, side, *wide], axis=0)
    theirs = permute(mine, lambda i: i ^ 1, n)
    got = [[far, far ^ near, near], [far, far ^ near, near]]
    for j in pairs:
        for core in range(2):
            d = 2 * (2 * j + core)
            got[core] += [d, d ^ 1]
    offsets = [[0, 1, *got[core], *[o ^ 1 for o in got[1 - core]]] for core in range(2)]
    return [shard, mate, mine, theirs], offsets


def use_gather(mesh_size, parents, seg_rows, prompt_rows):
    power = mesh_size >= 8 and mesh_size & (mesh_size - 1) == 0
    return power and parents * seg_rows + prompt_rows <= 2 * (seg_rows + prompt_rows)


def body(child_q, child_kv, prompt_kv, parent_kv, fork_list, owner_map, lengths):
    n = lax.axis_size("ctx")
    seg_rows, prompt_rows = parent_kv.shape[0], prompt_kv.shape[0]
    parents = parent_kv.shape[1]
    span, width = child_kv.shape[1], child_kv.shape[3]
    kv_heads = width // HD
    gather = use_gather(n, parents, seg_rows, prompt_rows)
    if gather:
        rows = 2 * (parents * seg_rows + prompt_rows)
        shard = pl.pallas_call(
            shard_kernel,
            out_shape=jax.ShapeDtypeStruct((rows, width), BF16),
            in_specs=[HBM, HBM],
            out_specs=VMEM,
            scratch_shapes=[
                pltpu.VMEM(prompt_kv.shape, BF16),
                pltpu.VMEM(parent_kv.shape, BF16),
                pltpu.SemaphoreType.DMA((2,)),
            ],
            compiler_params=limit(2),
            name="shard",
        )(*in_hbm(prompt_kv, parent_kv))
        shards, offsets = gather_shards(shard, n)
    else:
        rows = 2 * (seg_rows + prompt_rows)
        send = pl.pallas_call(
            pack_kernel,
            out_shape=jax.ShapeDtypeStruct((n, rows, width), BF16),
            in_specs=[SMEM, VMEM, VMEM],
            out_specs=VMEM,
            scratch_shapes=[pltpu.VMEM((parents, rows, width), BF16)],
            name="pack",
        )(fork_list, prompt_kv, parent_kv)
        shards, offsets = [lax.all_to_all(send, "ctx", split_axis=0, concat_axis=0, tiled=True)], None
    shards = [s.reshape(-1, rows, width) for s in shards]
    near, far = shards[: 2 * gather], shards[2 * gather :]
    counts = [sum(s.shape[0] for s in batch) for batch in (near, far)]
    slots = seg_rows + 2 * prompt_rows
    sizes = [span + counts[0] * slots, counts[1] * slots]
    masks = [jax.ShapeDtypeStruct(*shape) for k in sizes for shape in (((k, HD), F32), ((16, k), BF16))]
    stride = 2 * seg_rows if gather else 0
    near_down, near_across, far_down, far_across, first = pl.pallas_call(
        functools.partial(mask_kernel, (span, seg_rows, prompt_rows, counts, offsets), stride),
        out_shape=[*masks, jax.ShapeDtypeStruct((1,), jnp.int32)],
        in_specs=[HBM] * 3,
        out_specs=[VMEM] * 4 + [SMEM],
        scratch_shapes=[pltpu.SMEM(x.shape, jnp.int32) for x in (fork_list, owner_map, lengths)]
        + [pltpu.SemaphoreType.DMA((3,))],
        compiler_params=limit(4),
        name="mask",
    )(*in_hbm(fork_list, owner_map, lengths))
    query, state, fill = pl.pallas_call(
        functools.partial(near_kernel, seg_rows, prompt_rows),
        out_shape=[
            jax.ShapeDtypeStruct(child_q.shape, BF16),
            jax.ShapeDtypeStruct((HD + 16, child_q.shape[2] // HD * span), F32),
            jax.ShapeDtypeStruct((kv_heads, 8, HD), F32),
        ],
        in_specs=[SMEM, HBM, HBM, VMEM, VMEM] + [VMEM] * len(near),
        out_specs=[VMEM, VMEM, VMEM],
        scratch_shapes=[pltpu.VMEM(child_kv.shape[1:], BF16), pltpu.SemaphoreType.DMA((kv_heads + 1,))],
        compiler_params=limit(16),
        name="near",
    )(first, *in_hbm(child_q, child_kv[0]), near_down, near_across, *near)
    return pl.pallas_call(
        functools.partial(far_kernel, seg_rows, prompt_rows),
        out_shape=jax.ShapeDtypeStruct(child_q.shape, BF16),
        in_specs=[SMEM] + [VMEM] * (5 + len(far)),
        out_specs=HBM,
        scratch_shapes=[pltpu.VMEM(child_q.shape[1:], BF16), pltpu.SemaphoreType.DMA((kv_heads,))],
        compiler_params=limit(16 if gather else 48),
        name="far",
    )(first, query, state, fill, far_down, far_across, *far)


def solution(mesh):
    placed = (
        P(("groups", "ctx"), None, None),
        P(("groups", "ctx"), None, None, None),
        P(("groups", "ctx"), None, None),
        P(("groups", "ctx"), None, None, None),
        P("groups"),
        P("groups", None),
        P("groups"),
    )
    return jax.shard_map(
        body,
        mesh=mesh,
        in_specs=placed,
        out_specs=P(("groups", "ctx"), None, None),
        check_vma=False,
    )
```

time: 23.1 us -> 25.4 us (1.100)
  Pallas kernels: 5.08 us -> 10.7 us
  local copies, waits for them, and re-layouts: 2.73 us -> 0.03 us
  waiting for transfers between devices: 6.36 us -> 5.78 us
    pallas_call x2 -> x3, Pallas kernels: 5.05 us -> 9.85 us  [the longest x1 4.45 us: body(): pl.pallas_call(functools.partial(near_kernel, seg_rows, prompt_rows), out...]
    unnamed x18 -> x4, local copies, waits for them, and re-layouts: 2.72 us -> 0.02 us
    pallas_call x1, Pallas kernels: 0.03 us -> 0.81 us  [body(): pl.pallas_call(shard_kernel, out_shape=jax.ShapeDtypeStruct((rows, width)...]
    ppermute x7, waiting for transfers between devices: 6.36 us -> 5.78 us  [permute(): return lax.ppermute(x, 'ctx', [(i, target(i)) for i in range(n)])]
  transfers between devices with their start and end apart: 7 -> 7, of which waited for: 3 -> 2; matrix products, arithmetic and copies ran while one was open for 0% -> 0% of each run, Pallas kernels for 3% -> 23%
where the time goes in v3:
time: 25.4 us; the launch traced here: 25.1 us
  Pallas kernels  10.7 us (42%)
  starting transfers between devices  8.57 us (34%)
  waiting for transfers between devices  5.78 us (23%)
    ppermute x7, starting transfers between devices, permute(): return lax.ppermute(x, 'ctx', [(i, target(i)) for i in range(n)])  8.57 us
    ppermute x7, waiting for transfers between devices, permute(): return lax.ppermute(x, 'ctx', [(i, target(i)) for i in range(n)])  5.78 us
    pallas_call x1, Pallas kernels, body(): pl.pallas_call(functools.partial(near_kernel, seg_rows, prompt_rows), out...  4.45 us
    pallas_call x1, Pallas kernels, body(): pl.pallas_call(functools.partial(far_kernel, seg_rows, prompt_rows), out_...  4.08 us
    pallas_call x1, Pallas kernels, body(): pl.pallas_call(functools.partial(mask_kernel, (span, seg_rows, prompt_row...  1.32 us
    pallas_call x1, Pallas kernels, body(): pl.pallas_call(shard_kernel, out_shape=jax.ShapeDtypeStruct((rows, width)...  0.81 us
  transfers between devices with their start and end apart: 7, of which 2 were waited for; matrix products, arithmetic and copies ran while one was open for 0% of the time, Pallas kernels for 23%

profile of v3, /device:TPU:0, one launch (start us, length us, event | category | flops | bytes accessed | tf_op | source)
XLA Modules:
  0.0 25.1 jit_solution(23219830119699572)
XLA Ops:
  0.0 0.8 %shard.1 = bf16[40,512]{1,0:T(8,128)(2,1)S(1)} custom-call(bf16[4,2,512]{2,1,0:T(2,128)(2,1)} %prompt_hbm.1, bf16[8,2,2,512]{3,2,1,0:T(2,128)(2,1)} %parent_hbm.1), custom_call_target="tpu_custom_call" | custom-call | tf_op jit(solution)/shard_map/shard/pallas_call | solution.py:276
  0.8 0.6 %collective-permute-start = (bf16[40,512]{1,0:T(8,128)(2,1)S(1)}, bf16[40,512]{1,0:T(8,128)(2,1)S(1)}, u32[]{:S(2)}, u32[]{:S(2)}) collective-permute-start(bf16[40,512]{1,0:T(8,128)(2,1)S(1)} %shard.1), channel_id=1, source_target_pairs={{0,1},{1,0},{2,3},{3,2},{4,5},{5,4},{6,7},{7,6},{8,9},{9,8},{10,11... | collective-permute-start | bytes 122888 | tf_op jit(solution)/shard_map/ppermute | solution.py:235
  1.4 2.6 %collective-permute-start.3 = (bf16[40,512]{1,0:T(8,128)(2,1)S(1)}, bf16[40,512]{1,0:T(8,128)(2,1)S(1)}, u32[]{:S(2)}, u32[]{:S(2)}) collective-permute-start(bf16[40,512]{1,0:T(8,128)(2,1)S(1)} %shard.1), channel_id=1, source_target_pairs={{0,2},{1,3},{2,0},{3,1},{4,6},{5,7},{6,4},{7,5},{8,10},{9,11},{10,... | collective-permute-start | bytes 122888 | tf_op jit(solution)/shard_map/ppermute | solution.py:235
  3.9 3.6 %collective-permute-start.1 = (bf16[40,512]{1,0:T(8,128)(2,1)S(1)}, bf16[40,512]{1,0:T(8,128)(2,1)S(1)}, u32[]{:S(2)}, u32[]{:S(2)}) collective-permute-start(bf16[40,512]{1,0:T(8,128)(2,1)S(1)} %shard.1), channel_id=1, source_target_pairs={{0,12},{1,13},{2,14},{3,15},{4,8},{5,9},{6,10},{7,11},{8,4},{9,5},... | collective-permute-start | bytes 122888 | tf_op jit(solution)/shard_map/ppermute | solution.py:235
  7.5 0.0 collective-permute-done
  7.5 0.1 collective-permute-start.5
  7.6 0.8 %collective-permute-start.4 = (bf16[80,512]{1,0:T(8,128)(2,1)S(1)}, bf16[80,512]{1,0:T(8,128)(2,1)S(1)}, u32[]{:S(2)}, u32[]{:S(2)}) collective-permute-start(bf16[80,512]{1,0:T(8,128)(2,1)S(1)} %pad_maximum_fusion), channel_id=1, source_target_pairs={{0,8},{1,11},{2,10},{3,9},{4,12},{5,15},{6,14},{7,13},{8,0},{9,3},... | collective-permute-start | bytes 245768 | tf_op jit(solution)/shard_map/ppermute | solution.py:235
  8.4 1.8 %collective-permute-done.1 = bf16[40,512]{1,0:T(8,128)(2,1)S(1)} collective-permute-done((bf16[40,512]{1,0:T(8,128)(2,1)S(1)}, bf16[40,512]{1,0:T(8,128)(2,1)S(1)}, u32[]{:S(2)}, u32[]{:S(2)}) %collective-permute-start.1) | collective-permute-done | bytes 40992 | tf_op jit(solution)/shard_map/ppermute | solution.py:235
  10.2 0.0 collective-permute-start.2
  10.2 4.0 %collective-permute-done.2 = bf16[40,512]{1,0:T(8,128)(2,1)S(1)} collective-permute-done((bf16[40,512]{1,0:T(8,128)(2,1)S(1)}, bf16[40,512]{1,0:T(8,128)(2,1)S(1)}, u32[]{:S(2)}, u32[]{:S(2)}) %collective-permute-start.2) | collective-permute-done | bytes 40992 | tf_op jit(solution)/shard_map/ppermute | solution.py:235
  14.2 0.0 collective-permute-done.3
  14.2 0.0 collective-permute-done.4
  14.2 0.0 collective-permute-done.5
  14.2 1.0 %collective-permute-start.6 = (bf16[280,512]{1,0:T(8,128)(2,1)S(1)}, bf16[280,512]{1,0:T(8,128)(2,1)S(1)}, u32[]{:S(2)}, u32[]{:S(2)}) collective-permute-start(bf16[280,512]{1,0:T(8,128)(2,1)S(1)} %constant_dynamic-update-slice_fusion), channel_id=1, source_target_pairs={{0,1},{1,0},{2,3},{3,2},{4,5},{5,4},{6,7},{7,6},{8,9},{9,8},{10,11... | collective-permute-start | bytes 860168 | tf_op jit(solution)/shard_map/ppermute | solution.py:235
  15.2 1.3 %mask.1 = (f32[160,128]{1,0:T(8,128)S(1)}, bf16[16,160]{1,0:T(8,128)(2,1)S(1)}, f32[224,128]{1,0:T(8,128)S(1)}, bf16[16,224]{1,0:T(8,128)(2,1)S(1)}, s32[1]{0:T(128)}) custom-call(s32[16]{0:T(128)} %fork_hbm.1, s32[2,16]{1,0:T(2,128)} %owner_hbm.1, s32[2]{0:T(128)} %lengths_hbm.1), custom_call_target="tpu_custom_call" | custom-call | tf_op jit(solution)/shard_map/mask/pallas_call | solution.py:308
  16.6 4.5 %near.1 = (bf16[1,128,4096]{2,1,0:T(8,128)(2,1)S(1)}, f32[144,4096]{1,0:T(8,128)S(1)}, f32[4,8,128]{2,1,0:T(8,128)S(1)}) custom-call(s32[1]{0:T(128)} %get-tuple-element.13.first_ref, bf16[1,128,4096]{2,1,0:T(8,128)(2,1)} %q_hbm.1, bf16[128,2,512]{2,1,0:T(2,128)(2,1)} %bitcast.9, f32[160,128]{1,0:T(8,128)S(1)} %get-tuple-element.14.down_ref, ...), custom_call_target="tpu_custom_call" | custom-call | tf_op jit(solution)/shard_map/near/pallas_call | solution.py:318
  21.0 0.0 collective-permute-done.6
  21.0 4.1 %far.1 = bf16[1,128,4096]{2,1,0:T(8,128)(2,1)} custom-call(s32[1]{0:T(128)} %get-tuple-element.13.first_ref, bf16[1,128,4096]{2,1,0:T(8,128)(2,1)S(1)} %get-tuple-element.16.q_ref, f32[144,4096]{1,0:T(8,128)S(1)} %get-tuple-element.17.state_ref, f32[4,8,128]{2,1,0:T(8,128)S(1)} %get-tuple-element.18.fill_ref, f32[224,128]{1,0:T(8,128)S(1)} %get-tuple-element.19.down_ref, ...), custom_call_target="tpu_custom_call" | custom-call | tf_op jit(solution)/shard_map/far/pallas_call | solution.py:331
  (6 shorter events, 0.0 us)
Async XLA Ops:
  0.8 6.7 %collective-permute-start = (bf16[40,512]{1,0:T(8,128)(2,1)S(1)}, bf16[40,512]{1,0:T(8,128)(2,1)S(1)}, u32[]{:S(2)}, u32[]{:S(2)}) collective-permute-start(bf16[40,512]{1,0:T(8,128)(2,1)S(1)} %shard.1), channel_id=1, source_target_pairs={{0,1},{1,0},{2,3},{3,2},{4,5},{5,4},{6,7},{7,6},{8,9},{9,8},{10,11... | collective-permute-start | bytes 122888 | tf_op jit(solution)/shard_map/ppermute | solution.py:235
  1.4 12.8 %collective-permute-start.3 = (bf16[40,512]{1,0:T(8,128)(2,1)S(1)}, bf16[40,512]{1,0:T(8,128)(2,1)S(1)}, u32[]{:S(2)}, u32[]{:S(2)}) collective-permute-start(bf16[40,512]{1,0:T(8,128)(2,1)S(1)} %shard.1), channel_id=1, source_target_pairs={{0,2},{1,3},{2,0},{3,1},{4,6},{5,7},{6,4},{7,5},{8,10},{9,11},{10,... | collective-permute-start | bytes 122888 | tf_op jit(solution)/shard_map/ppermute | solution.py:235
  3.9 6.2 %collective-permute-start.1 = (bf16[40,512]{1,0:T(8,128)(2,1)S(1)}, bf16[40,512]{1,0:T(8,128)(2,1)S(1)}, u32[]{:S(2)}, u32[]{:S(2)}) collective-permute-start(bf16[40,512]{1,0:T(8,128)(2,1)S(1)} %shard.1), channel_id=1, source_target_pairs={{0,12},{1,13},{2,14},{3,15},{4,8},{5,9},{6,10},{7,11},{8,4},{9,5},... | collective-permute-start | bytes 122888 | tf_op jit(solution)/shard_map/ppermute | solution.py:235
  7.5 6.7 %collective-permute-start.5 = (bf16[80,512]{1,0:T(8,128)(2,1)S(1)}, bf16[80,512]{1,0:T(8,128)(2,1)S(1)}, u32[]{:S(2)}, u32[]{:S(2)}) collective-permute-start(bf16[80,512]{1,0:T(8,128)(2,1)S(1)} %pad_maximum_fusion), channel_id=1, source_target_pairs={{0,4},{1,7},{2,6},{3,5},{4,0},{5,3},{6,2},{7,1},{8,12},{9,15},{10,... | collective-permute-start | bytes 245768 | tf_op jit(solution)/shard_map/ppermute | solution.py:235
  7.6 6.6 %collective-permute-start.4 = (bf16[80,512]{1,0:T(8,128)(2,1)S(1)}, bf16[80,512]{1,0:T(8,128)(2,1)S(1)}, u32[]{:S(2)}, u32[]{:S(2)}) collective-permute-start(bf16[80,512]{1,0:T(8,128)(2,1)S(1)} %pad_maximum_fusion), channel_id=1, source_target_pairs={{0,8},{1,11},{2,10},{3,9},{4,12},{5,15},{6,14},{7,13},{8,0},{9,3},... | collective-permute-start | bytes 245768 | tf_op jit(solution)/shard_map/ppermute | solution.py:235
  10.2 4.0 %collective-permute-start.2 = (bf16[40,512]{1,0:T(8,128)(2,1)S(1)}, bf16[40,512]{1,0:T(8,128)(2,1)S(1)}, u32[]{:S(2)}, u32[]{:S(2)}) collective-permute-start(bf16[40,512]{1,0:T(8,128)(2,1)S(1)} %collective-permute-done.1), channel_id=1, source_target_pairs={{0,2},{1,3},{2,0},{3,1},{4,6},{5,7},{6,4},{7,5},{8,10},{9,11},{10,... | collective-permute-start | bytes 122888 | tf_op jit(solution)/shard_map/ppermute | solution.py:235
  14.2 6.8 %collective-permute-start.6 = (bf16[280,512]{1,0:T(8,128)(2,1)S(1)}, bf16[280,512]{1,0:T(8,128)(2,1)S(1)}, u32[]{:S(2)}, u32[]{:S(2)}) collective-permute-start(bf16[280,512]{1,0:T(8,128)(2,1)S(1)} %constant_dynamic-update-slice_fusion), channel_id=1, source_target_pairs={{0,1},{1,0},{2,3},{3,2},{4,5},{5,4},{6,7},{7,6},{8,9},{9,8},{10,11... | collective-permute-start | bytes 860168 | tf_op jit(solution)/shard_map/ppermute | solution.py:235

commit v4 on v3

v4 whole, which is shorter than its diff:
```python
import functools

import jax
import jax.numpy as jnp
from jax import lax
from jax.experimental import pallas as pl
from jax.experimental.pallas import tpu as pltpu
from jax.sharding import PartitionSpec as P

HD = 128
LOG2E = 1.4426950408889634
F32 = jnp.float32
BF16 = jnp.bfloat16
NEAR_HEADS, FAR_HEADS = 4, 8
VMEM = pl.BlockSpec(memory_space=pltpu.VMEM)
SMEM = pl.BlockSpec(memory_space=pltpu.SMEM)
HBM = pl.BlockSpec(memory_space=pltpu.HBM)


def in_hbm(*arrays):
    return [pltpu.with_memory_space_constraint(x, pltpu.HBM) for x in arrays]


def limit(mib):
    return pltpu.CompilerParams(vmem_limit_bytes=mib << 20)


def shard_rows(prompt_ref, parent_ref):
    prompt = prompt_ref[...].astype(F32)
    rows = []
    for p in range(parent_ref.shape[1]):
        piece = parent_ref[:, p].astype(F32)
        rows += [piece[:, 0, :], piece[:, 1, :]]
    return rows, [prompt[:, 0, :], prompt[:, 1, :]]


def shard_kernel(prompt_hbm, parent_hbm, out_ref, wide_ref, prompt_ref, parent_ref, sems):
    copies = [
        pltpu.make_async_copy(parent_hbm, parent_ref, sems.at[0]),
        pltpu.make_async_copy(prompt_hbm, prompt_ref, sems.at[1]),
    ]
    for copy in copies:
        copy.start()
    for copy in copies:
        copy.wait()
    pieces, shared = shard_rows(prompt_ref, parent_ref)
    rows = jnp.concatenate(pieces + shared, axis=0)
    out_ref[...] = rows.astype(BF16)
    wide_ref[...] = jnp.concatenate([rows, jnp.zeros_like(rows)], axis=0).astype(BF16)


def pack_kernel(fork_ref, prompt_ref, parent_ref, send_ref, table_ref):
    pieces, shared = shard_rows(prompt_ref, parent_ref)
    for p in range(parent_ref.shape[1]):
        table_ref[p] = jnp.concatenate(pieces[2 * p : 2 * p + 2] + shared, axis=0).astype(BF16)

    def place(d, carry):
        send_ref[d] = table_ref[fork_ref[d]]
        return carry

    lax.fori_loop(0, send_ref.shape[0], place, 0, unroll=min(8, send_ref.shape[0]))


def valid_keys(key, seg_rows, prompt_rows, counts, offsets, fork_ref, owner_ref, lengths_ref):
    n = owner_ref.shape[1]
    device = lax.axis_index("ctx")
    parent = fork_ref[device]
    place, row = jnp.full_like(key, -1), jnp.zeros_like(key)
    prompt = key < 0
    start, shard = 0, 0
    for count in counts:
        slot = key - start
        here = (slot >= 0) & (slot < count * seg_rows)
        place = jnp.where(here, shard + slot // seg_rows, place)
        row = jnp.where(here, slot % seg_rows, row)
        slot = slot - count * seg_rows
        here = (slot >= 0) & (slot < count * 2 * prompt_rows)
        prompt = prompt | (here & (slot % (2 * prompt_rows) < prompt_rows))
        start += count * (seg_rows + 2 * prompt_rows)
        shard += count
    block = place
    if offsets is not None:
        block = jnp.full_like(key, -1)
        for k in range(n):
            owner = device ^ jnp.where(device % 2 == 0, offsets[0][k], offsets[1][k])
            block = jnp.where(place == k, owner, block)

    def step(j, position):
        return jnp.where(block == owner_ref[parent, j], j * seg_rows + row, position)

    beyond = jnp.full_like(key, n * seg_rows)
    position = lax.fori_loop(0, n, step, beyond, unroll=min(16, n))
    return prompt | (position < lengths_ref[parent])


def split_keys(keys):
    keys = keys * (LOG2E * HD**-0.5)
    high = keys.astype(BF16)
    return jnp.concatenate([high, (keys - high.astype(F32)).astype(BF16)], axis=1)


def shard_keys(shards, seg_rows, prompt_rows, first, mask, fill, g):
    def rows(start, size):
        parts = [r[:, pl.ds(start, size), g * HD : (g + 1) * HD].astype(F32).reshape(-1, HD) for r in shards]
        return jnp.concatenate(parts, axis=0)

    prompt = rows(shards[0].shape[1] - 2 * prompt_rows, 2 * prompt_rows)
    keys = jnp.concatenate([rows(pl.multiple_of(first, 8), seg_rows), prompt], axis=0)
    shifted = pltpu.roll(prompt, prompt.shape[0] - prompt_rows, 0)
    values = jnp.concatenate([rows(pl.multiple_of(first + seg_rows, 8), seg_rows), shifted], axis=0)
    keys = split_keys(jnp.where(mask > 0, keys, fill))
    return keys, jnp.where(mask > 0, values, 0.0).astype(BF16)


def attend(q_ref, ready, causal, take, group, many):
    span, columns = q_ref.shape[1:]
    kept = {}

    def score(c):
        g = c * many // group
        if g not in kept:
            kept.clear()
            kept[g] = ready(g)
        keys, values = kept[g]
        query = jnp.concatenate([q_ref[0, :, i * HD : (i + 1) * HD] for i in range(c * many, (c + 1) * many)], axis=0)
        query = jnp.concatenate([query, query], axis=1)
        scores = lax.dot_general(keys, query, (((1,), (1,)), ((), ())), preferred_element_type=F32)
        if causal is not None:
            own = scores[:span] + causal
            scores = jnp.concatenate([own, scores[span:]], axis=0) if scores.shape[0] > span else own
        return scores, jnp.max(scores, axis=0, keepdims=True), values

    chunks = columns // HD // many
    made = score(0)
    for c in range(chunks):
        (scores, highest, values), made = made, score(c + 1) if c + 1 < chunks else None

        def weigh(top, scores=scores, values=values):
            weights = jnp.exp2(scores - top).astype(BF16)
            return jnp.dot(values, weights, preferred_element_type=F32)

        take(c, pl.ds(c * many * span, many * span), highest, weigh)


def near_kernel(sizes, stride, *refs):
    ins, refs = refs[:5], refs[5:]
    q_ref, state_ref, fill_ref, down_ref, across_ref, first_ref, own_ref, own_kv_ref, *tables, sems = refs
    fork_ref, owner_ref, lengths_ref = tables
    span = q_ref.shape[1]
    kv_heads = own_ref.shape[2] // HD
    group = q_ref.shape[2] // HD // kv_heads
    pairs = list(zip(ins[1:], (own_ref, *tables), strict=True))
    for g in range(kv_heads):
        part = pl.ds(g * group * HD, group * HD)
        pairs.append((ins[0].at[:, :, part], q_ref.at[:, :, part]))
    copies = [pltpu.make_async_copy(src, dst, sems.at[k]) for k, (src, dst) in enumerate(pairs)]
    for copy in copies:
        copy.start()
    for copy in copies[:4]:
        copy.wait()
    first_ref[0] = fork_ref[lax.axis_index("ctx")] * stride
    key = lax.broadcasted_iota(jnp.int32, (8, across_ref.shape[1]), 1)
    valid = valid_keys(key, *sizes, fork_ref, owner_ref, lengths_ref).astype(F32)
    across_ref[...] = jnp.concatenate([valid, valid], axis=0).astype(BF16)
    down_ref[...] = jnp.concatenate([valid] * (HD // 8), axis=0).T
    own_kv_ref[...] = jnp.swapaxes(own_ref[...], 0, 1)
    time = lax.broadcasted_iota(jnp.int32, (span, NEAR_HEADS * span), 1) % span
    causal = jnp.where(lax.broadcasted_iota(jnp.int32, time.shape, 0) <= time, 0.0, -jnp.inf)
    ones = jnp.ones((16, span), BF16)

    def ready(g):
        copies[4 + g].wait()
        part = slice(g * HD, (g + 1) * HD)
        keys = own_kv_ref[0, :, part].astype(F32)
        fill_ref[g] = jnp.broadcast_to(keys[0:1], (8, HD))
        return split_keys(keys), jnp.concatenate([own_kv_ref[1, :, part].T, ones], axis=0)

    def take(c, lanes, highest, weigh):
        state_ref[: HD + 8, lanes] = weigh(highest)[: HD + 8]
        state_ref[HD + 8 :, lanes] = jnp.broadcast_to(highest, (8, highest.shape[1]))

    attend(q_ref, ready, causal, take, group, NEAR_HEADS)


def ready_kernel(seg_rows, prompt_rows, first_ref, fill_ref, down_ref, *refs):
    *shards, keys_ref, values_ref = refs
    for g in range(fill_ref.shape[0]):
        mask = down_ref[: keys_ref.shape[1]]
        made = shard_keys(shards, seg_rows, prompt_rows, first_ref[0], mask, fill_ref[g, 0:1], g)
        keys_ref[g], values_ref[g] = made


def far_kernel(seg_rows, prompt_rows, count, first_ref, q_ref, state_ref, fill_ref, down_ref, across_ref, *refs):
    shards, (*former_refs, out_ref, stage, sems) = refs[:count], refs[count:]
    span, columns = q_ref.shape[1:]
    kv_heads = fill_ref.shape[0]
    group = columns // HD // kv_heads
    first = first_ref[0]
    copies = []

    def ready(g):
        known = former_refs[0].shape[1] if former_refs else 0
        keys, values = shard_keys(shards, seg_rows, prompt_rows, first, down_ref[known:], fill_ref[g, 0:1], g)
        if former_refs:
            keys = jnp.concatenate([former_refs[0][g], keys], axis=0)
            values = jnp.concatenate([former_refs[1][g], values], axis=0)
        return keys, jnp.concatenate([values.T, across_ref[...]], axis=0)

    def take(c, lanes, highest, weigh):
        former = state_ref[HD + 8 :, lanes]
        top = jnp.maximum(former, highest)
        both = weigh(top[0:1])
        scale = jnp.exp2(former - top)
        share = 1.0 / (state_ref[HD : HD + 8, lanes] * scale + both[HD : HD + 8])
        scale = scale * share
        rows = (HD // 8, 8, -1)
        result = state_ref[:HD, lanes].reshape(rows) * scale[None] + both[:HD].reshape(rows) * share[None]
        result = result.reshape(HD, -1).astype(BF16)
        for k in range(FAR_HEADS):
            i = c * FAR_HEADS + k
            stage[:, i * HD : (i + 1) * HD] = result[:, k * span : (k + 1) * span].T
        if (c + 1) * FAR_HEADS % group == 0:
            g = c * FAR_HEADS // group
            part = pl.ds(g * group * HD, group * HD)
            copies.append(pltpu.make_async_copy(stage.at[:, part], out_ref.at[0, :, part], sems.at[g]))
            copies[-1].start()

    attend(q_ref, ready, None, take, group, FAR_HEADS)
    for copy in copies:
        copy.wait()


def permute(x, target, n):
    return lax.ppermute(x, "ctx", [(i, target(i)) for i in range(n)])


def pair_steps(n):
    return range(n // 4 - 2, 0, -1)


def gather_shards(shard, both, n):
    far, near = n - 4, 2
    mate = permute(shard, lambda i: i ^ 1, n)
    first = permute(shard, lambda i: i ^ far, n)
    both = lax.dynamic_update_slice(both, mate, (shard.shape[0], 0))
    pairs = pair_steps(n)
    wide = [permute(both, lambda i, j=j: i ^ (2 * (2 * j + i % 2)), n) for j in pairs]
    passed = permute(jnp.concatenate([shard, first], axis=0), lambda i: i ^ near, n)
    mine = jnp.concatenate([first, passed, *wide], axis=0)
    theirs = permute(mine, lambda i: i ^ 1, n)
    got = [[far, near, far ^ near], [far, near, far ^ near]]
    for j in pairs:
        for core in range(2):
            d = 2 * (2 * j + core)
            got[core] += [d, d ^ 1]
    offsets = [[0, 1, *got[core], *[o ^ 1 for o in got[1 - core]]] for core in range(2)]
    return [shard, mate, mine, theirs], offsets


def use_gather(mesh_size, parents, seg_rows, prompt_rows):
    power = mesh_size >= 8 and mesh_size & (mesh_size - 1) == 0
    return power and parents * seg_rows + prompt_rows <= 2 * (seg_rows + prompt_rows)


def body(child_q, child_kv, prompt_kv, parent_kv, fork_list, owner_map, lengths):
    n = lax.axis_size("ctx")
    seg_rows, prompt_rows = parent_kv.shape[0], prompt_kv.shape[0]
    parents = parent_kv.shape[1]
    span, width = child_kv.shape[1], child_kv.shape[3]
    kv_heads = width // HD
    gather = use_gather(n, parents, seg_rows, prompt_rows)
    if gather:
        rows = 2 * (parents * seg_rows + prompt_rows)
        shard, both = pl.pallas_call(
            shard_kernel,
            out_shape=[jax.ShapeDtypeStruct((k * rows, width), BF16) for k in (1, 2)],
            in_specs=[HBM, HBM],
            out_specs=[VMEM, VMEM],
            scratch_shapes=[
                pltpu.VMEM(prompt_kv.shape, BF16),
                pltpu.VMEM(parent_kv.shape, BF16),
                pltpu.SemaphoreType.DMA((2,)),
            ],
            compiler_params=limit(2),
            name="shard",
        )(*in_hbm(prompt_kv, parent_kv))
        shards, offsets = gather_shards(shard, both, n)
    else:
        rows = 2 * (seg_rows + prompt_rows)
        send = pl.pallas_call(
            pack_kernel,
            out_shape=jax.ShapeDtypeStruct((n, rows, width), BF16),
            in_specs=[SMEM, VMEM, VMEM],
            out_specs=VMEM,
            scratch_shapes=[pltpu.VMEM((parents, rows, width), BF16)],
            name="pack",
        )(fork_list, prompt_kv, parent_kv)
        shards, offsets = [lax.all_to_all(send, "ctx", split_axis=0, concat_axis=0, tiled=True)], None
    shards = [s.reshape(-1, rows, width) for s in shards]
    batches = [shards[:-1], shards[-1:]] if gather else [shards]
    counts = [sum(s.shape[0] for s in batch) for batch in batches]
    slots = seg_rows + 2 * prompt_rows
    query, state, fill, down, across, first = pl.pallas_call(
        functools.partial(near_kernel, (seg_rows, prompt_rows, counts, offsets), 2 * seg_rows if gather else 0),
        out_shape=[
            jax.ShapeDtypeStruct(child_q.shape, BF16),
            jax.ShapeDtypeStruct((HD + 16, child_q.shape[2] // HD * span), F32),
            jax.ShapeDtypeStruct((kv_heads, 8, HD), F32),
            jax.ShapeDtypeStruct((n * slots, HD), F32),
            jax.ShapeDtypeStruct((16, n * slots), BF16),
            jax.ShapeDtypeStruct((1,), jnp.int32),
        ],
        in_specs=[HBM] * 5,
        out_specs=[VMEM] * 5 + [SMEM],
        scratch_shapes=[
            pltpu.VMEM(child_kv.shape[1:], BF16),
            pltpu.VMEM((2, span, width), BF16),
            *[pltpu.SMEM(x.shape, jnp.int32) for x in (fork_list, owner_map, lengths)],
            pltpu.SemaphoreType.DMA((4 + kv_heads,)),
        ],
        compiler_params=limit(16),
        name="near",
    )(*in_hbm(child_q, child_kv[0], fork_list, owner_map, lengths))
    former = []
    if gather:
        former = pl.pallas_call(
            functools.partial(ready_kernel, seg_rows, prompt_rows),
            out_shape=[jax.ShapeDtypeStruct((kv_heads, counts[0] * slots, k * HD), BF16) for k in (2, 1)],
            in_specs=[SMEM] + [VMEM] * (2 + len(batches[0])),
            out_specs=[VMEM] * 2,
            compiler_params=limit(4),
            name="ready",
        )(first, fill, down, *batches[0])
    last = batches[-1]
    return pl.pallas_call(
        functools.partial(far_kernel, seg_rows, prompt_rows, len(last)),
        out_shape=jax.ShapeDtypeStruct(child_q.shape, BF16),
        in_specs=[SMEM] + [VMEM] * (5 + len(last) + len(former)),
        out_specs=HBM,
        scratch_shapes=[pltpu.VMEM(child_q.shape[1:], BF16), pltpu.SemaphoreType.DMA((kv_heads,))],
        compiler_params=limit(16 if gather else 48),
        name="far",
    )(first, query, state, fill, down, across, *last, *former)


def solution(mesh):
    placed = (
        P(("groups", "ctx"), None, None),
        P(("groups", "ctx"), None, None, None),
        P(("groups", "ctx"), None, None),
        P(("groups", "ctx"), None, None, None),
        P("groups"),
        P("groups", None),
        P("groups"),
    )
    return jax.shard_map(
        body,
        mesh=mesh,
        in_specs=placed,
        out_specs=P(("groups", "ctx"), None, None),
        check_vma=False,
    )
```

time: 25.4 us -> 21.6 us (0.85)
  Pallas kernels: 10.7 us -> 8.06 us
  waiting for transfers between devices: 5.78 us -> 4.78 us
    pallas_call x4, Pallas kernels: 10.7 us -> 8.06 us  [the longest x1 3.3 us: body(): pl.pallas_call(functools.partial(near_kernel, (seg_rows, prompt_rows, cou...]
    ppermute x7 -> x6, waiting for transfers between devices: 5.78 us -> 4.78 us  [permute(): return lax.ppermute(x, 'ctx', [(i, target(i)) for i in range(n)])]
    ppermute x7 -> x6, starting transfers between devices: 8.57 us -> 8.48 us  [permute(): return lax.ppermute(x, 'ctx', [(i, target(i)) for i in range(n)])]
  transfers between devices with their start and end apart: 7 -> 6, of which waited for: 2 -> 3; matrix products, arithmetic and copies ran while one was open for 0% -> 0% of each run, Pallas kernels for 23% -> 19%
where the time goes in v4:
time: 21.6 us; the launch traced here: 21.4 us
  starting transfers between devices  8.48 us (39%)
  Pallas kernels  8.06 us (37%)
  waiting for transfers between devices  4.78 us (22%)
    ppermute x6, starting transfers between devices, permute(): return lax.ppermute(x, 'ctx', [(i, target(i)) for i in range(n)])  8.48 us
    ppermute x6, waiting for transfers between devices, permute(): return lax.ppermute(x, 'ctx', [(i, target(i)) for i in range(n)])  4.78 us
    pallas_call x1, Pallas kernels, body(): pl.pallas_call(functools.partial(near_kernel, (seg_rows, prompt_rows, cou...  3.3 us
    pallas_call x1, Pallas kernels, body(): pl.pallas_call(functools.partial(far_kernel, seg_rows, prompt_rows, len(l...  3.16 us
    pallas_call x1, Pallas kernels, body(): pl.pallas_call(shard_kernel, out_shape=[jax.ShapeDtypeStruct((k * rows, w...  0.81 us
    pallas_call x1, Pallas kernels, body(): pl.pallas_call(functools.partial(ready_kernel, seg_rows, prompt_rows), ou...  0.79 us
  transfers between devices with their start and end apart: 6, of which 3 were waited for; matrix products, arithmetic and copies ran while one was open for 0% of the time, Pallas kernels for 19%

profile of v4, /device:TPU:0, one launch (start us, length us, event | category | flops | bytes accessed | tf_op | source)
XLA Modules:
  0.0 21.4 jit_solution(12893220067873695251)
XLA Ops:
  0.0 0.8 %shard.1 = (bf16[40,512]{1,0:T(8,128)(2,1)S(1)}, bf16[80,512]{1,0:T(8,128)(2,1)S(1)}) custom-call(bf16[4,2,512]{2,1,0:T(2,128)(2,1)} %prompt_hbm.1, bf16[8,2,2,512]{3,2,1,0:T(2,128)(2,1)} %parent_hbm.1), custom_call_target="tpu_custom_call" | custom-call | tf_op jit(solution)/shard_map/shard/pallas_call | solution.py:274
  0.8 0.6 %collective-permute-start.2 = (bf16[40,512]{1,0:T(8,128)(2,1)S(1)}, bf16[40,512]{1,0:T(8,128)(2,1)S(1)}, u32[]{:S(2)}, u32[]{:S(2)}) collective-permute-start(bf16[40,512]{1,0:T(8,128)(2,1)S(1)} %get-tuple-element.21), channel_id=1, source_target_pairs={{0,1},{1,0},{2,3},{3,2},{4,5},{5,4},{6,7},{7,6},{8,9},{9,8},{10,11... | collective-permute-start | bytes 122888 | tf_op jit(solution)/shard_map/ppermute | solution.py:234
  1.4 4.7 %collective-permute-start = (bf16[40,512]{1,0:T(8,128)(2,1)S(1)}, bf16[40,512]{1,0:T(8,128)(2,1)S(1)}, u32[]{:S(2)}, u32[]{:S(2)}) collective-permute-start(bf16[40,512]{1,0:T(8,128)(2,1)S(1)} %get-tuple-element.21), channel_id=1, source_target_pairs={{0,12},{1,13},{2,14},{3,15},{4,8},{5,9},{6,10},{7,11},{8,4},{9,5},... | collective-permute-start | bytes 122888 | tf_op jit(solution)/shard_map/ppermute | solution.py:234
  6.0 0.0 collective-permute-done.2
  6.0 0.0 collective-permute-start.4
  6.1 1.7 %collective-permute-start.3 = (bf16[80,512]{1,0:T(8,128)(2,1)S(1)}, bf16[80,512]{1,0:T(8,128)(2,1)S(1)}, u32[]{:S(2)}, u32[]{:S(2)}) collective-permute-start(bf16[80,512]{1,0:T(8,128)(2,1)S(1)} %constant_dynamic-update-slice_fusion.4), channel_id=1, source_target_pairs={{0,8},{1,11},{2,10},{3,9},{4,12},{5,15},{6,14},{7,13},{8,0},{9,3},... | collective-permute-start | bytes 245768 | tf_op jit(solution)/shard_map/ppermute | solution.py:234
  7.7 0.6 %collective-permute-done = bf16[40,512]{1,0:T(8,128)(2,1)S(1)} collective-permute-done((bf16[40,512]{1,0:T(8,128)(2,1)S(1)}, bf16[40,512]{1,0:T(8,128)(2,1)S(1)}, u32[]{:S(2)}, u32[]{:S(2)}) %collective-permute-start) | collective-permute-done | bytes 40992 | tf_op jit(solution)/shard_map/ppermute | solution.py:234
  8.3 1.5 %collective-permute-start.1 = (bf16[80,512]{1,0:T(8,128)(2,1)S(1)}, bf16[80,512]{1,0:T(8,128)(2,1)S(1)}, u32[]{:S(2)}, u32[]{:S(2)}) collective-permute-start(bf16[80,512]{1,0:T(8,128)(2,1)S(1)} %pad_maximum_fusion), channel_id=1, source_target_pairs={{0,2},{1,3},{2,0},{3,1},{4,6},{5,7},{6,4},{7,5},{8,10},{9,11},{10,... | collective-permute-start | bytes 245768 | tf_op jit(solution)/shard_map/ppermute | solution.py:234
  9.8 3.7 %collective-permute-done.1 = bf16[80,512]{1,0:T(8,128)(2,1)S(1)} collective-permute-done((bf16[80,512]{1,0:T(8,128)(2,1)S(1)}, bf16[80,512]{1,0:T(8,128)(2,1)S(1)}, u32[]{:S(2)}, u32[]{:S(2)}) %collective-permute-start.1) | collective-permute-done | bytes 81952 | tf_op jit(solution)/shard_map/ppermute | solution.py:234
  13.5 0.5 %collective-permute-done.3 = bf16[80,512]{1,0:T(8,128)(2,1)S(1)} collective-permute-done((bf16[80,512]{1,0:T(8,128)(2,1)S(1)}, bf16[80,512]{1,0:T(8,128)(2,1)S(1)}, u32[]{:S(2)}, u32[]{:S(2)}) %collective-permute-start.3) | collective-permute-done | bytes 81952 | tf_op jit(solution)/shard_map/ppermute | solution.py:234
  14.0 0.0 collective-permute-done.4
  14.1 0.1 collective-permute-start.5
  14.1 3.3 %near.1 = (bf16[1,128,4096]{2,1,0:T(8,128)(2,1)S(1)}, f32[144,4096]{1,0:T(8,128)S(1)}, f32[4,8,128]{2,1,0:T(8,128)S(1)}, f32[256,128]{1,0:T(8,128)S(1)}, bf16[16,256]{1,0:T(8,128)(2,1)S(1)}, /*index=5*/s32[1]{0:T(128)}) custom-call(bf16[1,128,4096]{2,1,0:T(8,128)(2,1)} %refs_0_.1, bf16[128,2,512]{2,1,0:T(2,128)(2,1)} %bitcast.9, s32[16]{0:T(128)} %refs_2_.1, ...), custom_call_target="tpu_custom_call" | custom-call | tf_op jit(solution)/shard_map/near/pallas_call | solution.py:303
  17.5 0.8 %ready.1 = (bf16[4,144,256]{2,1,0:T(8,128)(2,1)S(1)}, bf16[4,144,128]{2,1,0:T(8,128)(2,1)S(1)}) custom-call(s32[1]{0:T(128)} %get-tuple-element.15.first_ref, f32[4,8,128]{2,1,0:T(8,128)S(1)} %get-tuple-element.18.fill_ref, f32[256,128]{1,0:T(8,128)S(1)} %get-tuple-element.19.down_ref, bf16[1,40,512]{2,1,0:T(8,128)(2,1)S(1)} %bitcast.7, ...), custom_call_target="tpu_custom_call" | custom-call | tf_op jit(solution)/shard_map/ready/pallas_call | solution.py:326
  18.2 0.0 collective-permute-done.5
  18.3 3.2 %far.1 = bf16[1,128,4096]{2,1,0:T(8,128)(2,1)} custom-call(s32[1]{0:T(128)} %get-tuple-element.15.first_ref, bf16[1,128,4096]{2,1,0:T(8,128)(2,1)S(1)} %get-tuple-element.16.q_ref, f32[144,4096]{1,0:T(8,128)S(1)} %get-tuple-element.17.state_ref, f32[4,8,128]{2,1,0:T(8,128)S(1)} %get-tuple-element.18.fill_ref, f32[256,128]{1,0:T(8,128)S(1)} %get-tuple-element.19.down_ref, ...), custom_call_target="tpu_custom_call" | custom-call | tf_op jit(solution)/shard_map/far/pallas_call | solution.py:335
  (6 shorter events, 0.0 us)
Async XLA Ops:
  0.8 5.2 %collective-permute-start.2 = (bf16[40,512]{1,0:T(8,128)(2,1)S(1)}, bf16[40,512]{1,0:T(8,128)(2,1)S(1)}, u32[]{:S(2)}, u32[]{:S(2)}) collective-permute-start(bf16[40,512]{1,0:T(8,128)(2,1)S(1)} %get-tuple-element.21), channel_id=1, source_target_pairs={{0,1},{1,0},{2,3},{3,2},{4,5},{5,4},{6,7},{7,6},{8,9},{9,8},{10,11... | collective-permute-start | bytes 122888 | tf_op jit(solution)/shard_map/ppermute | solution.py:234
  1.4 6.9 %collective-permute-start = (bf16[40,512]{1,0:T(8,128)(2,1)S(1)}, bf16[40,512]{1,0:T(8,128)(2,1)S(1)}, u32[]{:S(2)}, u32[]{:S(2)}) collective-permute-start(bf16[40,512]{1,0:T(8,128)(2,1)S(1)} %get-tuple-element.21), channel_id=1, source_target_pairs={{0,12},{1,13},{2,14},{3,15},{4,8},{5,9},{6,10},{7,11},{8,4},{9,5},... | collective-permute-start | bytes 122888 | tf_op jit(solution)/shard_map/ppermute | solution.py:234
  6.0 8.0 %collective-permute-start.4 = (bf16[80,512]{1,0:T(8,128)(2,1)S(1)}, bf16[80,512]{1,0:T(8,128)(2,1)S(1)}, u32[]{:S(2)}, u32[]{:S(2)}) collective-permute-start(bf16[80,512]{1,0:T(8,128)(2,1)S(1)} %constant_dynamic-update-slice_fusion.4), channel_id=1, source_target_pairs={{0,4},{1,7},{2,6},{3,5},{4,0},{5,3},{6,2},{7,1},{8,12},{9,15},{10,... | collective-permute-start | bytes 245768 | tf_op jit(solution)/shard_map/ppermute | solution.py:234
  6.1 8.0 %collective-permute-start.3 = (bf16[80,512]{1,0:T(8,128)(2,1)S(1)}, bf16[80,512]{1,0:T(8,128)(2,1)S(1)}, u32[]{:S(2)}, u32[]{:S(2)}) collective-permute-start(bf16[80,512]{1,0:T(8,128)(2,1)S(1)} %constant_dynamic-update-slice_fusion.4), channel_id=1, source_target_pairs={{0,8},{1,11},{2,10},{3,9},{4,12},{5,15},{6,14},{7,13},{8,0},{9,3},... | collective-permute-start | bytes 245768 | tf_op jit(solution)/shard_map/ppermute | solution.py:234
  8.3 5.2 %collective-permute-start.1 = (bf16[80,512]{1,0:T(8,128)(2,1)S(1)}, bf16[80,512]{1,0:T(8,128)(2,1)S(1)}, u32[]{:S(2)}, u32[]{:S(2)}) collective-permute-start(bf16[80,512]{1,0:T(8,128)(2,1)S(1)} %pad_maximum_fusion), channel_id=1, source_target_pairs={{0,2},{1,3},{2,0},{3,1},{4,6},{5,7},{6,4},{7,5},{8,10},{9,11},{10,... | collective-permute-start | bytes 245768 | tf_op jit(solution)/shard_map/ppermute | solution.py:234
  14.1 4.2 %collective-permute-start.5 = (bf16[280,512]{1,0:T(8,128)(2,1)S(1)}, bf16[280,512]{1,0:T(8,128)(2,1)S(1)}, u32[]{:S(2)}, u32[]{:S(2)}) collective-permute-start(bf16[280,512]{1,0:T(8,128)(2,1)S(1)} %constant_dynamic-update-slice_fusion), channel_id=1, source_target_pairs={{0,1},{1,0},{2,3},{3,2},{4,5},{5,4},{6,7},{7,6},{8,9},{9,8},{10,11... | collective-permute-start | bytes 860168 | tf_op jit(solution)/shard_map/ppermute | solution.py:234

commit v5 on v4

--- a/solution.py
+++ b/solution.py
@@ -99,15 +99,22 @@
     return jnp.concatenate([high, (keys - high.astype(F32)).astype(BF16)], axis=1)
 
 
-def shard_keys(shards, seg_rows, prompt_rows, first, mask, fill, g):
+def shard_keys(shards, seg_rows, prompt_rows, choice_ref, mask, fill, g):
     def rows(start, size):
         parts = [r[:, pl.ds(start, size), g * HD : (g + 1) * HD].astype(F32).reshape(-1, HD) for r in shards]
         return jnp.concatenate(parts, axis=0)
 
+    def parent_rows(start):
+        found = rows(start, seg_rows)
+        for p in range(1, choice_ref.shape[0]):
+            chosen = choice_ref[p, 0:1, :] > 0
+            found = jnp.where(chosen, rows(start + p * 2 * seg_rows, seg_rows), found)
+        return found
+
     prompt = rows(shards[0].shape[1] - 2 * prompt_rows, 2 * prompt_rows)
-    keys = jnp.concatenate([rows(pl.multiple_of(first, 8), seg_rows), prompt], axis=0)
+    keys = jnp.concatenate([parent_rows(0), prompt], axis=0)
     shifted = pltpu.roll(prompt, prompt.shape[0] - prompt_rows, 0)
-    values = jnp.concatenate([rows(pl.multiple_of(first + seg_rows, 8), seg_rows), shifted], axis=0)
+    values = jnp.concatenate([parent_rows(seg_rows), shifted], axis=0)
     keys = split_keys(jnp.where(mask > 0, keys, fill))
     return keys, jnp.where(mask > 0, values, 0.0).astype(BF16)
 
@@ -142,9 +149,9 @@
         take(c, pl.ds(c * many * span, many * span), highest, weigh)
 
 
-def near_kernel(sizes, stride, *refs):
+def near_kernel(sizes, *refs):
     ins, refs = refs[:5], refs[5:]
-    q_ref, state_ref, fill_ref, down_ref, across_ref, first_ref, own_ref, own_kv_ref, *tables, sems = refs
+    q_ref, state_ref, fill_ref, down_ref, across_ref, choice_ref, own_ref, own_kv_ref, *tables, sems = refs
     fork_ref, owner_ref, lengths_ref = tables
     span = q_ref.shape[1]
     kv_heads = own_ref.shape[2] // HD
@@ -158,7 +165,9 @@
         copy.start()
     for copy in copies[:4]:
         copy.wait()
-    first_ref[0] = fork_ref[lax.axis_index("ctx")] * stride
+    parent = fork_ref[lax.axis_index("ctx")]
+    for p in range(choice_ref.shape[0]):
+        choice_ref[p] = jnp.full((8, HD), jnp.where(parent == p, 1.0, 0.0), F32)
     key = lax.broadcasted_iota(jnp.int32, (8, across_ref.shape[1]), 1)
     valid = valid_keys(key, *sizes, fork_ref, owner_ref, lengths_ref).astype(F32)
     across_ref[...] = jnp.concatenate([valid, valid], axis=0).astype(BF16)
@@ -182,25 +191,24 @@
     attend(q_ref, ready, causal, take, group, NEAR_HEADS)
 
 
-def ready_kernel(seg_rows, prompt_rows, first_ref, fill_ref, down_ref, *refs):
+def ready_kernel(seg_rows, prompt_rows, choice_ref, fill_ref, down_ref, *refs):
     *shards, keys_ref, values_ref = refs
     for g in range(fill_ref.shape[0]):
         mask = down_ref[: keys_ref.shape[1]]
-        made = shard_keys(shards, seg_rows, prompt_rows, first_ref[0], mask, fill_ref[g, 0:1], g)
+        made = shard_keys(shards, seg_rows, prompt_rows, choice_ref, mask, fill_ref[g, 0:1], g)
         keys_ref[g], values_ref[g] = made
 
 
-def far_kernel(seg_rows, prompt_rows, count, first_ref, q_ref, state_ref, fill_ref, down_ref, across_ref, *refs):
+def far_kernel(seg_rows, prompt_rows, count, choice_ref, q_ref, state_ref, fill_ref, down_ref, across_ref, *refs):
     shards, (*former_refs, out_ref, stage, sems) = refs[:count], refs[count:]
     span, columns = q_ref.shape[1:]
     kv_heads = fill_ref.shape[0]
     group = columns // HD // kv_heads
-    first = first_ref[0]
     copies = []
 
     def ready(g):
         known = former_refs[0].shape[1] if former_refs else 0
-        keys, values = shard_keys(shards, seg_rows, prompt_rows, first, down_ref[known:], fill_ref[g, 0:1], g)
+        keys, values = shard_keys(shards, seg_rows, prompt_rows, choice_ref, down_ref[known:], fill_ref[g, 0:1], g)
         if former_refs:
             keys = jnp.concatenate([former_refs[0][g], keys], axis=0)
             values = jnp.concatenate([former_refs[1][g], values], axis=0)
@@ -245,14 +253,14 @@
     both = lax.dynamic_update_slice(both, mate, (shard.shape[0], 0))
     pairs = pair_steps(n)
     wide = [permute(both, lambda i, j=j: i ^ (2 * (2 * j + i % 2)), n) for j in pairs]
-    passed = permute(jnp.concatenate([shard, first], axis=0), lambda i: i ^ near, n)
-    mine = jnp.concatenate([first, passed, *wide], axis=0)
+    side = permute(shard, lambda i: i ^ near, n)
+    passed = permute(first, lambda i: i ^ near, n)
+    mine = jnp.concatenate([first, *wide, side, passed], axis=0)
     theirs = permute(mine, lambda i: i ^ 1, n)
-    got = [[far, near, far ^ near], [far, near, far ^ near]]
-    for j in pairs:
-        for core in range(2):
-            d = 2 * (2 * j + core)
-            got[core] += [d, d ^ 1]
+    got = []
+    for core in range(2):
+        steps = [2 * (2 * j + core) for j in pairs]
+        got.append([far, *[o for d in steps for o in (d, d ^ 1)], near, far ^ near])
     offsets = [[0, 1, *got[core], *[o ^ 1 for o in got[1 - core]]] for core in range(2)]
     return [shard, mate, mine, theirs], offsets
 
@@ -300,18 +308,18 @@
     batches = [shards[:-1], shards[-1:]] if gather else [shards]
     counts = [sum(s.shape[0] for s in batch) for batch in batches]
     slots = seg_rows + 2 * prompt_rows
-    query, state, fill, down, across, first = pl.pallas_call(
-        functools.partial(near_kernel, (seg_rows, prompt_rows, counts, offsets), 2 * seg_rows if gather else 0),
+    query, state, fill, down, across, choice = pl.pallas_call(
+        functools.partial(near_kernel, (seg_rows, prompt_rows, counts, offsets)),
         out_shape=[
             jax.ShapeDtypeStruct(child_q.shape, BF16),
             jax.ShapeDtypeStruct((HD + 16, child_q.shape[2] // HD * span), F32),
             jax.ShapeDtypeStruct((kv_heads, 8, HD), F32),
             jax.ShapeDtypeStruct((n * slots, HD), F32),
             jax.ShapeDtypeStruct((16, n * slots), BF16),
-            jax.ShapeDtypeStruct((1,), jnp.int32),
+            jax.ShapeDtypeStruct((parents if gather else 1, 8, HD), F32),
         ],
         in_specs=[HBM] * 5,
-        out_specs=[VMEM] * 5 + [SMEM],
+        out_specs=[VMEM] * 6,
         scratch_shapes=[
             pltpu.VMEM(child_kv.shape[1:], BF16),
             pltpu.VMEM((2, span, width), BF16),
@@ -326,21 +334,21 @@
         former = pl.pallas_call(
             functools.partial(ready_kernel, seg_rows, prompt_rows),
             out_shape=[jax.ShapeDtypeStruct((kv_heads, counts[0] * slots, k * HD), BF16) for k in (2, 1)],
-            in_specs=[SMEM] + [VMEM] * (2 + len(batches[0])),
+            in_specs=[VMEM] * (3 + len(batches[0])),
             out_specs=[VMEM] * 2,
             compiler_params=limit(4),
             name="ready",
-        )(first, fill, down, *batches[0])
+        )(choice, fill, down, *batches[0])
     last = batches[-1]
     return pl.pallas_call(
         functools.partial(far_kernel, seg_rows, prompt_rows, len(last)),
         out_shape=jax.ShapeDtypeStruct(child_q.shape, BF16),
-        in_specs=[SMEM] + [VMEM] * (5 + len(last) + len(former)),
+        in_specs=[VMEM] * (6 + len(last) + len(former)),
         out_specs=HBM,
         scratch_shapes=[pltpu.VMEM(child_q.shape[1:], BF16), pltpu.SemaphoreType.DMA((kv_heads,))],
         compiler_params=limit(16 if gather else 48),
         name="far",
-    )(first, query, state, fill, down, across, *last, *former)
+    )(choice, query, state, fill, down, across, *last, *former)
 
 
 def solution(mesh):

time: 21.6 us -> 21.3 us (0.986)
  Pallas kernels: 8.06 us -> 6.71 us
  waiting for transfers between devices: 4.78 us -> 5.8 us
    ppermute x6 -> x7, waiting for transfers between devices: 4.78 us -> 5.8 us  [permute(): return lax.ppermute(x, 'ctx', [(i, target(i)) for i in range(n)])]
    pallas_call x1, Pallas kernels: 3.16 us -> 2.49 us  [body(): pl.pallas_call(functools.partial(far_kernel, seg_rows, prompt_rows, len(l...]
    pallas_call x1, Pallas kernels: 0.79 us -> 0.13 us  [body(): pl.pallas_call(functools.partial(ready_kernel, seg_rows, prompt_rows), ou...]
    ppermute x6 -> x7, starting transfers between devices: 8.48 us -> 8.55 us  [permute(): return lax.ppermute(x, 'ctx', [(i, target(i)) for i in range(n)])]
  transfers between devices with their start and end apart: 6 -> 7, of which waited for: 3 -> 4; matrix products, arithmetic and copies ran while one was open for 0% -> 0% of each run, Pallas kernels for 19% -> 16%
where the time goes in v5:
time: 21.3 us; the launch traced here: 21.1 us
  starting transfers between devices  8.55 us (40%)
  Pallas kernels  6.71 us (32%)
  waiting for transfers between devices  5.8 us (27%)
    ppermute x7, starting transfers between devices, permute(): return lax.ppermute(x, 'ctx', [(i, target(i)) for i in range(n)])  8.55 us
    ppermute x7, waiting for transfers between devices, permute(): return lax.ppermute(x, 'ctx', [(i, target(i)) for i in range(n)])  5.8 us
    pallas_call x1, Pallas kernels, body(): pl.pallas_call(functools.partial(near_kernel, (seg_rows, prompt_rows, cou...  3.28 us
    pallas_call x1, Pallas kernels, body(): pl.pallas_call(functools.partial(far_kernel, seg_rows, prompt_rows, len(l...  2.49 us
    pallas_call x1, Pallas kernels, body(): pl.pallas_call(shard_kernel, out_shape=[jax.ShapeDtypeStruct((k * rows, w...  0.81 us
  transfers between devices with their start and end apart: 7, of which 4 were waited for; matrix products, arithmetic and copies ran while one was open for 0% of the time, Pallas kernels for 16%

profile of v5, /device:TPU:0, one launch (start us, length us, event | category | flops | bytes accessed | tf_op | source)
XLA Modules:
  0.0 21.1 jit_solution(16819714824636069842)
XLA Ops:
  0.0 0.8 %shard.1 = (bf16[40,512]{1,0:T(8,128)(2,1)S(1)}, bf16[80,512]{1,0:T(8,128)(2,1)S(1)}) custom-call(bf16[4,2,512]{2,1,0:T(2,128)(2,1)} %prompt_hbm.1, bf16[8,2,2,512]{3,2,1,0:T(2,128)(2,1)} %parent_hbm.1), custom_call_target="tpu_custom_call" | custom-call | tf_op jit(solution)/shard_map/shard/pallas_call | solution.py:282
  0.8 0.6 %collective-permute-start.1 = (bf16[40,512]{1,0:T(8,128)(2,1)S(1)}, bf16[40,512]{1,0:T(8,128)(2,1)S(1)}, u32[]{:S(2)}, u32[]{:S(2)}) collective-permute-start(bf16[40,512]{1,0:T(8,128)(2,1)S(1)} %get-tuple-element.21), channel_id=1, source_target_pairs={{0,1},{1,0},{2,3},{3,2},{4,5},{5,4},{6,7},{7,6},{8,9},{9,8},{10,11... | collective-permute-start | bytes 122888 | tf_op jit(solution)/shard_map/ppermute | solution.py:242
  1.4 2.6 %collective-permute-start.4 = (bf16[40,512]{1,0:T(8,128)(2,1)S(1)}, bf16[40,512]{1,0:T(8,128)(2,1)S(1)}, u32[]{:S(2)}, u32[]{:S(2)}) collective-permute-start(bf16[40,512]{1,0:T(8,128)(2,1)S(1)} %get-tuple-element.21), channel_id=1, source_target_pairs={{0,2},{1,3},{2,0},{3,1},{4,6},{5,7},{6,4},{7,5},{8,10},{9,11},{10,... | collective-permute-start | bytes 122888 | tf_op jit(solution)/shard_map/ppermute | solution.py:242
  3.9 3.6 %collective-permute-start = (bf16[40,512]{1,0:T(8,128)(2,1)S(1)}, bf16[40,512]{1,0:T(8,128)(2,1)S(1)}, u32[]{:S(2)}, u32[]{:S(2)}) collective-permute-start(bf16[40,512]{1,0:T(8,128)(2,1)S(1)} %get-tuple-element.21), channel_id=1, source_target_pairs={{0,12},{1,13},{2,14},{3,15},{4,8},{5,9},{6,10},{7,11},{8,4},{9,5},... | collective-permute-start | bytes 122888 | tf_op jit(solution)/shard_map/ppermute | solution.py:242
  7.5 0.0 collective-permute-done.1
  7.5 0.0 collective-permute-start.3
  7.5 0.8 %collective-permute-start.2 = (bf16[80,512]{1,0:T(8,128)(2,1)S(1)}, bf16[80,512]{1,0:T(8,128)(2,1)S(1)}, u32[]{:S(2)}, u32[]{:S(2)}) collective-permute-start(bf16[80,512]{1,0:T(8,128)(2,1)S(1)} %constant_dynamic-update-slice_fusion.5), channel_id=1, source_target_pairs={{0,8},{1,11},{2,10},{3,9},{4,12},{5,15},{6,14},{7,13},{8,0},{9,3},... | collective-permute-start | bytes 245768 | tf_op jit(solution)/shard_map/ppermute | solution.py:242
  8.3 1.8 %collective-permute-done = bf16[40,512]{1,0:T(8,128)(2,1)S(1)} collective-permute-done((bf16[40,512]{1,0:T(8,128)(2,1)S(1)}, bf16[40,512]{1,0:T(8,128)(2,1)S(1)}, u32[]{:S(2)}, u32[]{:S(2)}) %collective-permute-start) | collective-permute-done | bytes 40992 | tf_op jit(solution)/shard_map/ppermute | solution.py:242
  10.2 0.0 collective-permute-start.5
  10.2 2.8 %collective-permute-done.2 = bf16[80,512]{1,0:T(8,128)(2,1)S(1)} collective-permute-done((bf16[80,512]{1,0:T(8,128)(2,1)S(1)}, bf16[80,512]{1,0:T(8,128)(2,1)S(1)}, u32[]{:S(2)}, u32[]{:S(2)}) %collective-permute-start.2) | collective-permute-done | bytes 81952 | tf_op jit(solution)/shard_map/ppermute | solution.py:242
  13.0 0.7 %collective-permute-done.3 = bf16[80,512]{1,0:T(8,128)(2,1)S(1)} collective-permute-done((bf16[80,512]{1,0:T(8,128)(2,1)S(1)}, bf16[80,512]{1,0:T(8,128)(2,1)S(1)}, u32[]{:S(2)}, u32[]{:S(2)}) %collective-permute-start.3) | collective-permute-done | bytes 81952 | tf_op jit(solution)/shard_map/ppermute | solution.py:242
  13.7 0.0 collective-permute-done.4
  13.7 0.4 %collective-permute-done.5 = bf16[40,512]{1,0:T(8,128)(2,1)S(1)} collective-permute-done((bf16[40,512]{1,0:T(8,128)(2,1)S(1)}, bf16[40,512]{1,0:T(8,128)(2,1)S(1)}, u32[]{:S(2)}, u32[]{:S(2)}) %collective-permute-start.5) | collective-permute-done | bytes 40992 | tf_op jit(solution)/shard_map/ppermute | solution.py:242
  14.2 1.1 %collective-permute-start.6 = (bf16[280,512]{1,0:T(8,128)(2,1)S(1)}, bf16[280,512]{1,0:T(8,128)(2,1)S(1)}, u32[]{:S(2)}, u32[]{:S(2)}) collective-permute-start(bf16[280,512]{1,0:T(8,128)(2,1)S(1)} %constant_dynamic-update-slice_fusion), channel_id=1, source_target_pairs={{0,1},{1,0},{2,3},{3,2},{4,5},{5,4},{6,7},{7,6},{8,9},{9,8},{10,11... | collective-permute-start | bytes 860168 | tf_op jit(solution)/shard_map/ppermute | solution.py:242
  15.2 3.3 %near.1 = (bf16[1,128,4096]{2,1,0:T(8,128)(2,1)S(1)}, f32[144,4096]{1,0:T(8,128)S(1)}, f32[4,8,128]{2,1,0:T(8,128)S(1)}, f32[256,128]{1,0:T(8,128)S(1)}, bf16[16...) custom-call(bf16[1,128,4096]{2,1,0:T(8,128)(2,1)} %refs_0_.1, bf16[128,2,512]{2,1,0:T(2,128)(2,1)} %bitcast.9, s32[16]{0:T(128)} %refs_2_.1, ...), custom_call_target="tpu_custom_call" | custom-call | tf_op jit(solution)/shard_map/near/pallas_call | solution.py:311
  18.5 0.1 ready.1
  18.6 0.0 collective-permute-done.6
  18.7 2.5 %far.1 = bf16[1,128,4096]{2,1,0:T(8,128)(2,1)} custom-call(f32[2,8,128]{2,1,0:T(8,128)S(1)} %get-tuple-element.15.choice_ref, bf16[1,128,4096]{2,1,0:T(8,128)(2,1)S(1)} %get-tuple-element.16.q_ref, f32[144,4096]{1,0:T(8,128)S(1)} %get-tuple-element.17.state_ref, f32[4,8,128]{2,1,0:T(8,128)S(1)} %get-tuple-element.18.fill_ref, ...), custom_call_target="tpu_custom_call" | custom-call | tf_op jit(solution)/shard_map/far/pallas_call | solution.py:343
  (6 shorter events, 0.0 us)
Async XLA Ops:
  0.8 6.7 %collective-permute-start.1 = (bf16[40,512]{1,0:T(8,128)(2,1)S(1)}, bf16[40,512]{1,0:T(8,128)(2,1)S(1)}, u32[]{:S(2)}, u32[]{:S(2)}) collective-permute-start(bf16[40,512]{1,0:T(8,128)(2,1)S(1)} %get-tuple-element.21), channel_id=1, source_target_pairs={{0,1},{1,0},{2,3},{3,2},{4,5},{5,4},{6,7},{7,6},{8,9},{9,8},{10,11... | collective-permute-start | bytes 122888 | tf_op jit(solution)/shard_map/ppermute | solution.py:242
  1.4 12.3 %collective-permute-start.4 = (bf16[40,512]{1,0:T(8,128)(2,1)S(1)}, bf16[40,512]{1,0:T(8,128)(2,1)S(1)}, u32[]{:S(2)}, u32[]{:S(2)}) collective-permute-start(bf16[40,512]{1,0:T(8,128)(2,1)S(1)} %get-tuple-element.21), channel_id=1, source_target_pairs={{0,2},{1,3},{2,0},{3,1},{4,6},{5,7},{6,4},{7,5},{8,10},{9,11},{10,... | collective-permute-start | bytes 122888 | tf_op jit(solution)/shard_map/ppermute | solution.py:242
  3.9 6.2 %collective-permute-start = (bf16[40,512]{1,0:T(8,128)(2,1)S(1)}, bf16[40,512]{1,0:T(8,128)(2,1)S(1)}, u32[]{:S(2)}, u32[]{:S(2)}) collective-permute-start(bf16[40,512]{1,0:T(8,128)(2,1)S(1)} %get-tuple-element.21), channel_id=1, source_target_pairs={{0,12},{1,13},{2,14},{3,15},{4,8},{5,9},{6,10},{7,11},{8,4},{9,5},... | collective-permute-start | bytes 122888 | tf_op jit(solution)/shard_map/ppermute | solution.py:242
  7.5 6.2 %collective-permute-start.3 = (bf16[80,512]{1,0:T(8,128)(2,1)S(1)}, bf16[80,512]{1,0:T(8,128)(2,1)S(1)}, u32[]{:S(2)}, u32[]{:S(2)}) collective-permute-start(bf16[80,512]{1,0:T(8,128)(2,1)S(1)} %constant_dynamic-update-slice_fusion.5), channel_id=1, source_target_pairs={{0,4},{1,7},{2,6},{3,5},{4,0},{5,3},{6,2},{7,1},{8,12},{9,15},{10,... | collective-permute-start | bytes 245768 | tf_op jit(solution)/shard_map/ppermute | solution.py:242
  7.5 5.4 %collective-permute-start.2 = (bf16[80,512]{1,0:T(8,128)(2,1)S(1)}, bf16[80,512]{1,0:T(8,128)(2,1)S(1)}, u32[]{:S(2)}, u32[]{:S(2)}) collective-permute-start(bf16[80,512]{1,0:T(8,128)(2,1)S(1)} %constant_dynamic-update-slice_fusion.5), channel_id=1, source_target_pairs={{0,8},{1,11},{2,10},{3,9},{4,12},{5,15},{6,14},{7,13},{8,0},{9,3},... | collective-permute-start | bytes 245768 | tf_op jit(solution)/shard_map/ppermute | solution.py:242
  10.2 4.0 %collective-permute-start.5 = (bf16[40,512]{1,0:T(8,128)(2,1)S(1)}, bf16[40,512]{1,0:T(8,128)(2,1)S(1)}, u32[]{:S(2)}, u32[]{:S(2)}) collective-permute-start(bf16[40,512]{1,0:T(8,128)(2,1)S(1)} %collective-permute-done), channel_id=1, source_target_pairs={{0,2},{1,3},{2,0},{3,1},{4,6},{5,7},{6,4},{7,5},{8,10},{9,11},{10,... | collective-permute-start | bytes 122888 | tf_op jit(solution)/shard_map/ppermute | solution.py:242
  14.2 4.5 %collective-permute-start.6 = (bf16[280,512]{1,0:T(8,128)(2,1)S(1)}, bf16[280,512]{1,0:T(8,128)(2,1)S(1)}, u32[]{:S(2)}, u32[]{:S(2)}) collective-permute-start(bf16[280,512]{1,0:T(8,128)(2,1)S(1)} %constant_dynamic-update-slice_fusion), channel_id=1, source_target_pairs={{0,1},{1,0},{2,3},{3,2},{4,5},{5,4},{6,7},{7,6},{8,9},{9,8},{10,11... | collective-permute-start | bytes 860168 | tf_op jit(solution)/shard_map/ppermute | solution.py:242

commit v6 on v5

--- a/solution.py
+++ b/solution.py
@@ -11,7 +11,7 @@
 LOG2E = 1.4426950408889634
 F32 = jnp.float32
 BF16 = jnp.bfloat16
-NEAR_HEADS, FAR_HEADS = 4, 8
+NEAR_HEADS, FAR_HEADS, OUT_HEADS, LOADS = 8, 8, 8, 4
 VMEM = pl.BlockSpec(memory_space=pltpu.VMEM)
 SMEM = pl.BlockSpec(memory_space=pltpu.SMEM)
 HBM = pl.BlockSpec(memory_space=pltpu.HBM)
@@ -149,21 +149,17 @@
         take(c, pl.ds(c * many * span, many * span), highest, weigh)
 
 
-def near_kernel(sizes, *refs):
-    ins, refs = refs[:5], refs[5:]
-    q_ref, state_ref, fill_ref, down_ref, across_ref, choice_ref, own_ref, own_kv_ref, *tables, sems = refs
+def load_kernel(sizes, *refs):
+    ins, (q_ref, own_ref, down_ref, across_ref, choice_ref, raw_ref, *tables, sems) = refs[:5], refs[5:]
     fork_ref, owner_ref, lengths_ref = tables
-    span = q_ref.shape[1]
-    kv_heads = own_ref.shape[2] // HD
-    group = q_ref.shape[2] // HD // kv_heads
-    pairs = list(zip(ins[1:], (own_ref, *tables), strict=True))
-    for g in range(kv_heads):
-        part = pl.ds(g * group * HD, group * HD)
-        pairs.append((ins[0].at[:, :, part], q_ref.at[:, :, part]))
+    pairs = list(zip(ins, (*tables, raw_ref), strict=False))
+    rows = q_ref.shape[1] // LOADS
+    for k in range(LOADS):
+        pairs.append((ins[4].at[:, pl.ds(k * rows, rows)], q_ref.at[:, pl.ds(k * rows, rows)]))
     copies = [pltpu.make_async_copy(src, dst, sems.at[k]) for k, (src, dst) in enumerate(pairs)]
     for copy in copies:
         copy.start()
-    for copy in copies[:4]:
+    for copy in copies[:3]:
         copy.wait()
     parent = fork_ref[lax.axis_index("ctx")]
     for p in range(choice_ref.shape[0]):
@@ -172,17 +168,25 @@
     valid = valid_keys(key, *sizes, fork_ref, owner_ref, lengths_ref).astype(F32)
     across_ref[...] = jnp.concatenate([valid, valid], axis=0).astype(BF16)
     down_ref[...] = jnp.concatenate([valid] * (HD // 8), axis=0).T
-    own_kv_ref[...] = jnp.swapaxes(own_ref[...], 0, 1)
+    copies[3].wait()
+    own_ref[...] = jnp.swapaxes(raw_ref[...], 0, 1)
+    for copy in copies[4:]:
+        copy.wait()
+
+
+def near_kernel(q_ref, own_ref, state_ref, fill_ref):
+    span = q_ref.shape[1]
+    kv_heads = own_ref.shape[2] // HD
+    group = q_ref.shape[2] // HD // kv_heads
     time = lax.broadcasted_iota(jnp.int32, (span, NEAR_HEADS * span), 1) % span
     causal = jnp.where(lax.broadcasted_iota(jnp.int32, time.shape, 0) <= time, 0.0, -jnp.inf)
     ones = jnp.ones((16, span), BF16)
 
     def ready(g):
-        copies[4 + g].wait()
         part = slice(g * HD, (g + 1) * HD)
-        keys = own_kv_ref[0, :, part].astype(F32)
+        keys = own_ref[0, :, part].astype(F32)
         fill_ref[g] = jnp.broadcast_to(keys[0:1], (8, HD))
-        return split_keys(keys), jnp.concatenate([own_kv_ref[1, :, part].T, ones], axis=0)
+        return split_keys(keys), jnp.concatenate([own_ref[1, :, part].T, ones], axis=0)
 
     def take(c, lanes, highest, weigh):
         state_ref[: HD + 8, lanes] = weigh(highest)[: HD + 8]
@@ -191,10 +195,10 @@
     attend(q_ref, ready, causal, take, group, NEAR_HEADS)
 
 
-def ready_kernel(seg_rows, prompt_rows, choice_ref, fill_ref, down_ref, *refs):
+def ready_kernel(seg_rows, prompt_rows, start, choice_ref, fill_ref, down_ref, *refs):
     *shards, keys_ref, values_ref = refs
     for g in range(fill_ref.shape[0]):
-        mask = down_ref[: keys_ref.shape[1]]
+        mask = down_ref[start : start + keys_ref.shape[1]]
         made = shard_keys(shards, seg_rows, prompt_rows, choice_ref, mask, fill_ref[g, 0:1], g)
         keys_ref[g], values_ref[g] = made
 
@@ -207,11 +211,11 @@
     copies = []
 
     def ready(g):
-        known = former_refs[0].shape[1] if former_refs else 0
+        known = sum(r.shape[1] for r in former_refs[::2])
         keys, values = shard_keys(shards, seg_rows, prompt_rows, choice_ref, down_ref[known:], fill_ref[g, 0:1], g)
         if former_refs:
-            keys = jnp.concatenate([former_refs[0][g], keys], axis=0)
-            values = jnp.concatenate([former_refs[1][g], values], axis=0)
+            keys = jnp.concatenate([*[r[g] for r in former_refs[::2]], keys], axis=0)
+            values = jnp.concatenate([*[r[g] for r in former_refs[1::2]], values], axis=0)
         return keys, jnp.concatenate([values.T, across_ref[...]], axis=0)
 
     def take(c, lanes, highest, weigh):
@@ -227,11 +231,10 @@
         for k in range(FAR_HEADS):
             i = c * FAR_HEADS + k
             stage[:, i * HD : (i + 1) * HD] = result[:, k * span : (k + 1) * span].T
-        if (c + 1) * FAR_HEADS % group == 0:
-            g = c * FAR_HEADS // group
-            part = pl.ds(g * group * HD, group * HD)
-            copies.append(pltpu.make_async_copy(stage.at[:, part], out_ref.at[0, :, part], sems.at[g]))
-            copies[-1].start()
+            if (i + 1) % OUT_HEADS == 0:
+                part = pl.ds((i + 1 - OUT_HEADS) * HD, OUT_HEADS * HD)
+                copies.append(pltpu.make_async_copy(stage.at[:, part], out_ref.at[0, :, part], sems.at[len(copies)]))
+                copies[-1].start()
 
     attend(q_ref, ready, None, take, group, FAR_HEADS)
     for copy in copies:
@@ -255,14 +258,19 @@
     wide = [permute(both, lambda i, j=j: i ^ (2 * (2 * j + i % 2)), n) for j in pairs]
     side = permute(shard, lambda i: i ^ near, n)
     passed = permute(first, lambda i: i ^ near, n)
-    mine = jnp.concatenate([first, *wide, side, passed], axis=0)
-    theirs = permute(mine, lambda i: i ^ 1, n)
+    soon = jnp.concatenate([first, side, *wide[1:]], axis=0)
+    late = jnp.concatenate([*wide[:1], passed], axis=0)
+    soon_theirs = permute(soon, lambda i: i ^ 1, n)
+    late_theirs = permute(late, lambda i: i ^ 1, n)
     got = []
     for core in range(2):
-        steps = [2 * (2 * j + core) for j in pairs]
-        got.append([far, *[o for d in steps for o in (d, d ^ 1)], near, far ^ near])
-    offsets = [[0, 1, *got[core], *[o ^ 1 for o in got[1 - core]]] for core in range(2)]
-    return [shard, mate, mine, theirs], offsets
+        steps = [[2 * (2 * j + core), 2 * (2 * j + core) ^ 1] for j in pairs]
+        got.append(([far, near, *[o for step in steps[1:] for o in step]], [*steps[0], far ^ near]))
+    offsets = []
+    for core in range(2):
+        theirs = [[o ^ 1 for o in part] for part in got[1 - core]]
+        offsets.append([0, 1, *got[core][0], *theirs[0], *got[core][1], *theirs[1]])
+    return [[shard, mate, soon], [soon_theirs, late], [late_theirs]], offsets
 
 
 def use_gather(mesh_size, parents, seg_rows, prompt_rows):
@@ -292,7 +300,7 @@
             compiler_params=limit(2),
             name="shard",
         )(*in_hbm(prompt_kv, parent_kv))
-        shards, offsets = gather_shards(shard, both, n)
+        batches, offsets = gather_shards(shard, both, n)
     else:
         rows = 2 * (seg_rows + prompt_rows)
         send = pl.pallas_call(
@@ -303,49 +311,56 @@
             scratch_shapes=[pltpu.VMEM((parents, rows, width), BF16)],
             name="pack",
         )(fork_list, prompt_kv, parent_kv)
-        shards, offsets = [lax.all_to_all(send, "ctx", split_axis=0, concat_axis=0, tiled=True)], None
-    shards = [s.reshape(-1, rows, width) for s in shards]
-    batches = [shards[:-1], shards[-1:]] if gather else [shards]
+        batches, offsets = [[lax.all_to_all(send, "ctx", split_axis=0, concat_axis=0, tiled=True)]], None
+    batches = [[s.reshape(-1, rows, width) for s in batch] for batch in batches]
     counts = [sum(s.shape[0] for s in batch) for batch in batches]
     slots = seg_rows + 2 * prompt_rows
-    query, state, fill, down, across, choice = pl.pallas_call(
-        functools.partial(near_kernel, (seg_rows, prompt_rows, counts, offsets)),
+    query, own, down, across, choice = pl.pallas_call(
+        functools.partial(load_kernel, (seg_rows, prompt_rows, counts, offsets)),
         out_shape=[
             jax.ShapeDtypeStruct(child_q.shape, BF16),
-            jax.ShapeDtypeStruct((HD + 16, child_q.shape[2] // HD * span), F32),
-            jax.ShapeDtypeStruct((kv_heads, 8, HD), F32),
+            jax.ShapeDtypeStruct((2, span, width), BF16),
             jax.ShapeDtypeStruct((n * slots, HD), F32),
             jax.ShapeDtypeStruct((16, n * slots), BF16),
             jax.ShapeDtypeStruct((parents if gather else 1, 8, HD), F32),
         ],
         in_specs=[HBM] * 5,
-        out_specs=[VMEM] * 6,
+        out_specs=[VMEM] * 5,
         scratch_shapes=[
             pltpu.VMEM(child_kv.shape[1:], BF16),
-            pltpu.VMEM((2, span, width), BF16),
             *[pltpu.SMEM(x.shape, jnp.int32) for x in (fork_list, owner_map, lengths)],
-            pltpu.SemaphoreType.DMA((4 + kv_heads,)),
+            pltpu.SemaphoreType.DMA((4 + LOADS,)),
         ],
+        compiler_params=limit(8),
+        name="load",
+    )(*in_hbm(fork_list, owner_map, lengths, child_kv[0], child_q))
+    state, fill = pl.pallas_call(
+        near_kernel,
+        out_shape=[
+            jax.ShapeDtypeStruct((HD + 16, child_q.shape[2] // HD * span), F32),
+            jax.ShapeDtypeStruct((kv_heads, 8, HD), F32),
+        ],
+        in_specs=[VMEM] * 2,
+        out_specs=[VMEM] * 2,
         compiler_params=limit(16),
         name="near",
-    )(*in_hbm(child_q, child_kv[0], fork_list, owner_map, lengths))
+    )(query, own)
     former = []
-    if gather:
-        former = pl.pallas_call(
-            functools.partial(ready_kernel, seg_rows, prompt_rows),
-            out_shape=[jax.ShapeDtypeStruct((kv_heads, counts[0] * slots, k * HD), BF16) for k in (2, 1)],
-            in_specs=[VMEM] * (3 + len(batches[0])),
+    for k, (batch, count) in enumerate(zip(batches[:-1], counts)):
+        former += pl.pallas_call(
+            functools.partial(ready_kernel, seg_rows, prompt_rows, sum(counts[:k]) * slots),
+            out_shape=[jax.ShapeDtypeStruct((kv_heads, count * slots, k * HD), BF16) for k in (2, 1)],
+            in_specs=[VMEM] * (3 + len(batch)),
             out_specs=[VMEM] * 2,
             compiler_params=limit(4),
-            name="ready",
-        )(choice, fill, down, *batches[0])
+        )(choice, fill, down, *batch)
     last = batches[-1]
     return pl.pallas_call(
         functools.partial(far_kernel, seg_rows, prompt_rows, len(last)),
         out_shape=jax.ShapeDtypeStruct(child_q.shape, BF16),
         in_specs=[VMEM] * (6 + len(last) + len(former)),
         out_specs=HBM,
-        scratch_shapes=[pltpu.VMEM(child_q.shape[1:], BF16), pltpu.SemaphoreType.DMA((kv_heads,))],
+        scratch_shapes=[pltpu.VMEM(child_q.shape[1:], BF16), pltpu.SemaphoreType.DMA((child_q.shape[2] // HD // OUT_HEADS,))],
         compiler_params=limit(16 if gather else 48),
         name="far",
     )(choice, query, state, fill, down, across, *last, *former)

time: 21.3 us -> 20.8 us (0.977)
  Pallas kernels: 6.71 us -> 6.16 us
    pallas_call x2 -> x4, Pallas kernels: 3.41 us -> 2.82 us  [the longest x1 1.34 us: body(): pl.pallas_call(functools.partial(load_kernel, (seg_rows, prompt_rows, cou...]
    ppermute x7 -> x8, starting transfers between devices: 8.55 us -> 8.5 us  [permute(): return lax.ppermute(x, 'ctx', [(i, target(i)) for i in range(n)])]
    ppermute x7 -> x8, waiting for transfers between devices: 5.8 us -> 5.78 us  [permute(): return lax.ppermute(x, 'ctx', [(i, target(i)) for i in range(n)])]
  transfers between devices with their start and end apart: 7 -> 8, of which waited for: 4 -> 3; matrix products, arithmetic and copies ran while one was open for 0% -> 0% of each run, Pallas kernels for 16% -> 14%
where the time goes in v6:
time: 20.8 us; the launch traced here: 20.6 us
  starting transfers between devices  8.5 us (41%)
  Pallas kernels  6.16 us (30%)
  waiting for transfers between devices  5.78 us (28%)
    ppermute x8, starting transfers between devices, permute(): return lax.ppermute(x, 'ctx', [(i, target(i)) for i in range(n)])  8.5 us
    ppermute x8, waiting for transfers between devices, permute(): return lax.ppermute(x, 'ctx', [(i, target(i)) for i in range(n)])  5.78 us
    pallas_call x1, Pallas kernels, body(): pl.pallas_call(functools.partial(far_kernel, seg_rows, prompt_rows, len(l...  2.54 us
    pallas_call x1, Pallas kernels, body(): pl.pallas_call(functools.partial(load_kernel, (seg_rows, prompt_rows, cou...  1.34 us
    pallas_call x1, Pallas kernels, body(): pl.pallas_call(near_kernel, out_shape=[jax.ShapeDtypeStruct((HD + 16, chi...  1.3 us
    pallas_call x1, Pallas kernels, body(): pl.pallas_call(shard_kernel, out_shape=[jax.ShapeDtypeStruct((k * rows, w...  0.81 us
  transfers between devices with their start and end apart: 8, of which 3 were waited for; matrix products, arithmetic and copies ran while one was open for 0% of the time, Pallas kernels for 14%

profile of v6, /device:TPU:0, one launch (start us, length us, event | category | flops | bytes accessed | tf_op | source)
XLA Modules:
  0.0 20.6 jit_solution(11208973115734540973)
XLA Ops:
  0.0 0.8 %shard.1 = (bf16[40,512]{1,0:T(8,128)(2,1)S(1)}, bf16[80,512]{1,0:T(8,128)(2,1)S(1)}) custom-call(bf16[4,2,512]{2,1,0:T(2,128)(2,1)} %prompt_hbm.1, bf16[8,2,2,512]{3,2,1,0:T(2,128)(2,1)} %parent_hbm.1), custom_call_target="tpu_custom_call" | custom-call | tf_op jit(solution)/shard_map/shard/pallas_call | solution.py:290
  0.8 0.6 %collective-permute-start = (bf16[40,512]{1,0:T(8,128)(2,1)S(1)}, bf16[40,512]{1,0:T(8,128)(2,1)S(1)}, u32[]{:S(2)}, u32[]{:S(2)}) collective-permute-start(bf16[40,512]{1,0:T(8,128)(2,1)S(1)} %get-tuple-element.26), channel_id=1, source_target_pairs={{0,1},{1,0},{2,3},{3,2},{4,5},{5,4},{6,7},{7,6},{8,9},{9,8},{10,11... | collective-permute-start | bytes 122888 | tf_op jit(solution)/shard_map/ppermute | solution.py:245
  1.4 2.6 %collective-permute-start.5 = (bf16[40,512]{1,0:T(8,128)(2,1)S(1)}, bf16[40,512]{1,0:T(8,128)(2,1)S(1)}, u32[]{:S(2)}, u32[]{:S(2)}) collective-permute-start(bf16[40,512]{1,0:T(8,128)(2,1)S(1)} %get-tuple-element.26), channel_id=1, source_target_pairs={{0,2},{1,3},{2,0},{3,1},{4,6},{5,7},{6,4},{7,5},{8,10},{9,11},{10,... | collective-permute-start | bytes 122888 | tf_op jit(solution)/shard_map/ppermute | solution.py:245
  3.9 3.6 %collective-permute-start.2 = (bf16[40,512]{1,0:T(8,128)(2,1)S(1)}, bf16[40,512]{1,0:T(8,128)(2,1)S(1)}, u32[]{:S(2)}, u32[]{:S(2)}) collective-permute-start(bf16[40,512]{1,0:T(8,128)(2,1)S(1)} %get-tuple-element.26), channel_id=1, source_target_pairs={{0,12},{1,13},{2,14},{3,15},{4,8},{5,9},{6,10},{7,11},{8,4},{9,5},... | collective-permute-start | bytes 122888 | tf_op jit(solution)/shard_map/ppermute | solution.py:245
  7.5 0.0 collective-permute-done
  7.5 0.0 collective-permute-start.6
  7.5 0.8 %collective-permute-start.1 = (bf16[80,512]{1,0:T(8,128)(2,1)S(1)}, bf16[80,512]{1,0:T(8,128)(2,1)S(1)}, u32[]{:S(2)}, u32[]{:S(2)}) collective-permute-start(bf16[80,512]{1,0:T(8,128)(2,1)S(1)} %constant_dynamic-update-slice_fusion.5), channel_id=1, source_target_pairs={{0,8},{1,11},{2,10},{3,9},{4,12},{5,15},{6,14},{7,13},{8,0},{9,3},... | collective-permute-start | bytes 245768 | tf_op jit(solution)/shard_map/ppermute | solution.py:245
  8.3 1.8 %collective-permute-done.2 = bf16[40,512]{1,0:T(8,128)(2,1)S(1)} collective-permute-done((bf16[40,512]{1,0:T(8,128)(2,1)S(1)}, bf16[40,512]{1,0:T(8,128)(2,1)S(1)}, u32[]{:S(2)}, u32[]{:S(2)}) %collective-permute-start.2) | collective-permute-done | bytes 40992 | tf_op jit(solution)/shard_map/ppermute | solution.py:245
  10.2 0.0 collective-permute-start.3
  10.2 0.0 collective-permute-done.5
  10.2 3.5 %collective-permute-done.6 = bf16[80,512]{1,0:T(8,128)(2,1)S(1)} collective-permute-done((bf16[80,512]{1,0:T(8,128)(2,1)S(1)}, bf16[80,512]{1,0:T(8,128)(2,1)S(1)}, u32[]{:S(2)}, u32[]{:S(2)}) %collective-permute-start.6) | collective-permute-done | bytes 81952 | tf_op jit(solution)/shard_map/ppermute | solution.py:245
  13.7 0.0 collective-permute-start.7
  13.7 0.0 collective-permute-done.1
  13.7 0.4 %collective-permute-done.3 = bf16[40,512]{1,0:T(8,128)(2,1)S(1)} collective-permute-done((bf16[40,512]{1,0:T(8,128)(2,1)S(1)}, bf16[40,512]{1,0:T(8,128)(2,1)S(1)}, u32[]{:S(2)}, u32[]{:S(2)}) %collective-permute-start.3) | collective-permute-done | bytes 40992 | tf_op jit(solution)/shard_map/ppermute | solution.py:245
  14.2 1.0 %collective-permute-start.4 = (bf16[120,512]{1,0:T(8,128)(2,1)S(1)}, bf16[120,512]{1,0:T(8,128)(2,1)S(1)}, u32[]{:S(2)}, u32[]{:S(2)}) collective-permute-start(bf16[120,512]{1,0:T(8,128)(2,1)S(1)} %constant_dynamic-update-slice_fusion), channel_id=1, source_target_pairs={{0,1},{1,0},{2,3},{3,2},{4,5},{5,4},{6,7},{7,6},{8,9},{9,8},{10,11... | collective-permute-start | bytes 368648 | tf_op jit(solution)/shard_map/ppermute | solution.py:245
  15.2 1.3 %load.1 = (bf16[1,128,4096]{2,1,0:T(8,128)(2,1)S(1)}, bf16[2,128,512]{2,1,0:T(8,128)(2,1)S(1)}, f32[256,128]{1,0:T(8,128)S(1)}, bf16[16,256]{1,0:T(8,128)(2,1)S(1)}, f32[2,8,128]{2,1,0:T(8,128)S(1)}) custom-call(s32[16]{0:T(128)} %refs_0_.1, s32[2,16]{1,0:T(2,128)} %refs_1_.1, s32[2]{0:T(128)} %refs_2_.1, bf16[128,2,512]{2,1,0:T(2,128)(2,1)} %bitcast.13, ...), custom_call_target="tpu_custom_call" | custom-call | tf_op jit(solution)/shard_map/load/pallas_call | solution.py:318
  16.5 1.3 %near.1 = (f32[144,4096]{1,0:T(8,128)S(1)}, f32[4,8,128]{2,1,0:T(8,128)S(1)}) custom-call(bf16[1,128,4096]{2,1,0:T(8,128)(2,1)S(1)} %get-tuple-element.19.q_ref, bf16[2,128,512]{2,1,0:T(8,128)(2,1)S(1)} %get-tuple-element.20.own_ref), custom_call_target="tpu_custom_call" | custom-call | tf_op jit(solution)/shard_map/near/pallas_call | solution.py:337
  17.8 0.1 shard_map.73
  17.9 0.0 collective-permute-done.7
  17.9 0.1 shard_map.74
  18.0 0.0 collective-permute-done.4
  18.0 2.5 %far.1 = bf16[1,128,4096]{2,1,0:T(8,128)(2,1)} custom-call(f32[2,8,128]{2,1,0:T(8,128)S(1)} %get-tuple-element.18.choice_ref, bf16[1,128,4096]{2,1,0:T(8,128)(2,1)S(1)} %get-tuple-element.19.q_ref, f32[144,4096]{1,0:T(8,128)S(1)} %get-tuple-element.21.state_ref, f32[4,8,128]{2,1,0:T(8,128)S(1)} %get-tuple-element.22.fill_ref, ...), custom_call_target="tpu_custom_call" | custom-call | tf_op jit(solution)/shard_map/far/pallas_call | solution.py:358
  (6 shorter events, 0.0 us)
Async XLA Ops:
  0.8 6.7 %collective-permute-start = (bf16[40,512]{1,0:T(8,128)(2,1)S(1)}, bf16[40,512]{1,0:T(8,128)(2,1)S(1)}, u32[]{:S(2)}, u32[]{:S(2)}) collective-permute-start(bf16[40,512]{1,0:T(8,128)(2,1)S(1)} %get-tuple-element.26), channel_id=1, source_target_pairs={{0,1},{1,0},{2,3},{3,2},{4,5},{5,4},{6,7},{7,6},{8,9},{9,8},{10,11... | collective-permute-start | bytes 122888 | tf_op jit(solution)/shard_map/ppermute | solution.py:245
  1.4 8.8 %collective-permute-start.5 = (bf16[40,512]{1,0:T(8,128)(2,1)S(1)}, bf16[40,512]{1,0:T(8,128)(2,1)S(1)}, u32[]{:S(2)}, u32[]{:S(2)}) collective-permute-start(bf16[40,512]{1,0:T(8,128)(2,1)S(1)} %get-tuple-element.26), channel_id=1, source_target_pairs={{0,2},{1,3},{2,0},{3,1},{4,6},{5,7},{6,4},{7,5},{8,10},{9,11},{10,... | collective-permute-start | bytes 122888 | tf_op jit(solution)/shard_map/ppermute | solution.py:245
  3.9 6.2 %collective-permute-start.2 = (bf16[40,512]{1,0:T(8,128)(2,1)S(1)}, bf16[40,512]{1,0:T(8,128)(2,1)S(1)}, u32[]{:S(2)}, u32[]{:S(2)}) collective-permute-start(bf16[40,512]{1,0:T(8,128)(2,1)S(1)} %get-tuple-element.26), channel_id=1, source_target_pairs={{0,12},{1,13},{2,14},{3,15},{4,8},{5,9},{6,10},{7,11},{8,4},{9,5},... | collective-permute-start | bytes 122888 | tf_op jit(solution)/shard_map/ppermute | solution.py:245
  7.5 6.2 %collective-permute-start.6 = (bf16[80,512]{1,0:T(8,128)(2,1)S(1)}, bf16[80,512]{1,0:T(8,128)(2,1)S(1)}, u32[]{:S(2)}, u32[]{:S(2)}) collective-permute-start(bf16[80,512]{1,0:T(8,128)(2,1)S(1)} %constant_dynamic-update-slice_fusion.5), channel_id=1, source_target_pairs={{0,4},{1,7},{2,6},{3,5},{4,0},{5,3},{6,2},{7,1},{8,12},{9,15},{10,... | collective-permute-start | bytes 245768 | tf_op jit(solution)/shard_map/ppermute | solution.py:245
  7.5 6.2 %collective-permute-start.1 = (bf16[80,512]{1,0:T(8,128)(2,1)S(1)}, bf16[80,512]{1,0:T(8,128)(2,1)S(1)}, u32[]{:S(2)}, u32[]{:S(2)}) collective-permute-start(bf16[80,512]{1,0:T(8,128)(2,1)S(1)} %constant_dynamic-update-slice_fusion.5), channel_id=1, source_target_pairs={{0,8},{1,11},{2,10},{3,9},{4,12},{5,15},{6,14},{7,13},{8,0},{9,3},... | collective-permute-start | bytes 245768 | tf_op jit(solution)/shard_map/ppermute | solution.py:245
  10.2 4.0 %collective-permute-start.3 = (bf16[40,512]{1,0:T(8,128)(2,1)S(1)}, bf16[40,512]{1,0:T(8,128)(2,1)S(1)}, u32[]{:S(2)}, u32[]{:S(2)}) collective-permute-start(bf16[40,512]{1,0:T(8,128)(2,1)S(1)} %collective-permute-done.2), channel_id=1, source_target_pairs={{0,2},{1,3},{2,0},{3,1},{4,6},{5,7},{6,4},{7,5},{8,10},{9,11},{10,... | collective-permute-start | bytes 122888 | tf_op jit(solution)/shard_map/ppermute | solution.py:245
  13.7 4.2 %collective-permute-start.7 = (bf16[160,512]{1,0:T(8,128)(2,1)S(1)}, bf16[160,512]{1,0:T(8,128)(2,1)S(1)}, u32[]{:S(2)}, u32[]{:S(2)}) collective-permute-start(bf16[160,512]{1,0:T(8,128)(2,1)S(1)} %constant_dynamic-update-slice_fusion.2), channel_id=1, source_target_pairs={{0,1},{1,0},{2,3},{3,2},{4,5},{5,4},{6,7},{7,6},{8,9},{9,8},{10,11... | collective-permute-start | bytes 491528 | tf_op jit(solution)/shard_map/ppermute | solution.py:245
  14.2 3.9 %collective-permute-start.4 = (bf16[120,512]{1,0:T(8,128)(2,1)S(1)}, bf16[120,512]{1,0:T(8,128)(2,1)S(1)}, u32[]{:S(2)}, u32[]{:S(2)}) collective-permute-start(bf16[120,512]{1,0:T(8,128)(2,1)S(1)} %constant_dynamic-update-slice_fusion), channel_id=1, source_target_pairs={{0,1},{1,0},{2,3},{3,2},{4,5},{5,4},{6,7},{7,6},{8,9},{9,8},{10,11... | collective-permute-start | bytes 368648 | tf_op jit(solution)/shard_map/ppermute | solution.py:245

commit v7 on v6

--- a/solution.py
+++ b/solution.py
@@ -11,7 +11,7 @@
 LOG2E = 1.4426950408889634
 F32 = jnp.float32
 BF16 = jnp.bfloat16
-NEAR_HEADS, FAR_HEADS, OUT_HEADS, LOADS = 8, 8, 8, 4
+NEAR_HEADS, JOIN_HEADS, LAST_HEADS, OUT_HEADS, LOADS = 8, 8, 8, 8, 4
 VMEM = pl.BlockSpec(memory_space=pltpu.VMEM)
 SMEM = pl.BlockSpec(memory_space=pltpu.SMEM)
 HBM = pl.BlockSpec(memory_space=pltpu.HBM)
@@ -150,8 +150,9 @@
 
 
 def load_kernel(sizes, *refs):
-    ins, (q_ref, own_ref, down_ref, across_ref, choice_ref, raw_ref, *tables, sems) = refs[:5], refs[5:]
-    fork_ref, owner_ref, lengths_ref = tables
+    ins, refs = refs[:5], refs[5:]
+    q_ref, own_ref, choice_ref, *marks, raw_ref, fork_ref, owner_ref, lengths_ref, sems = refs
+    tables = fork_ref, owner_ref, lengths_ref
     pairs = list(zip(ins, (*tables, raw_ref), strict=False))
     rows = q_ref.shape[1] // LOADS
     for k in range(LOADS):
@@ -164,29 +165,45 @@
     parent = fork_ref[lax.axis_index("ctx")]
     for p in range(choice_ref.shape[0]):
         choice_ref[p] = jnp.full((8, HD), jnp.where(parent == p, 1.0, 0.0), F32)
-    key = lax.broadcasted_iota(jnp.int32, (8, across_ref.shape[1]), 1)
-    valid = valid_keys(key, *sizes, fork_ref, owner_ref, lengths_ref).astype(F32)
-    across_ref[...] = jnp.concatenate([valid, valid], axis=0).astype(BF16)
-    down_ref[...] = jnp.concatenate([valid] * (HD // 8), axis=0).T
+    start = 0
+    for across_ref, down_ref in zip(marks[::2], marks[1::2], strict=True):
+        key = lax.broadcasted_iota(jnp.int32, (8, down_ref.shape[0]), 1)
+        valid = valid_keys(key + start, *sizes, *tables).astype(F32)
+        down_ref[...] = jnp.concatenate([valid] * (HD // 8), axis=0).T
+        ahead = across_ref.shape[1] - down_ref.shape[0]
+        if ahead:
+            key = lax.broadcasted_iota(jnp.int32, (8, across_ref.shape[1]), 1) - ahead
+            valid = ((key < 0) | valid_keys(key + start, *sizes, *tables)).astype(F32)
+        across_ref[...] = jnp.concatenate([valid, valid], axis=0).astype(BF16)
+        start += down_ref.shape[0]
     copies[3].wait()
     own_ref[...] = jnp.swapaxes(raw_ref[...], 0, 1)
     for copy in copies[4:]:
         copy.wait()
 
 
-def near_kernel(q_ref, own_ref, state_ref, fill_ref):
+def near_kernel(seg_rows, prompt_rows, q_ref, own_ref, choice_ref, *refs):
+    *others, state_ref, fill_ref = refs
     span = q_ref.shape[1]
     kv_heads = own_ref.shape[2] // HD
     group = q_ref.shape[2] // HD // kv_heads
     time = lax.broadcasted_iota(jnp.int32, (span, NEAR_HEADS * span), 1) % span
     causal = jnp.where(lax.broadcasted_iota(jnp.int32, time.shape, 0) <= time, 0.0, -jnp.inf)
-    ones = jnp.ones((16, span), BF16)
 
     def ready(g):
         part = slice(g * HD, (g + 1) * HD)
         keys = own_ref[0, :, part].astype(F32)
-        fill_ref[g] = jnp.broadcast_to(keys[0:1], (8, HD))
-        return split_keys(keys), jnp.concatenate([own_ref[1, :, part].T, ones], axis=0)
+        fill = keys[0:1]
+        fill_ref[g] = jnp.broadcast_to(fill, (8, HD))
+        keys, values = split_keys(keys), own_ref[1, :, part]
+        if others:
+            across_ref, down_ref, *shards = others
+            more = shard_keys(shards, seg_rows, prompt_rows, choice_ref, down_ref[...], fill, g)
+            keys, values = jnp.concatenate([keys, more[0]], axis=0), jnp.concatenate([values, more[1]], axis=0)
+            ones = across_ref[...]
+        else:
+            ones = jnp.ones((16, span), BF16)
+        return keys, jnp.concatenate([values.T, ones], axis=0)
 
     def take(c, lanes, highest, weigh):
         state_ref[: HD + 8, lanes] = weigh(highest)[: HD + 8]
@@ -195,27 +212,15 @@
     attend(q_ref, ready, causal, take, group, NEAR_HEADS)
 
 
-def ready_kernel(seg_rows, prompt_rows, start, choice_ref, fill_ref, down_ref, *refs):
-    *shards, keys_ref, values_ref = refs
-    for g in range(fill_ref.shape[0]):
-        mask = down_ref[start : start + keys_ref.shape[1]]
-        made = shard_keys(shards, seg_rows, prompt_rows, choice_ref, mask, fill_ref[g, 0:1], g)
-        keys_ref[g], values_ref[g] = made
-
-
-def far_kernel(seg_rows, prompt_rows, count, choice_ref, q_ref, state_ref, fill_ref, down_ref, across_ref, *refs):
-    shards, (*former_refs, out_ref, stage, sems) = refs[:count], refs[count:]
+def join_kernel(seg_rows, prompt_rows, final, q_ref, choice_ref, fill_ref, state_ref, across_ref, down_ref, *refs):
+    kept, many = (3, LAST_HEADS) if final else (1, JOIN_HEADS)
+    shards, refs = refs[:-kept], refs[-kept:]
     span, columns = q_ref.shape[1:]
-    kv_heads = fill_ref.shape[0]
-    group = columns // HD // kv_heads
+    group = columns // HD // fill_ref.shape[0]
     copies = []
 
     def ready(g):
-        known = sum(r.shape[1] for r in former_refs[::2])
-        keys, values = shard_keys(shards, seg_rows, prompt_rows, choice_ref, down_ref[known:], fill_ref[g, 0:1], g)
-        if former_refs:
-            keys = jnp.concatenate([*[r[g] for r in former_refs[::2]], keys], axis=0)
-            values = jnp.concatenate([*[r[g] for r in former_refs[1::2]], values], axis=0)
+        keys, values = shard_keys(shards, seg_rows, prompt_rows, choice_ref, down_ref[...], fill_ref[g, 0:1], g)
         return keys, jnp.concatenate([values.T, across_ref[...]], axis=0)
 
     def take(c, lanes, highest, weigh):
@@ -223,20 +228,28 @@
         top = jnp.maximum(former, highest)
         both = weigh(top[0:1])
         scale = jnp.exp2(former - top)
-        share = 1.0 / (state_ref[HD : HD + 8, lanes] * scale + both[HD : HD + 8])
+        total = state_ref[HD : HD + 8, lanes] * scale + both[HD : HD + 8]
+        rows = (HD // 8, 8, -1)
+        if not final:
+            joined = state_ref[:HD, lanes].reshape(rows) * scale[None] + both[:HD].reshape(rows)
+            refs[0][:HD, lanes] = joined.reshape(HD, -1)
+            refs[0][HD : HD + 8, lanes] = total
+            refs[0][HD + 8 :, lanes] = top
+            return
+        out_ref, stage, sems = refs
+        share = 1.0 / total
         scale = scale * share
-        rows = (HD // 8, 8, -1)
         result = state_ref[:HD, lanes].reshape(rows) * scale[None] + both[:HD].reshape(rows) * share[None]
         result = result.reshape(HD, -1).astype(BF16)
-        for k in range(FAR_HEADS):
-            i = c * FAR_HEADS + k
+        for k in range(many):
+            i = c * many + k
             stage[:, i * HD : (i + 1) * HD] = result[:, k * span : (k + 1) * span].T
             if (i + 1) % OUT_HEADS == 0:
                 part = pl.ds((i + 1 - OUT_HEADS) * HD, OUT_HEADS * HD)
                 copies.append(pltpu.make_async_copy(stage.at[:, part], out_ref.at[0, :, part], sems.at[len(copies)]))
                 copies[-1].start()
 
-    attend(q_ref, ready, None, take, group, FAR_HEADS)
+    attend(q_ref, ready, None, take, group, many)
     for copy in copies:
         copy.wait()
 
@@ -258,19 +271,20 @@
     wide = [permute(both, lambda i, j=j: i ^ (2 * (2 * j + i % 2)), n) for j in pairs]
     side = permute(shard, lambda i: i ^ near, n)
     passed = permute(first, lambda i: i ^ near, n)
-    soon = jnp.concatenate([first, side, *wide[1:]], axis=0)
+    soon = jnp.concatenate([*wide[1:], first, side], axis=0)
     late = jnp.concatenate([*wide[:1], passed], axis=0)
     soon_theirs = permute(soon, lambda i: i ^ 1, n)
     late_theirs = permute(late, lambda i: i ^ 1, n)
-    got = []
+    straight, early = [far, near], []
     for core in range(2):
         steps = [[2 * (2 * j + core), 2 * (2 * j + core) ^ 1] for j in pairs]
-        got.append(([far, near, *[o for step in steps[1:] for o in step]], [*steps[0], far ^ near]))
+        early.append(([o for step in steps[1:] for o in step], [*steps[0], far ^ near]))
     offsets = []
     for core in range(2):
-        theirs = [[o ^ 1 for o in part] for part in got[1 - core]]
-        offsets.append([0, 1, *got[core][0], *theirs[0], *got[core][1], *theirs[1]])
-    return [[shard, mate, soon], [soon_theirs, late], [late_theirs]], offsets
+        (mine, last), other = early[core], early[1 - core]
+        theirs = [o ^ 1 for o in (*other[0], *straight)]
+        offsets.append([0, 1, *straight, *mine, *theirs, *last, *[o ^ 1 for o in other[1]]])
+    return [[shard, mate, first, side], [*wide[1:], soon_theirs, late], [late_theirs]], offsets
 
 
 def use_gather(mesh_size, parents, seg_rows, prompt_rows):
@@ -311,21 +325,26 @@
             scratch_shapes=[pltpu.VMEM((parents, rows, width), BF16)],
             name="pack",
         )(fork_list, prompt_kv, parent_kv)
-        batches, offsets = [[lax.all_to_all(send, "ctx", split_axis=0, concat_axis=0, tiled=True)]], None
+        batches, offsets = [[], [lax.all_to_all(send, "ctx", split_axis=0, concat_axis=0, tiled=True)]], None
     batches = [[s.reshape(-1, rows, width) for s in batch] for batch in batches]
     counts = [sum(s.shape[0] for s in batch) for batch in batches]
     slots = seg_rows + 2 * prompt_rows
-    query, own, down, across, choice = pl.pallas_call(
+    heads = child_q.shape[2] // HD
+    masks = []
+    for k, count in enumerate(counts):
+        if count:
+            ahead = 0 if k else span
+            masks += [((16, ahead + count * slots), BF16), ((count * slots, HD), F32)]
+    query, own, choice, *marks = pl.pallas_call(
         functools.partial(load_kernel, (seg_rows, prompt_rows, counts, offsets)),
         out_shape=[
             jax.ShapeDtypeStruct(child_q.shape, BF16),
             jax.ShapeDtypeStruct((2, span, width), BF16),
-            jax.ShapeDtypeStruct((n * slots, HD), F32),
-            jax.ShapeDtypeStruct((16, n * slots), BF16),
             jax.ShapeDtypeStruct((parents if gather else 1, 8, HD), F32),
+            *[jax.ShapeDtypeStruct(*mask) for mask in masks],
         ],
         in_specs=[HBM] * 5,
-        out_specs=[VMEM] * 5,
+        out_specs=[VMEM] * (3 + len(masks)),
         scratch_shapes=[
             pltpu.VMEM(child_kv.shape[1:], BF16),
             *[pltpu.SMEM(x.shape, jnp.int32) for x in (fork_list, owner_map, lengths)],
@@ -334,36 +353,31 @@
         compiler_params=limit(8),
         name="load",
     )(*in_hbm(fork_list, owner_map, lengths, child_kv[0], child_q))
+    marks = [marks[2 * k : 2 * k + 2] for k in range(len(marks) // 2)]
+    marks = [[]] * (len(counts) - len(marks)) + marks
+    state_shape = jax.ShapeDtypeStruct((HD + 16, heads * span), F32)
     state, fill = pl.pallas_call(
-        near_kernel,
-        out_shape=[
-            jax.ShapeDtypeStruct((HD + 16, child_q.shape[2] // HD * span), F32),
-            jax.ShapeDtypeStruct((kv_heads, 8, HD), F32),
-        ],
-        in_specs=[VMEM] * 2,
+        functools.partial(near_kernel, seg_rows, prompt_rows),
+        out_shape=[state_shape, jax.ShapeDtypeStruct((kv_heads, 8, HD), F32)],
+        in_specs=[VMEM] * (3 + len(marks[0]) + len(batches[0])),
         out_specs=[VMEM] * 2,
         compiler_params=limit(16),
         name="near",
-    )(query, own)
-    former = []
-    for k, (batch, count) in enumerate(zip(batches[:-1], counts)):
-        former += pl.pallas_call(
-            functools.partial(ready_kernel, seg_rows, prompt_rows, sum(counts[:k]) * slots),
-            out_shape=[jax.ShapeDtypeStruct((kv_heads, count * slots, k * HD), BF16) for k in (2, 1)],
-            in_specs=[VMEM] * (3 + len(batch)),
-            out_specs=[VMEM] * 2,
-            compiler_params=limit(4),
-        )(choice, fill, down, *batch)
-    last = batches[-1]
-    return pl.pallas_call(
-        functools.partial(far_kernel, seg_rows, prompt_rows, len(last)),
-        out_shape=jax.ShapeDtypeStruct(child_q.shape, BF16),
-        in_specs=[VMEM] * (6 + len(last) + len(former)),
-        out_specs=HBM,
-        scratch_shapes=[pltpu.VMEM(child_q.shape[1:], BF16), pltpu.SemaphoreType.DMA((child_q.shape[2] // HD // OUT_HEADS,))],
-        compiler_params=limit(16 if gather else 48),
-        name="far",
-    )(choice, query, state, fill, down, across, *last, *former)
+    )(query, own, choice, *marks[0], *batches[0])
+    for k in range(1, len(batches)):
+        final = k == len(batches) - 1
+        state = pl.pallas_call(
+            functools.partial(join_kernel, seg_rows, prompt_rows, final),
+            out_shape=jax.ShapeDtypeStruct(child_q.shape, BF16) if final else state_shape,
+            in_specs=[VMEM] * (6 + len(batches[k])),
+            out_specs=HBM if final else VMEM,
+            scratch_shapes=[
+                pltpu.VMEM(child_q.shape[1:], BF16),
+                pltpu.SemaphoreType.DMA((heads // OUT_HEADS,)),
+            ][: 2 * final],
+            compiler_params=limit(16 if gather else 48),
+        )(query, choice, fill, state, *marks[k], *batches[k])
+    return state
 
 
 def solution(mesh):

time: 20.8 us -> 22.8 us (1.096)
  waiting for transfers between devices: 5.78 us -> 7.11 us
  Pallas kernels: 6.16 us -> 6.88 us
    ppermute x8, waiting for transfers between devices: 5.78 us -> 7.11 us  [permute(): return lax.ppermute(x, 'ctx', [(i, target(i)) for i in range(n)])]
    pallas_call x4 -> x3, Pallas kernels: 4.02 us -> 4.72 us  [the longest x2 3.35 us: body(): pl.pallas_call(functools.partial(join_kernel, seg_rows, prompt_rows, fina...]
  transfers between devices with their start and end apart: 8 -> 8, of which waited for: 3 -> 3; matrix products, arithmetic and copies ran while one was open for 0% -> 0% of each run, Pallas kernels for 14% -> 18%
where the time goes in v7:
time: 22.8 us; the launch traced here: 22.6 us
  starting transfers between devices  8.47 us (37%)
  waiting for transfers between devices  7.11 us (31%)
  Pallas kernels  6.88 us (30%)
    ppermute x8, starting transfers between devices, permute(): return lax.ppermute(x, 'ctx', [(i, target(i)) for i in range(n)])  8.47 us
    ppermute x8, waiting for transfers between devices, permute(): return lax.ppermute(x, 'ctx', [(i, target(i)) for i in range(n)])  7.11 us
    pallas_call x2, Pallas kernels, body(): pl.pallas_call(functools.partial(join_kernel, seg_rows, prompt_rows, fina...  3.35 us
    pallas_call x1, Pallas kernels, body(): pl.pallas_call(functools.partial(near_kernel, seg_rows, prompt_rows), out...  1.38 us
    pallas_call x1, Pallas kernels, body(): pl.pallas_call(functools.partial(load_kernel, (seg_rows, prompt_rows, cou...  1.34 us
    pallas_call x1, Pallas kernels, body(): pl.pallas_call(shard_kernel, out_shape=[jax.ShapeDtypeStruct((k * rows, w...  0.81 us
  transfers between devices with their start and end apart: 8, of which 3 were waited for; matrix products, arithmetic and copies ran while one was open for 0% of the time, Pallas kernels for 18%

profile of v7, /device:TPU:0, one launch (start us, length us, event | category | flops | bytes accessed | tf_op | source)
XLA Modules:
  0.0 22.6 jit_solution(12478833926906547763)
XLA Ops:
  0.0 0.8 %shard.1 = (bf16[40,512]{1,0:T(8,128)(2,1)S(1)}, bf16[80,512]{1,0:T(8,128)(2,1)S(1)}) custom-call(bf16[4,2,512]{2,1,0:T(2,128)(2,1)} %prompt_hbm.1, bf16[8,2,2,512]{3,2,1,0:T(2,128)(2,1)} %parent_hbm.1), custom_call_target="tpu_custom_call" | custom-call | tf_op jit(solution)/shard_map/shard/pallas_call | solution.py:304
  0.8 0.6 %collective-permute-start = (bf16[40,512]{1,0:T(8,128)(2,1)S(1)}, bf16[40,512]{1,0:T(8,128)(2,1)S(1)}, u32[]{:S(2)}, u32[]{:S(2)}) collective-permute-start(bf16[40,512]{1,0:T(8,128)(2,1)S(1)} %get-tuple-element.23), channel_id=1, source_target_pairs={{0,1},{1,0},{2,3},{3,2},{4,5},{5,4},{6,7},{7,6},{8,9},{9,8},{10,11... | collective-permute-start | bytes 122888 | tf_op jit(solution)/shard_map/ppermute | solution.py:258
  1.4 0.9 %collective-permute-done = bf16[40,512]{1,0:T(8,128)(2,1)S(1)} collective-permute-done((bf16[40,512]{1,0:T(8,128)(2,1)S(1)}, bf16[40,512]{1,0:T(8,128)(2,1)S(1)}, u32[]{:S(2)}, u32[]{:S(2)}) %collective-permute-start) | collective-permute-done | bytes 40992 | tf_op jit(solution)/shard_map/ppermute | solution.py:258
  2.2 2.9 %collective-permute-start.3 = (bf16[80,512]{1,0:T(8,128)(2,1)S(1)}, bf16[80,512]{1,0:T(8,128)(2,1)S(1)}, u32[]{:S(2)}, u32[]{:S(2)}) collective-permute-start(bf16[80,512]{1,0:T(8,128)(2,1)S(1)} %constant_dynamic-update-slice_fusion.2), channel_id=1, source_target_pairs={{0,4},{1,7},{2,6},{3,5},{4,0},{5,3},{6,2},{7,1},{8,12},{9,15},{10,... | collective-permute-start | bytes 245768 | tf_op jit(solution)/shard_map/ppermute | solution.py:258
  5.2 2.5 %collective-permute-start.1 = (bf16[40,512]{1,0:T(8,128)(2,1)S(1)}, bf16[40,512]{1,0:T(8,128)(2,1)S(1)}, u32[]{:S(2)}, u32[]{:S(2)}) collective-permute-start(bf16[40,512]{1,0:T(8,128)(2,1)S(1)} %get-tuple-element.23), channel_id=1, source_target_pairs={{0,12},{1,13},{2,14},{3,15},{4,8},{5,9},{6,10},{7,11},{8,4},{9,5},... | collective-permute-start | bytes 122888 | tf_op jit(solution)/shard_map/ppermute | solution.py:258
  7.6 1.5 %collective-permute-start.2 = (bf16[40,512]{1,0:T(8,128)(2,1)S(1)}, bf16[40,512]{1,0:T(8,128)(2,1)S(1)}, u32[]{:S(2)}, u32[]{:S(2)}) collective-permute-start(bf16[40,512]{1,0:T(8,128)(2,1)S(1)} %get-tuple-element.23), channel_id=1, source_target_pairs={{0,2},{1,3},{2,0},{3,1},{4,6},{5,7},{6,4},{7,5},{8,10},{9,11},{10,... | collective-permute-start | bytes 122888 | tf_op jit(solution)/shard_map/ppermute | solution.py:258
  9.1 0.1 collective-permute-start.5
  9.2 2.4 %collective-permute-done.1 = bf16[40,512]{1,0:T(8,128)(2,1)S(1)} collective-permute-done((bf16[40,512]{1,0:T(8,128)(2,1)S(1)}, bf16[40,512]{1,0:T(8,128)(2,1)S(1)}, u32[]{:S(2)}, u32[]{:S(2)}) %collective-permute-start.1) | collective-permute-done | bytes 40992 | tf_op jit(solution)/shard_map/ppermute | solution.py:258
  11.7 0.8 %collective-permute-start.6 = (bf16[40,512]{1,0:T(8,128)(2,1)S(1)}, bf16[40,512]{1,0:T(8,128)(2,1)S(1)}, u32[]{:S(2)}, u32[]{:S(2)}) collective-permute-start(bf16[40,512]{1,0:T(8,128)(2,1)S(1)} %collective-permute-done.1), channel_id=1, source_target_pairs={{0,2},{1,3},{2,0},{3,1},{4,6},{5,7},{6,4},{7,5},{8,10},{9,11},{10,... | collective-permute-start | bytes 122888 | tf_op jit(solution)/shard_map/ppermute | solution.py:258
  12.5 0.0 collective-permute-done.2
  12.5 0.0 collective-permute-done.3
  12.5 0.1 collective-permute-start.4
  12.6 3.8 %collective-permute-done.5 = bf16[80,512]{1,0:T(8,128)(2,1)S(1)} collective-permute-done((bf16[80,512]{1,0:T(8,128)(2,1)S(1)}, bf16[80,512]{1,0:T(8,128)(2,1)S(1)}, u32[]{:S(2)}, u32[]{:S(2)}) %collective-permute-start.5) | collective-permute-done | bytes 81952 | tf_op jit(solution)/shard_map/ppermute | solution.py:258
  16.4 0.0 collective-permute-done.6
  16.4 0.1 collective-permute-start.7
  16.5 1.3 %load.1 = (bf16[1,128,4096]{2,1,0:T(8,128)(2,1)S(1)}, bf16[2,128,512]{2,1,0:T(8,128)(2,1)S(1)}, f32[2,8,128]{2,1,0:T(8,128)S(1)}, bf16[16,192]{1,0:T(8,128)(2,1)...) custom-call(s32[16]{0:T(128)} %refs_0_.1, ...), custom_call_target="tpu_custom_call" | custom-call | tf_op jit(solution)/shard_map/load/pallas_call | solution.py:338
  17.8 1.4 %near.1 = (f32[144,4096]{1,0:T(8,128)S(1)}, f32[4,8,128]{2,1,0:T(8,128)S(1)}) custom-call(bf16[1,128,4096]{2,1,0:T(8,128)(2,1)S(1)} %get-tuple-element.18.q_ref, bf16[2,128,512]{2,1,0:T(8,128)(2,1)S(1)} %get-tuple-element.20.own_ref, f32[2,8,128]{2,1,0:T(8,128)S(1)} %get-tuple-element.19.choice_ref, bf16[16,192]{1,0:T(8,128)(2,1)S(1)} %get-tuple-element.21.refs_0_, ...), custom_call_target="tpu_custom_call" | custom-call | tf_op jit(solution)/shard_map/near/pallas_call | solution.py:359
  19.2 0.0 collective-permute-done.4
  19.2 1.3 %shard_map.73.state_ref = f32[144,4096]{1,0:T(8,128)S(1)} custom-call(bf16[1,128,4096]{2,1,0:T(8,128)(2,1)S(1)} %get-tuple-element.18.q_ref, f32[2,8,128]{2,1,0:T(8,128)S(1)} %get-tuple-element.19.choice_ref, f32[4,8,128]{2,1,0:T(8,128)S(1)} %get-tuple-element.24.fill_ref, f32[144,4096]{1,0:T(8,128)S(1)} %get-tuple-element.25.state_ref, ...), custom_call_target="tpu_custom_call" | custom-call | tf_op jit(solution)/shard_map/pallas_call | solution.py:369
  20.5 0.0 collective-permute-done.7
  20.5 2.0 %shard_map.74 = bf16[1,128,4096]{2,1,0:T(8,128)(2,1)} custom-call(bf16[1,128,4096]{2,1,0:T(8,128)(2,1)S(1)} %get-tuple-element.18.q_ref, f32[2,8,128]{2,1,0:T(8,128)S(1)} %get-tuple-element.19.choice_ref, f32[4,8,128]{2,1,0:T(8,128)S(1)} %get-tuple-element.24.fill_ref, f32[144,4096]{1,0:T(8,128)S(1)} %shard_map.73.state_ref, ...), custom_call_target="tpu_custom_call" | custom-call | tf_op jit(solution)/shard_map/pallas_call | solution.py:369
  (4 shorter events, 0.0 us)
Async XLA Ops:
  0.8 1.4 %collective-permute-start = (bf16[40,512]{1,0:T(8,128)(2,1)S(1)}, bf16[40,512]{1,0:T(8,128)(2,1)S(1)}, u32[]{:S(2)}, u32[]{:S(2)}) collective-permute-start(bf16[40,512]{1,0:T(8,128)(2,1)S(1)} %get-tuple-element.23), channel_id=1, source_target_pairs={{0,1},{1,0},{2,3},{3,2},{4,5},{5,4},{6,7},{7,6},{8,9},{9,8},{10,11... | collective-permute-start | bytes 122888 | tf_op jit(solution)/shard_map/ppermute | solution.py:258
  2.2 10.2 %collective-permute-start.3 = (bf16[80,512]{1,0:T(8,128)(2,1)S(1)}, bf16[80,512]{1,0:T(8,128)(2,1)S(1)}, u32[]{:S(2)}, u32[]{:S(2)}) collective-permute-start(bf16[80,512]{1,0:T(8,128)(2,1)S(1)} %constant_dynamic-update-slice_fusion.2), channel_id=1, source_target_pairs={{0,4},{1,7},{2,6},{3,5},{4,0},{5,3},{6,2},{7,1},{8,12},{9,15},{10,... | collective-permute-start | bytes 245768 | tf_op jit(solution)/shard_map/ppermute | solution.py:258
  5.2 6.5 %collective-permute-start.1 = (bf16[40,512]{1,0:T(8,128)(2,1)S(1)}, bf16[40,512]{1,0:T(8,128)(2,1)S(1)}, u32[]{:S(2)}, u32[]{:S(2)}) collective-permute-start(bf16[40,512]{1,0:T(8,128)(2,1)S(1)} %get-tuple-element.23), channel_id=1, source_target_pairs={{0,12},{1,13},{2,14},{3,15},{4,8},{5,9},{6,10},{7,11},{8,4},{9,5},... | collective-permute-start | bytes 122888 | tf_op jit(solution)/shard_map/ppermute | solution.py:258
  7.6 4.8 %collective-permute-start.2 = (bf16[40,512]{1,0:T(8,128)(2,1)S(1)}, bf16[40,512]{1,0:T(8,128)(2,1)S(1)}, u32[]{:S(2)}, u32[]{:S(2)}) collective-permute-start(bf16[40,512]{1,0:T(8,128)(2,1)S(1)} %get-tuple-element.23), channel_id=1, source_target_pairs={{0,2},{1,3},{2,0},{3,1},{4,6},{5,7},{6,4},{7,5},{8,10},{9,11},{10,... | collective-permute-start | bytes 122888 | tf_op jit(solution)/shard_map/ppermute | solution.py:258
  9.1 7.2 %collective-permute-start.5 = (bf16[80,512]{1,0:T(8,128)(2,1)S(1)}, bf16[80,512]{1,0:T(8,128)(2,1)S(1)}, u32[]{:S(2)}, u32[]{:S(2)}) collective-permute-start(bf16[80,512]{1,0:T(8,128)(2,1)S(1)} %constant_dynamic-update-slice_fusion.2), channel_id=1, source_target_pairs={{0,8},{1,11},{2,10},{3,9},{4,12},{5,15},{6,14},{7,13},{8,0},{9,3},... | collective-permute-start | bytes 245768 | tf_op jit(solution)/shard_map/ppermute | solution.py:258
  11.7 4.7 %collective-permute-start.6 = (bf16[40,512]{1,0:T(8,128)(2,1)S(1)}, bf16[40,512]{1,0:T(8,128)(2,1)S(1)}, u32[]{:S(2)}, u32[]{:S(2)}) collective-permute-start(bf16[40,512]{1,0:T(8,128)(2,1)S(1)} %collective-permute-done.1), channel_id=1, source_target_pairs={{0,2},{1,3},{2,0},{3,1},{4,6},{5,7},{6,4},{7,5},{8,10},{9,11},{10,... | collective-permute-start | bytes 122888 | tf_op jit(solution)/shard_map/ppermute | solution.py:258
  12.5 6.7 %collective-permute-start.4 = (bf16[160,512]{1,0:T(8,128)(2,1)S(1)}, bf16[160,512]{1,0:T(8,128)(2,1)S(1)}, u32[]{:S(2)}, u32[]{:S(2)}) collective-permute-start(bf16[160,512]{1,0:T(8,128)(2,1)S(1)} %pad_maximum_fusion), channel_id=1, source_target_pairs={{0,1},{1,0},{2,3},{3,2},{4,5},{5,4},{6,7},{7,6},{8,9},{9,8},{10,11... | collective-permute-start | bytes 491528 | tf_op jit(solution)/shard_map/ppermute | solution.py:258
  16.4 4.2 %collective-permute-start.7 = (bf16[120,512]{1,0:T(8,128)(2,1)S(1)}, bf16[120,512]{1,0:T(8,128)(2,1)S(1)}, u32[]{:S(2)}, u32[]{:S(2)}) collective-permute-start(bf16[120,512]{1,0:T(8,128)(2,1)S(1)} %constant_dynamic-update-slice_fusion), channel_id=1, source_target_pairs={{0,1},{1,0},{2,3},{3,2},{4,5},{5,4},{6,7},{7,6},{8,9},{9,8},{10,11... | collective-permute-start | bytes 368648 | tf_op jit(solution)/shard_map/ppermute | solution.py:258
